TPU v7x, 256 devices: a whole 4x4x8 slice. The times are simulated.
256 devices in a mesh: dp: 32 (over z, y), ctx: 8 (over x, core).
Axes of the slice: x: 4, y: 4, z: 8, core: 2. Of those that a mesh axis runs over, the one named last changes fastest.
Arguments:
- query_rows: bfloat16 [32768, 4096], P(('dp', 'ctx')), may hold values from -9 to 9
- key_rows: bfloat16 [32768, 1024], P(('dp', 'ctx')), may hold values from -4 to 4
- token_values: bfloat16 [32768, 1024], P(('dp', 'ctx')), may hold values from -6 to 6
- group_of_row: int32 [32768, 1], P(('dp', 'ctx')), may hold values from 0 to 31; in each aligned block of 128 rows (0 to 127, 128 to 255, ...) at most 8 rows name the same one
- doc_lengths: int32 [32, 2], P('dp'), may hold values from 1 to 1536, 2048 in all within a row
Outputs:
- attended: bfloat16 [32768, 4096], P(('dp', 'ctx'))
Inputs may be any that keep to these rules, and one draw needn't show every extreme that they name: `group_of_row`: within each device's block of 128 rows no group is named by more than 8 rows; in some blocks one group is named by exactly 8. `doc_lengths`: each group's 2 lengths sum to 2048; neither exceeds 1536.
All inputs are finite; a program needn't handle non-finite values.
Results may differ from a plain program's by a relative error of at most 0.0038.
Values may be sent and summed in bfloat16 or wider, within the bound.
No kernel may reach another device: no remote copies, remote signals or barrier semaphores. Data moves between devices by JAX's collectives and lax.ppermute only.
A program may use at most 128 MiB of HBM per device.

v0:
```python
import math

import jax
import jax.numpy as jnp
from jax import lax
from jax.sharding import PartitionSpec as P

QUERY_HEAD_COUNT = 32
KEY_VALUE_HEADS = 8
HEAD_SIZE = 128


masked_score = -1e30


def rank_rows(indices):
    count_all = indices.shape[0]
    rows_per_block = 128
    usable = indices >= 0

    def count_before(pieces):
        earlier = usable[None, :] & (indices[None, :] < pieces[:, None])
        return jnp.sum(earlier.astype(jnp.int32), axis=1)

    counted = lax.map(count_before, indices.reshape(count_all // rows_per_block, rows_per_block))
    return counted.reshape(count_all)


def document_ids(ranks, starts):
    return jnp.sum((starts[None, :] <= ranks[:, None]).astype(jnp.int32), axis=1) - 1


def attend(block_of_queries, key_heads, value_heads, query_index, query_doc, key_index, key_doc):
    head_dim = key_heads.shape[2]
    scores = jnp.einsum(
        "qjgd,kjd->jgqk", block_of_queries, key_heads, preferred_element_type=jnp.float32
    )
    scores = scores * (1.0 / math.sqrt(head_dim))
    allowed = (
        (query_doc[:, None] == key_doc[None, :])
        & (key_index[None, :] <= query_index[:, None])
        & (key_index[None, :] >= 0)
    )
    scores = jnp.where(allowed[None, None], scores, masked_score)
    row_max = jnp.max(scores, axis=3, keepdims=True)
    weights = jnp.exp(scores - row_max)
    totals = jnp.sum(weights, axis=3)
    output = jnp.einsum(
        "jgqk,kjd->qjgd",
        weights.astype(jnp.bfloat16),
        value_heads,
        preferred_element_type=jnp.float32,
    )
    output = output / jnp.transpose(totals, (2, 0, 1))[..., None]
    return output.reshape(
        output.shape[0], output.shape[1], output.shape[2] * output.shape[3]
    ).astype(jnp.bfloat16)


def attend_all(query_heads, query_index, query_doc, key_heads, value_heads, key_index, key_doc):
    count_q = query_heads.shape[0]
    rows_per_block = min(128, count_q)
    blocks = count_q // rows_per_block

    def one_block(inputs_block):
        return attend(
            inputs_block[0],
            key_heads,
            value_heads,
            inputs_block[1],
            inputs_block[2],
            key_index,
            key_doc,
        )

    shaped = (
        query_heads.reshape((blocks, rows_per_block) + query_heads.shape[1:]),
        query_index.reshape(blocks, rows_per_block),
        query_doc.reshape(blocks, rows_per_block),
    )
    result = lax.map(one_block, shaped)
    return result.reshape((count_q,) + result.shape[2:])


def body(query_rows, key_rows, token_values, group_of_row, doc_lengths):
    dp_count = lax.axis_size("dp")
    tok_rows = query_rows.shape[0]
    slot_rows = 2 * tok_rows // dp_count
    key_value_head_count = KEY_VALUE_HEADS
    head_dim = HEAD_SIZE
    rows_per_group = QUERY_HEAD_COUNT // KEY_VALUE_HEADS
    group_ids = group_of_row[:, 0]
    onehot = (group_ids[:, None] == jnp.arange(dp_count, dtype=jnp.int32)[None, :]).astype(
        jnp.int32
    )
    position = jnp.sum((jnp.cumsum(onehot, axis=0) - onehot) * onehot, axis=1)
    target = group_ids * slot_rows + position
    stream = lax.axis_index(("dp", "ctx")) * tok_rows + jnp.arange(tok_rows, dtype=jnp.int32)
    send_count = dp_count * slot_rows
    send_query = (
        jnp.zeros((send_count, query_rows.shape[1]), jnp.bfloat16).at[target].set(query_rows)
    )
    send_key = jnp.zeros((send_count, key_rows.shape[1]), jnp.bfloat16).at[target].set(key_rows)
    send_value = (
        jnp.zeros((send_count, token_values.shape[1]), jnp.bfloat16).at[target].set(token_values)
    )
    send_index = jnp.full((send_count,), -1, jnp.int32).at[target].set(stream)
    arrived = (
        lax.all_to_all(
            send_query.reshape(dp_count, slot_rows, query_rows.shape[1]),
            "dp",
            split_axis=0,
            concat_axis=0,
            tiled=True,
        ),
        lax.all_to_all(
            send_key.reshape(dp_count, slot_rows, key_rows.shape[1]),
            "dp",
            split_axis=0,
            concat_axis=0,
            tiled=True,
        ),
        lax.all_to_all(
            send_value.reshape(dp_count, slot_rows, token_values.shape[1]),
            "dp",
            split_axis=0,
            concat_axis=0,
            tiled=True,
        ),
        lax.all_to_all(
            send_index.reshape(dp_count, slot_rows), "dp", split_axis=0, concat_axis=0, tiled=True
        ),
    )
    local_query = arrived[0].reshape(send_count, key_value_head_count, rows_per_group * head_dim)
    local_key = arrived[1].reshape(send_count, key_value_head_count, head_dim)
    local_value = arrived[2].reshape(send_count, key_value_head_count, head_dim)
    local_index = arrived[3].reshape(send_count)
    lengths = doc_lengths[0]
    starts = jnp.cumsum(lengths) - lengths
    group_key, group_value, group_index = (
        lax.all_gather(local_key, "ctx", axis=0, tiled=True),
        lax.all_gather(local_value, "ctx", axis=0, tiled=True),
        lax.all_gather(local_index, "ctx", axis=0, tiled=True),
    )
    group_doc = document_ids(rank_rows(group_index), starts)
    own_doc = lax.dynamic_slice_in_dim(group_doc, lax.axis_index("ctx") * send_count, send_count, 0)
    result = attend_all(
        local_query.reshape(send_count, key_value_head_count, rows_per_group, head_dim),
        local_index,
        own_doc,
        group_key,
        group_value,
        group_index,
        group_doc,
    )
    back_rows = result.reshape(send_count, key_value_head_count * rows_per_group * head_dim)
    returned = lax.all_to_all(
        back_rows.reshape(dp_count, slot_rows, back_rows.shape[1]),
        "dp",
        split_axis=0,
        concat_axis=0,
        tiled=True,
    )
    return returned.reshape(send_count, back_rows.shape[1])[target]


def solution(mesh):
    in_specs = (
        P(("dp", "ctx"), None),
        P(("dp", "ctx"), None),
        P(("dp", "ctx"), None),
        P(("dp", "ctx"), None),
        P("dp", None),
    )
    out_specs = P(("dp", "ctx"), None)
    return jax.shard_map(body, mesh=mesh, in_specs=in_specs, out_specs=out_specs, check_vma=False)
```

profile of v0, /device:TPU:1, one launch (start us, length us, event | category | flops | bytes accessed | tf_op | source)
XLA Modules:
  0.0 314.4 jit_solution(16999272624418811626)
XLA Ops:
  10.7 28.1 %all_to_all.29 = bf16[32,8,1024]{2,1,0:T(8,128)(2,1)S(1)} all-to-all(bf16[32,8,1024]{2,1,0:T(8,128)(2,1)S(1)} %bitcast.108), channel_id=1, replica_groups=mesh['dp'=32,'ctx'=8] {'dp'}, dimensions={0} | all-to-all | bytes 1048576 | tf_op jit(solution)/shard_map/all_to_all | solution.py:116
  39.8 1.7 scatter_custom_fusion.3
  41.5 20.3 %all_to_all.30 = bf16[32,8,1024]{2,1,0:T(8,128)(2,1)S(1)} all-to-all(bf16[32,8,1024]{2,1,0:T(8,128)(2,1)S(1)} %bitcast.109), channel_id=1, replica_groups=mesh['dp'=32,'ctx'=8] {'dp'}, dimensions={0} | all-to-all | bytes 1048576 | tf_op jit(solution)/shard_map/all_to_all | solution.py:123
  64.4 6.3 %all-to-all-start = ((s32[32,1,8]{2,1,0:T(1,128)}), s32[32,1,8]{2,1,0:T(1,128)S(1)}, u32[]{:S(2)}, u32[]{:S(2)}) async-start(s32[32,1,8]{2,1,0:T(1,128)} %bitcast.17), calls=%async_computation | async-start | bytes 32768 | tf_op jit(solution)/shard_map/all_to_all | solution.py:130
  70.9 4.4 %scatter_custom_fusion.1 = bf16[256,4096]{1,0:T(8,128)(2,1)} fusion(s32[128]{0:T(128)S(1)} %fusion.26, bf16[128,4096]{1,0:T(8,128)(2,1)} %param.9, bf16[]{:T(256)} %constant.33.clone.1), kind=kCustom, calls=%fused_computation.31 | custom fusion | bytes 2097664 | tf_op jit(solution)/shard_map/scatter | solution.py:101
  75.3 4.0 %all-to-all-done = s32[32,1,8]{2,1,0:T(1,128)S(1)} async-done(((s32[32,1,8]{2,1,0:T(1,128)}), s32[32,1,8]{2,1,0:T(1,128)S(1)}, u32[]{:S(2)}, u32[]{:S(2)}) %all-to-all-start) | async-done | bytes 1056 | tf_op jit(solution)/shard_map/all_to_all | solution.py:130
  79.3 5.2 %all-to-all-start.1 = ((bf16[32,8,4096]{2,1,0:T(8,128)(2,1)}), bf16[32,8,4096]{2,1,0:T(8,128)(2,1)S(1)}, u32[]{:S(2)}, u32[]{:S(2)}) async-start(bf16[32,8,4096]{2,1,0:T(8,128)(2,1)} %bitcast.22), calls=%async_computation.1 | async-start | bytes 4194304 | tf_op jit(solution)/shard_map/all_to_all | solution.py:109
  86.0 13.1 %all-gather = s32[8,1,256]{2,1,0:T(1,128)S(1)} all-gather(s32[1,1,256]{2,1,0:T(1,128)S(1)} %reshape.188), channel_id=1, replica_groups=mesh['dp'=32,'ctx'=8] {'ctx'}, dimensions={0}, use_global_device_ids=true | all-gather | bytes 9216 | tf_op jit(solution)/shard_map/all_gather | solution.py:143
  99.0 5.6 %while.20 = (s32[]{:T(128)}, s32[16,128]{1,0:T(8,128)S(1)}, pred[2048]{0:T(1024)(128)(4,1)S(1)}, s32[2048]{0:T(1024)S(1)}, s32[16,128]{1,0:T(8,128)S(1)}, /*index=5*/s32[]{:T(128)}, s32[]{:T(128)}) while((s32[]{:T(128)}, s32[16,128]{1,0:T(8,128)S(1)}, pred[2048]{0:T(1024)(128)(4,1)S(1)}, s32[2048]{0:T(1024)S(1)}, s32[16,128]{1,0:T(8,128)S(1)}, ...), condition=%wide.region_7.8_spmd, body=%wide.region_5.7_spmd.sunk | while | flops 1048450 | bytes 13397 | solution.py:25
  104.8 26.4 %all-to-all-done.1 = bf16[32,8,4096]{2,1,0:T(8,128)(2,1)S(1)} async-done(((bf16[32,8,4096]{2,1,0:T(8,128)(2,1)}), bf16[32,8,4096]{2,1,0:T(8,128)(2,1)S(1)}, u32[]{:S(2)}, u32[]{:S(2)}) %all-to-all-start.1) | async-done | bytes 2097184 | tf_op jit(solution)/shard_map/all_to_all | solution.py:109
  131.2 2.7 reshape_reshape_reshape.6
  133.9 4.8 %copy.18 = bf16[2048,8,128]{2,0,1:T(8,128)(2,1)} copy(bf16[2048,8,128]{2,1,0:T(8,128)(2,1)} %all-gather.4.cloned.1.call-done) | data formatting | bytes 8388608 | tf_op jit(solution)/shard_map/while | solution.py:81
  138.7 6.7 %copy.19 = bf16[2048,8,128]{0,2,1:T(8,128)(2,1)} copy(bf16[2048,8,128]{2,1,0:T(8,128)(2,1)} %all-gather.6.cloned.1.call-done) | data formatting | bytes 8388608 | tf_op jit(solution)/shard_map/while | solution.py:81
  145.3 102.2 %while.21 = (s32[]{:T(128)}, bf16[2,128,8,512]{3,2,1,0:T(8,128)(2,1)}, s32[2,128]{1,0:T(2,128)S(1)}, s32[2048]{0:T(1024)S(1)}, s32[2048]{0:T(1024)S(1)}, /*index...) while((s32[]{:T(128)}, ...), condition=%wide.region_14.15_spmd, body=%wide.region_11.14_spmd.sunk | while | flops 4389332992 | bytes 118603368 | solution.py:81
  147.3 16.3 %bitcast_reduce_fusion.2 = (f32[8,4,128]{2,1,0:T(4,128)S(1)}, f32[8,128,4,2048]{3,1,2,0:T(8,128)}) fusion(pred[128,2048]{1,0:T(8,128)(4,1)S(1)} %and_and_fusion.2, bf16[2048,8,128]{2,0,1:T(8,128)(2,1)} %get-tuple-element.282, bf16[1,128,8,4,128]{4,3,2,1,0:T(4,128)(2,1)S(1)} %constant_dynamic-slice_fusion.4), kind=kOutput, calls=%fused_computation.8.clone.1 | convolution fusion | flops 2172645376 | bytes 39075840 | tf_op jit(solution)/shard_map/while/body/eval_jaxpr/qjgd,kjd->jgqk/dot_general | solution.py:35
  163.5 15.0 %fusion.37 = f32[8,4,128]{2,1,0:T(4,128)S(1)} fusion(f32[8,128,4,2048]{3,1,2,0:T(8,128)} %get-tuple-element.232, f32[8,4,128]{2,1,0:T(4,128)S(1)} %get-tuple-element.233, pred[128,2048]{1,0:T(8,128)(4,1)S(1)} %and_and_fusion.2), kind=kLoop, calls=%fused_computation.11.clone.1 | loop fusion | flops 33550336 | bytes 33849344 | tf_op jit(solution)/shard_map/while/body/eval_jaxpr/reduce_sum | solution.py:47
  178.5 15.9 %fusion.38 = bf16[128,8,4,128]{0,3,2,1:T(8,128)(2,1)S(1)} fusion(bf16[2048,8,128]{0,2,1:T(8,128)(2,1)} %get-tuple-element.283, f32[8,128,4,2048]{3,1,2,0:T(8,128)} %get-tuple-element.232, f32[8,4,128]{2,1,0:T(4,128)S(1)} %get-tuple-element.233, pred[128,2048]{1,0:T(8,128)(4,1)S(1)} %and_and_fusion.2, f32[128,8,4]{0,2,1:T(4,128)S(1)} %bitcast.110), kind=kOutput, calls=%fused_computation.19.clone.1 | convolution fusion | flops 2182086656 | bytes 39092224 | tf_op jit(solution)/shard_map/while/body/eval_jaxpr/jgqk,kjd->qjgd/dot_general | solution.py:48
  198.3 16.3 %bitcast_reduce_fusion.2 = (f32[8,4,128]{2,1,0:T(4,128)S(1)}, f32[8,128,4,2048]{3,1,2,0:T(8,128)}) fusion(pred[128,2048]{1,0:T(8,128)(4,1)S(1)} %and_and_fusion.2, bf16[2048,8,128]{2,0,1:T(8,128)(2,1)} %get-tuple-element.282, bf16[1,128,8,4,128]{4,3,2,1,0:T(4,128)(2,1)S(1)} %constant_dynamic-slice_fusion.4), kind=kOutput, calls=%fused_computation.8.clone.1 | convolution fusion | flops 2172645376 | bytes 39075840 | tf_op jit(solution)/shard_map/while/body/eval_jaxpr/qjgd,kjd->jgqk/dot_general | solution.py:35
  214.6 15.0 %fusion.37 = f32[8,4,128]{2,1,0:T(4,128)S(1)} fusion(f32[8,128,4,2048]{3,1,2,0:T(8,128)} %get-tuple-element.232, f32[8,4,128]{2,1,0:T(4,128)S(1)} %get-tuple-element.233, pred[128,2048]{1,0:T(8,128)(4,1)S(1)} %and_and_fusion.2), kind=kLoop, calls=%fused_computation.11.clone.1 | loop fusion | flops 33550336 | bytes 33849344 | tf_op jit(solution)/shard_map/while/body/eval_jaxpr/reduce_sum | solution.py:47
  229.6 15.9 %fusion.38 = bf16[128,8,4,128]{0,3,2,1:T(8,128)(2,1)S(1)} fusion(bf16[2048,8,128]{0,2,1:T(8,128)(2,1)} %get-tuple-element.283, f32[8,128,4,2048]{3,1,2,0:T(8,128)} %get-tuple-element.232, f32[8,4,128]{2,1,0:T(4,128)S(1)} %get-tuple-element.233, pred[128,2048]{1,0:T(8,128)(4,1)S(1)} %and_and_fusion.2, f32[128,8,4]{0,2,1:T(4,128)S(1)} %bitcast.110), kind=kOutput, calls=%fused_computation.19.clone.1 | convolution fusion | flops 2182086656 | bytes 39092224 | tf_op jit(solution)/shard_map/while/body/eval_jaxpr/jgqk,kjd->qjgd/dot_general | solution.py:48
  247.5 4.2 %reshape_reshape_reshape.7 = bf16[32,8,4096]{2,1,0:T(8,128)(2,1)} reshape(bf16[2,128,8,512]{3,2,1,0:T(8,128)(2,1)} %get-tuple-element.80) | data formatting | bytes 4194304 | tf_op jit(solution)/shard_map/reshape;reshape;reshape | solution.py:158
  251.7 7.1 %all-to-all-start.4 = ((bf16[32,8,4096]{2,1,0:T(8,128)(2,1)}), bf16[32,8,4096]{2,1,0:T(8,128)(2,1)S(1)}, u32[]{:S(2)}, u32[]{:S(2)}) async-start(bf16[32,8,4096]{2,1,0:T(8,128)(2,1)} %reshape_reshape_reshape.7), calls=%async_computation.4 | async-start | bytes 4194304 | tf_op jit(solution)/shard_map/all_to_all | solution.py:157
  258.9 46.5 %all-to-all-done.4 = bf16[32,8,4096]{2,1,0:T(8,128)(2,1)S(1)} async-done(((bf16[32,8,4096]{2,1,0:T(8,128)(2,1)}), bf16[32,8,4096]{2,1,0:T(8,128)(2,1)S(1)}, u32[]{:S(2)}, u32[]{:S(2)}) %all-to-all-start.4) | async-done | bytes 2097184 | tf_op jit(solution)/shard_map/all_to_all | solution.py:157
  305.4 2.2 gather_fusion
  (95 shorter events, 22.5 us)
Async XLA Ops:
  6.5 64.2 %copy-start.2 = (s32[1,2]{1,0:T(1,128)S(1)}, s32[1,2]{1,0:T(1,128)}, u32[]{:S(2)}) copy-start(s32[1,2]{1,0:T(1,128)} %param.13) | copy-start | bytes 28
  6.5 127.3 %all-gather.4.cloned.1.call-start = ((), (), s32[]{:S(2)}) async-start(), calls=%async_computation.5 | async-start | bytes 4718592 | tf_op jit(solution)/shard_map/all_gather | solution.py:141
  9.0 66.3 %copy-start = (s32[128]{0:T(128)}, s32[128]{0:T(128)S(1)}, u32[]{:S(2)}) copy-start(s32[128]{0:T(128)S(1)} %fusion.26) | copy-start | bytes 1540
  39.7 98.9 %all-gather.6.cloned.1.call-start = ((), (), s32[]{:S(2)}) async-start(), calls=%async_computation.6 | async-start | bytes 4718592 | tf_op jit(solution)/shard_map/all_gather | solution.py:142
  64.4 14.9 %all-to-all-start = ((s32[32,1,8]{2,1,0:T(1,128)}), s32[32,1,8]{2,1,0:T(1,128)S(1)}, u32[]{:S(2)}, u32[]{:S(2)}) async-start(s32[32,1,8]{2,1,0:T(1,128)} %bitcast.17), calls=%async_computation | async-start | bytes 32768 | tf_op jit(solution)/shard_map/all_to_all | solution.py:130
  79.3 51.9 %all-to-all-start.1 = ((bf16[32,8,4096]{2,1,0:T(8,128)(2,1)}), bf16[32,8,4096]{2,1,0:T(8,128)(2,1)S(1)}, u32[]{:S(2)}, u32[]{:S(2)}) async-start(bf16[32,8,4096]{2,1,0:T(8,128)(2,1)} %bitcast.22), calls=%async_computation.1 | async-start | bytes 4194304 | tf_op jit(solution)/shard_map/all_to_all | solution.py:109
  247.5 11.4 %copy-start.1 = (s32[128]{0:T(128)S(1)}, s32[128]{0:T(128)}, u32[]{:S(2)}) copy-start(s32[128]{0:T(128)} %copy-done) | copy-start | bytes 1540
  251.7 53.6 %all-to-all-start.4 = ((bf16[32,8,4096]{2,1,0:T(8,128)(2,1)}), bf16[32,8,4096]{2,1,0:T(8,128)(2,1)S(1)}, u32[]{:S(2)}, u32[]{:S(2)}) async-start(bf16[32,8,4096]{2,1,0:T(8,128)(2,1)} %reshape_reshape_reshape.7), calls=%async_computation.4 | async-start | bytes 4194304 | tf_op jit(solution)/shard_map/all_to_all | solution.py:157
Sparse Core Ops, SparseCore 0:
  39.8 32.8 all-gather.3
  74.6 34.5 all-gather.5
where the time goes:
time: 319 us; the launch traced here: 314 us
  waiting for transfers between devices  76.9 us (24%)
  matrix products  64.3 us (20%)
  blocking collectives  61.5 us (19%)
  local copies, waits for them, and re-layouts  40.5 us (13%)
  other arithmetic  38.6 us (12%)
  starting transfers between devices  18.7 us (6%)
  between operations  13.5 us (4%)
    all_to_all x1, waiting for transfers between devices, body(): lax.all_to_all(back_rows.reshape(dp_count, slot_rows, back_rows.shape[1])...  46.5 us
    dot_general x2, matrix products, attend(): jnp.einsum('qjgd,kjd->jgqk', block_of_queries, key_heads, preferred_eleme...  32.5 us
    dot_general x2, matrix products, attend(): jnp.einsum('jgqk,kjd->qjgd', weights.astype(jnp.bfloat16), value_heads, p...  31.8 us
    reduce_sum x2, other arithmetic, attend(): totals = jnp.sum(weights, axis=3)  30 us
    all_to_all x1, blocking collectives, body(): lax.all_to_all(send_key.reshape(dp_count, slot_rows, key_rows.shape[1]),...  28.1 us
    all_to_all x1, waiting for transfers between devices, body(): lax.all_to_all(send_query.reshape(dp_count, slot_rows, query_rows.shape[1...  26.4 us
    all_to_all x1, blocking collectives, body(): lax.all_to_all(send_value.reshape(dp_count, slot_rows, token_values.shape...  20.3 us
    all_gather x1, blocking collectives, body(): lax.all_gather(local_index, 'ctx', axis=0, tiled=True)  13.1 us
  transfers between devices with their start and end apart: 5, of which 3 were waited for; matrix products, arithmetic and copies ran while one was open for 7% of the time, Pallas kernels for 0%

commit v1 on v0

v1 whole, which is shorter than its diff:
```python
import math

import jax
import jax.numpy as jnp
from jax import lax
from jax.experimental import pallas as pl
from jax.experimental.pallas import tpu as pltpu
from jax.sharding import PartitionSpec as P

KV_HEADS = 8
HEAD = 128
PER_KV = 4
GROUPS = 32
SLOT = 8
QW = PER_KV * HEAD
ROW_W = QW + 2 * HEAD
EMPTY = 64.0
FAR = 16384.0
TQ = 256
TK = 256


def slot_targets(group_col):
    rows = group_col.shape[0]
    col = jnp.broadcast_to(group_col.astype(jnp.float32), (rows, rows))
    row = jnp.transpose(col)
    earlier = lax.broadcasted_iota(jnp.int32, (rows, rows), 0) < lax.broadcasted_iota(
        jnp.int32, (rows, rows), 1
    )
    same = jnp.where((col == row) & earlier, 1.0, 0.0)
    position = jnp.sum(same, axis=0, keepdims=True)
    return row[0:1, :] * float(SLOT) + position


def pack_kernel(group_ref, q_ref, k_ref, v_ref, out_ref, pick_ref):
    slots = GROUPS * SLOT
    rows = q_ref.shape[0]

    @pl.when(pl.program_id(0) == 0)
    def _():
        target = slot_targets(group_ref[...])
        slot = lax.broadcasted_iota(jnp.int32, (slots, rows), 0).astype(jnp.float32)
        pick_ref[...] = jnp.where(slot == target, 1.0, 0.0).astype(jnp.bfloat16)

    pick = pick_ref[...]

    def moved(x):
        return jnp.dot(pick, x, preferred_element_type=jnp.float32)

    empty = 1.0 - jnp.sum(pick.astype(jnp.float32), axis=1, keepdims=True)
    v_out = moved(v_ref[...]) + empty * EMPTY
    shape = (GROUPS, 1, SLOT)
    out_ref[:, :, :, 0:QW] = moved(q_ref[...]).astype(jnp.bfloat16).reshape(shape + (QW,))
    out_ref[:, :, :, QW : QW + HEAD] = (
        moved(k_ref[...]).astype(jnp.bfloat16).reshape(shape + (HEAD,))
    )
    out_ref[:, :, :, QW + HEAD :] = v_out.astype(jnp.bfloat16).reshape(shape + (HEAD,))


def pack(group, q, k, v):
    rows = q.shape[0]
    return pl.pallas_call(
        pack_kernel,
        grid=(KV_HEADS,),
        in_specs=[
            pl.BlockSpec((rows, 1), lambda j: (0, 0)),
            pl.BlockSpec((rows, QW), lambda j: (0, j)),
            pl.BlockSpec((rows, HEAD), lambda j: (0, j)),
            pl.BlockSpec((rows, HEAD), lambda j: (0, j)),
        ],
        out_specs=pl.BlockSpec((GROUPS, 1, SLOT, ROW_W), lambda j: (0, j, 0, 0)),
        out_shape=jax.ShapeDtypeStruct((GROUPS, KV_HEADS, SLOT, ROW_W), jnp.bfloat16),
        scratch_shapes=[pltpu.VMEM((GROUPS * SLOT, rows), jnp.bfloat16)],
        name="pack",
    )(group, q, k, v)


def unpack_kernel(group_ref, o_ref, out_ref, pick_ref):
    slots = GROUPS * SLOT
    rows = out_ref.shape[0]

    @pl.when(pl.program_id(0) == 0)
    def _():
        target = slot_targets(group_ref[...])
        slot = lax.broadcasted_iota(jnp.int32, (slots, rows), 0).astype(jnp.float32)
        pick_ref[...] = jnp.transpose(jnp.where(slot == target, 1.0, 0.0)).astype(jnp.bfloat16)

    x = o_ref[...].reshape(slots, QW)
    out_ref[...] = jnp.dot(pick_ref[...], x, preferred_element_type=jnp.float32).astype(
        jnp.bfloat16
    )


def unpack(group, o):
    rows = group.shape[0]
    return pl.pallas_call(
        unpack_kernel,
        grid=(KV_HEADS,),
        in_specs=[
            pl.BlockSpec((rows, 1), lambda j: (0, 0)),
            pl.BlockSpec((GROUPS, 1, SLOT, QW), lambda j: (0, j, 0, 0)),
        ],
        out_specs=pl.BlockSpec((rows, QW), lambda j: (0, j)),
        out_shape=jax.ShapeDtypeStruct((rows, KV_HEADS * QW), jnp.bfloat16),
        scratch_shapes=[pltpu.VMEM((rows, GROUPS * SLOT), jnp.bfloat16)],
        name="unpack",
    )(group, o)


def attend_kernel(len_ref, q_ref, k_ref, v_ref, o_ref, key_ref, mask_ref, first_ref):
    count = k_ref.shape[0]
    block = pl.program_id(0)
    chunk = 128

    @pl.when(block == 0)
    def _():
        first_len = len_ref[0, 0].astype(jnp.float32)
        lower = jnp.where(
            lax.broadcasted_iota(jnp.int32, (chunk, chunk), 0)
            > lax.broadcasted_iota(jnp.int32, (chunk, chunk), 1),
            1.0,
            0.0,
        ).astype(jnp.bfloat16)
        lane = lax.broadcasted_iota(jnp.int32, (chunk, chunk), 1).astype(jnp.float32)
        row = lax.broadcasted_iota(jnp.int32, (chunk, chunk), 0).astype(jnp.float32)

        def one(i, carry):
            seen, first = carry
            at = pl.ds(pl.multiple_of(i * chunk, chunk), chunk)
            head = v_ref[at, :].astype(jnp.float32)[:, 0:1]
            used = jnp.broadcast_to(jnp.where(head < 0.5 * EMPTY, 1.0, 0.0), (chunk, chunk))
            rank = seen + jnp.dot(
                lower, used.astype(jnp.bfloat16), preferred_element_type=jnp.float32
            )
            code = jnp.where(used > 0.5, jnp.where(rank < first_len, 0.0, 1.0), 2.0)
            key_ref[at, 0:chunk] = k_ref[at, :]
            key_ref[at, chunk:] = jnp.where(lane == code, 1.0, 0.0).astype(jnp.bfloat16)
            mask_ref[at, :] = jnp.where(
                (lane < 2.5) & (lane != code), -FAR, 0.0
            ).astype(jnp.bfloat16)
            place = jnp.where(code == 1.0, row + (i * chunk).astype(jnp.float32), float(count))
            seen = seen + jnp.sum(used, axis=0, keepdims=True)
            return seen, jnp.minimum(first, jnp.min(place, axis=0, keepdims=True))

        start = (jnp.zeros((1, chunk), jnp.float32), jnp.full((1, chunk), float(count)))
        _, first = lax.fori_loop(0, count // chunk, one, start)
        first_ref[0] = jnp.min(first).astype(jnp.int32)

    first = first_ref[0]
    q_start = block * TQ
    scale = 1.0 / math.sqrt(HEAD)
    mask = mask_ref[pl.ds(pl.multiple_of(q_start, TQ), TQ), :]
    q = jnp.concatenate(
        [
            jnp.concatenate([q_ref[:, h * HEAD : (h + 1) * HEAD], mask], axis=1)
            for h in range(PER_KV)
        ],
        axis=0,
    )

    def step(b, carry, diagonal):
        m, total, acc = carry
        at = pl.ds(pl.multiple_of(b * TK, TK), TK)
        s = lax.dot_general(
            q, key_ref[at, :], (((1,), (1,)), ((), ())), preferred_element_type=jnp.float32
        )
        if diagonal:
            t = lax.broadcasted_iota(jnp.int32, (TQ, TK), 0)
            u = lax.broadcasted_iota(jnp.int32, (TQ, TK), 1)
            bias = jnp.where(u <= t, 0.0, -2.0 * FAR)
            s = (s.reshape(PER_KV, TQ, TK) + bias[None]).reshape(PER_KV * TQ, TK)
        m_new = jnp.maximum(m, jnp.max(s, axis=1, keepdims=True))
        w = jnp.exp((s - m_new) * scale)
        fade = jnp.exp((m - m_new) * scale)
        total = total * fade + jnp.sum(w, axis=1, keepdims=True)
        acc = acc * fade + jnp.dot(
            w.astype(jnp.bfloat16), v_ref[at, :], preferred_element_type=jnp.float32
        )
        return m_new, total, acc

    lowest = jnp.where(q_start >= first, first // TK, 0)
    rows = PER_KV * TQ
    carry = (
        jnp.full((rows, 1), -4.0 * FAR, jnp.float32),
        jnp.zeros((rows, 1), jnp.float32),
        jnp.zeros((rows, HEAD), jnp.float32),
    )
    carry = lax.fori_loop(lowest, block, lambda b, c: step(b, c, False), carry)
    _, total, acc = step(block, carry, True)
    out = (acc / total).astype(jnp.bfloat16)
    for h in range(PER_KV):
        o_ref[:, h * HEAD : (h + 1) * HEAD] = out[h * TQ : (h + 1) * TQ, :]


def attend(lengths, rows):
    count = rows.shape[0]
    return pl.pallas_call(
        attend_kernel,
        grid=(count // TQ,),
        in_specs=[
            pl.BlockSpec(memory_space=pltpu.SMEM),
            pl.BlockSpec((TQ, QW), lambda i: (i, 0)),
            pl.BlockSpec((count, HEAD), lambda i: (0, PER_KV)),
            pl.BlockSpec((count, HEAD), lambda i: (0, PER_KV + 1)),
        ],
        out_specs=pl.BlockSpec((TQ, QW), lambda i: (i, 0)),
        out_shape=jax.ShapeDtypeStruct((count, QW), jnp.bfloat16),
        scratch_shapes=[
            pltpu.VMEM((count, 2 * HEAD), jnp.bfloat16),
            pltpu.VMEM((count, HEAD), jnp.bfloat16),
            pltpu.SMEM((1,), jnp.int32),
        ],
        name="attend",
    )(lengths, rows, rows, rows)


def body(query_rows, key_rows, token_values, group_of_row, doc_lengths):
    devices = lax.axis_size("dp") * lax.axis_size("ctx")
    packed = pack(group_of_row, query_rows, key_rows, token_values)
    arrived = lax.all_to_all(
        packed.reshape(devices, SLOT, ROW_W), ("dp", "ctx"), split_axis=0, concat_axis=0, tiled=True
    )
    result = attend(doc_lengths, arrived.reshape(devices * SLOT, ROW_W))
    returned = lax.all_to_all(
        result.reshape(devices, SLOT, QW), ("dp", "ctx"), split_axis=0, concat_axis=0, tiled=True
    )
    return unpack(group_of_row, returned.reshape(GROUPS, KV_HEADS, SLOT, QW))


def solution(mesh):
    rows = P(("dp", "ctx"), None)
    return jax.shard_map(
        body,
        mesh=mesh,
        in_specs=(rows, rows, rows, rows, P("dp", None)),
        out_specs=rows,
        check_vma=False,
    )
```

time: 319 us -> 206 us (0.65); the launches traced: 314 us -> 206 us
  blocking collectives: 61.5 us -> 151 us
  waiting for transfers between devices: 76.9 us -> 0 us
  matrix products: 64.3 us -> 0 us
  Pallas kernels: 0 us -> 53 us
  local copies, waits for them, and re-layouts: 40.5 us -> 1.38 us
  other arithmetic: 38.6 us -> 0 us
  starting transfers between devices: 18.7 us -> 0 us
  between operations: 13.5 us -> 0.01 us
    all_to_all x2, blocking collectives: 48.4 us -> 151 us  [the longest x1 90.5 us: body(): lax.all_to_all(packed.reshape(devices, SLOT, ROW_W), ('dp', 'ctx'), split...]
    all_to_all x3 -> x0, waiting for transfers between devices: 76.9 us -> none  [the longest x1 46.5 us: body(): lax.all_to_all(back_rows.reshape(dp_count, slot_rows, back_rows.shape[1])...]
    dot_general x4 -> x0, matrix products: 64.3 us -> none  [the longest x2 32.5 us: attend(): jnp.einsum('qjgd,kjd->jgqk', block_of_queries, key_heads, preferred_eleme...]
    pallas_call x0 -> x3, Pallas kernels: none -> 53 us  [the longest x1 39.8 us: attend(): pl.pallas_call(attend_kernel, grid=(count // TQ,), in_specs=[pl.BlockSpec...]
    reduce_sum x20 -> x0, other arithmetic: 35.5 us -> none  [the longest x2 30 us: attend(): totals = jnp.sum(weights, axis=3)]
    all_to_all x3 -> x0, starting transfers between devices: 18.7 us -> none  [the longest x1 7.14 us: body(): lax.all_to_all(back_rows.reshape(dp_count, slot_rows, back_rows.shape[1])...]
    all_gather x1 -> x0, blocking collectives: 13.1 us -> none  [body(): lax.all_gather(local_index, 'ctx', axis=0, tiled=True)]
    while x2 -> x0, local copies, waits for them, and re-layouts: 11.5 us -> none  [attend_all(): result = lax.map(one_block, shaped)]
  transfers between devices with their start and end apart: 5 -> 0, of which waited for: 3 -> 0; matrix products, arithmetic and copies ran while one was open for 7% -> 0% of each run, Pallas kernels for 0% -> 0%
where the time goes in v1:
time: 206 us
  blocking collectives  151 us (73%)
  Pallas kernels  53 us (26%)
    all_to_all x1, blocking collectives, body(): lax.all_to_all(packed.reshape(devices, SLOT, ROW_W), ('dp', 'ctx'), split...  90.5 us
    all_to_all x1, blocking collectives, body(): lax.all_to_all(result.reshape(devices, SLOT, QW), ('dp', 'ctx'), split_ax...  61 us
    pallas_call x1, Pallas kernels, attend(): pl.pallas_call(attend_kernel, grid=(count // TQ,), in_specs=[pl.BlockSpec...  39.8 us
    pallas_call x1, Pallas kernels, pack(): pl.pallas_call(pack_kernel, grid=(KV_HEADS,), in_specs=[pl.BlockSpec((row...  6.88 us
    pallas_call x1, Pallas kernels, unpack(): pl.pallas_call(unpack_kernel, grid=(KV_HEADS,), in_specs=[pl.BlockSpec((r...  6.34 us

profile of v1, /device:TPU:1, one launch (start us, length us, event | category | flops | bytes accessed | tf_op | source)
XLA Modules:
  0.0 205.9 jit_solution(16687908417828227225)
XLA Ops:
  0.0 1.4 copy.7.group_ref
  1.4 6.9 %pack.1 = bf16[32,8,8,768]{3,2,1,0:T(8,128)(2,1)} custom-call(s32[128,1]{1,0:T(8,128)} %copy.7.group_ref, bf16[128,4096]{1,0:T(8,128)(2,1)} %q_ref.1, bf16[128,1024]{1,0:T(8,128)(2,1)} %k_ref.1, bf16[128,1024]{1,0:T(8,128)(2,1)} %v_ref.1), custom_call_target="tpu_custom_call" | custom-call | tf_op jit(solution)/shard_map/pack/pallas_call | solution.py:62
  8.3 90.5 %all_to_all.10 = bf16[256,8,768]{2,1,0:T(8,128)(2,1)} all-to-all(bf16[256,8,768]{2,1,0:T(8,128)(2,1)} %bitcast.7), channel_id=1, replica_groups=mesh['dp'=32,'ctx'=8] {'dp','ctx'}, dimensions={0} | all-to-all | bytes 6291456 | tf_op jit(solution)/shard_map/all_to_all | solution.py:220
  98.8 39.8 %attend.1 = bf16[2048,512]{1,0:T(8,128)(2,1)} custom-call(s32[1,2]{1,0:T(1,128)} %len_ref.1, bf16[2048,768]{1,0:T(8,128)(2,1)} %bitcast.4, bf16[2048,768]{1,0:T(8,128)(2,1)} %bitcast.5, bf16[2048,768]{1,0:T(8,128)(2,1)} %bitcast.6), custom_call_target="tpu_custom_call" | custom-call | tf_op jit(solution)/shard_map/attend/pallas_call | solution.py:197
  138.6 61.0 %all_to_all.11 = bf16[256,8,512]{2,1,0:T(8,128)(2,1)} all-to-all(bf16[256,8,512]{2,1,0:T(8,128)(2,1)} %bitcast.9), channel_id=1, replica_groups=mesh['dp'=32,'ctx'=8] {'dp','ctx'}, dimensions={0} | all-to-all | bytes 4194304 | tf_op jit(solution)/shard_map/all_to_all | solution.py:224
  199.6 6.3 %unpack.1 = bf16[128,4096]{1,0:T(8,128)(2,1)} custom-call(s32[128,1]{1,0:T(8,128)} %copy.7.group_ref, bf16[32,8,8,512]{3,2,1,0:T(8,128)(2,1)} %bitcast.8), custom_call_target="tpu_custom_call" | custom-call | tf_op jit(solution)/shard_map/unpack/pallas_call | solution.py:96

commit v2 on v1

v2 whole, which is shorter than its diff:
```python
import functools
import math

import jax
import jax.numpy as jnp
from jax import lax
from jax.experimental import pallas as pl
from jax.experimental.pallas import tpu as pltpu
from jax.sharding import PartitionSpec as P

KV_HEADS = 8
HEAD = 128
PER_KV = 4
GROUPS = 32
SLOT = 8
QW = PER_KV * HEAD
HALF = QW // 2
EMPTY = 64.0
FAR = 16384.0
TQ = 256
TK = 256
VALUE_ROWS = HEAD + 16


def slot_targets(group_col):
    rows = group_col.shape[0]
    col = jnp.broadcast_to(group_col.astype(jnp.float32), (rows, rows))
    row = jnp.transpose(col)
    earlier = lax.broadcasted_iota(jnp.int32, (rows, rows), 0) < lax.broadcasted_iota(
        jnp.int32, (rows, rows), 1
    )
    same = jnp.where((col == row) & earlier, 1.0, 0.0)
    position = jnp.sum(same, axis=0, keepdims=True)
    return row[0:1, :] * float(SLOT) + position


def pack_kernel(group_ref, q_ref, k_ref, v_ref, near_ref, far_ref, pick_ref):
    slots = GROUPS * SLOT
    rows = q_ref.shape[0]

    @pl.when(pl.program_id(0) == 0)
    def _():
        target = slot_targets(group_ref[...])
        slot = lax.broadcasted_iota(jnp.int32, (slots, rows), 0).astype(jnp.float32)
        pick_ref[...] = jnp.where(slot == target, 1.0, 0.0).astype(jnp.bfloat16)

    pick = pick_ref[...]

    def moved(x):
        return jnp.dot(pick, x, preferred_element_type=jnp.float32)

    def laid(x):
        return x.reshape(GROUPS, 1, SLOT, x.shape[1]).astype(jnp.bfloat16)

    empty = 1.0 - jnp.sum(pick.astype(jnp.float32), axis=1, keepdims=True)
    near_ref[:, :, :, 0:HALF] = laid(moved(q_ref[:, 0:HALF]))
    near_ref[:, :, :, HALF : HALF + HEAD] = laid(moved(k_ref[...]))
    near_ref[:, :, :, HALF + HEAD :] = laid(moved(v_ref[...]) + empty * EMPTY)
    far_ref[...] = laid(moved(q_ref[:, HALF:]))


def pack(group, q, k, v):
    rows = q.shape[0]
    widths = (HALF + 2 * HEAD, HALF)
    return pl.pallas_call(
        pack_kernel,
        grid=(KV_HEADS,),
        in_specs=[
            pl.BlockSpec((rows, 1), lambda j: (0, 0)),
            pl.BlockSpec((rows, QW), lambda j: (0, j)),
            pl.BlockSpec((rows, HEAD), lambda j: (0, j)),
            pl.BlockSpec((rows, HEAD), lambda j: (0, j)),
        ],
        out_specs=[
            pl.BlockSpec((GROUPS, 1, SLOT, w), lambda j: (0, j, 0, 0)) for w in widths
        ],
        out_shape=[
            jax.ShapeDtypeStruct((GROUPS, KV_HEADS, SLOT, w), jnp.bfloat16) for w in widths
        ],
        scratch_shapes=[pltpu.VMEM((GROUPS * SLOT, rows), jnp.bfloat16)],
        name="pack",
    )(group, q, k, v)


def unpack_kernel(group_ref, near_ref, far_ref, out_ref, pick_ref):
    slots = GROUPS * SLOT
    rows = out_ref.shape[0]

    @pl.when(pl.program_id(0) == 0)
    def _():
        target = slot_targets(group_ref[...])
        slot = lax.broadcasted_iota(jnp.int32, (slots, rows), 0).astype(jnp.float32)
        pick_ref[...] = jnp.transpose(jnp.where(slot == target, 1.0, 0.0)).astype(jnp.bfloat16)

    for part, ref in enumerate((near_ref, far_ref)):
        out_ref[:, part * HALF : (part + 1) * HALF] = jnp.dot(
            pick_ref[...], ref[...].reshape(slots, HALF), preferred_element_type=jnp.float32
        ).astype(jnp.bfloat16)


def unpack(group, near, far):
    rows = group.shape[0]
    part = pl.BlockSpec((GROUPS, 1, SLOT, HALF), lambda j: (0, j, 0, 0))
    return pl.pallas_call(
        unpack_kernel,
        grid=(KV_HEADS,),
        in_specs=[pl.BlockSpec((rows, 1), lambda j: (0, 0)), part, part],
        out_specs=pl.BlockSpec((rows, QW), lambda j: (0, j)),
        out_shape=jax.ShapeDtypeStruct((rows, KV_HEADS * QW), jnp.bfloat16),
        scratch_shapes=[pltpu.VMEM((rows, GROUPS * SLOT), jnp.bfloat16)],
        name="unpack",
    )(group, near, far)


def attend_kernel(heads, len_ref, q_ref, k_ref, v_ref, o_ref, key_ref, vt_ref, mask_ref, acc_ref, first_ref):
    count = k_ref.shape[0]
    block = pl.program_id(0)
    chunk = 128

    @pl.when(block == 0)
    def _():
        first_len = len_ref[0, 0].astype(jnp.float32)
        r = lax.broadcasted_iota(jnp.int32, (chunk, chunk), 0)
        l = lax.broadcasted_iota(jnp.int32, (chunk, chunk), 1)
        lower = jnp.where(r > l, 1.0, 0.0).astype(jnp.bfloat16)
        lane = l.astype(jnp.float32)
        row = r.astype(jnp.float32)
        seen = jnp.zeros((1, chunk), jnp.float32)
        first = jnp.full((1, chunk), float(count))
        ones = jnp.where(lax.broadcasted_iota(jnp.int32, (VALUE_ROWS - HEAD, chunk), 0) == 0, 1.0, 0.0).astype(jnp.bfloat16)
        for i in range(count // chunk):
            at = pl.ds(i * chunk, chunk)
            v = v_ref[at, :]
            vf = v.astype(jnp.float32)
            used = jnp.broadcast_to(jnp.where(vf[:, 0:1] < 0.5 * EMPTY, 1.0, 0.0), (chunk, chunk))
            rank = seen + jnp.dot(lower, used.astype(jnp.bfloat16), preferred_element_type=jnp.float32)
            code = jnp.where(used > 0.5, jnp.where(rank < first_len, 0.0, 1.0), 2.0)
            key_ref[at, 0:chunk] = k_ref[at, :]
            key_ref[at, chunk:] = jnp.where(lane == code, 1.0, 0.0).astype(jnp.bfloat16)
            mask_ref[at, :] = jnp.where((lane < 2.5) & (lane != code), -FAR, 0.0).astype(jnp.bfloat16)
            vt_ref[0:HEAD, at] = jnp.transpose(vf).astype(jnp.bfloat16)
            vt_ref[HEAD:, at] = ones
            place = jnp.where(code == 1.0, row + float(i * chunk), float(count))
            seen = seen + jnp.sum(used, axis=0, keepdims=True)
            first = jnp.minimum(first, jnp.min(place, axis=0, keepdims=True))
        first_ref[0] = jnp.min(first).astype(jnp.int32)
    first = first_ref[0]
    q_start = block * TQ
    scale = math.log2(math.e) / math.sqrt(HEAD)
    mask = mask_ref[pl.ds(pl.multiple_of(q_start, TQ), TQ), :]
    qs = [jnp.concatenate([q_ref[:, h*HEAD:(h+1)*HEAD], mask], axis=1) for h in range(heads)]
    def step(b, ms, kind):
        at = pl.ds(pl.multiple_of(b * TK, TK), TK)
        key = key_ref[at, :]
        vt = vt_ref[:, at]
        new = []
        if kind == "diag":
            t = q_start + lax.broadcasted_iota(jnp.int32, (TK, TQ), 1)
            u = b * TK + lax.broadcasted_iota(jnp.int32, (TK, TQ), 0)
            bias = jnp.where(u <= t, 0.0, -2.0 * FAR)
        for h in range(heads):
            s = lax.dot_general(key, qs[h], (((1,), (1,)), ((), ())), preferred_element_type=jnp.float32)
            if kind == "diag":
                s = s + bias
            m_new = jnp.maximum(ms[h], jnp.max(s, axis=0, keepdims=True))
            w = jnp.exp2((s - m_new) * scale).astype(jnp.bfloat16)
            fade = jnp.exp2((ms[h] - m_new) * scale)
            acc_ref[h] = acc_ref[h] * fade + jnp.dot(vt, w, preferred_element_type=jnp.float32)
            new.append(m_new)
        return tuple(new)
    acc_ref[...] = jnp.zeros_like(acc_ref)
    lowest = jnp.where(q_start >= first, first // TK, 0)
    last = (q_start + TQ - 1) // TK
    ms = tuple(jnp.full((1, TQ), -4.0 * FAR, jnp.float32) for _ in range(heads))
    full = q_start // TK
    ms = lax.fori_loop(lowest, full, lambda b, c: step(b, c, "full"), ms)
    ndiag = max(TQ // TK, 1)
    for d in range(ndiag):
        ms = step(full + d, ms, "diag")
    for h in range(heads):
        acc = acc_ref[h]
        o = acc[0:HEAD] * (1.0 / acc[HEAD:HEAD+1])
        o_ref[:, h*HEAD:(h+1)*HEAD] = jnp.transpose(o).astype(jnp.bfloat16)
def attend(lengths, q, kv):
    count, width = q.shape
    used = kv.shape[1] // HEAD
    heads = PER_KV // 2
    return pl.pallas_call(
        functools.partial(attend_kernel, heads),
        grid=(count // TQ,),
        in_specs=[
            pl.BlockSpec(memory_space=pltpu.SMEM),
            pl.BlockSpec((TQ, heads * HEAD), lambda i: (i, 0)),
            pl.BlockSpec((count, HEAD), lambda i: (0, used - 2)),
            pl.BlockSpec((count, HEAD), lambda i: (0, used - 1)),
        ],
        out_specs=pl.BlockSpec((TQ, heads * HEAD), lambda i: (i, 0)),
        out_shape=jax.ShapeDtypeStruct((count, heads * HEAD), jnp.bfloat16),
        scratch_shapes=[
            pltpu.VMEM((count, 2 * HEAD), jnp.bfloat16),
            pltpu.VMEM((VALUE_ROWS, count), jnp.bfloat16),
            pltpu.VMEM((count, HEAD), jnp.bfloat16),
            pltpu.VMEM((heads, VALUE_ROWS, TQ), jnp.float32),
            pltpu.SMEM((1,), jnp.int32),
        ],
        cost_estimate=pl.CostEstimate(
            flops=2 * heads * count * count * HEAD, transcendentals=heads * count * count // 2, bytes_accessed=6 * count * width
        ),
        name="attend",
    )(lengths, q, kv, kv)


def exchange(x):
    devices = lax.axis_size("dp") * lax.axis_size("ctx")
    return lax.all_to_all(
        x.reshape(devices, SLOT, x.shape[-1]), ("dp", "ctx"), split_axis=0, concat_axis=0, tiled=True
    )


def body(query_rows, key_rows, token_values, group_of_row, doc_lengths):
    def flat(x):
        return x.reshape(x.shape[0] * SLOT, x.shape[-1])

    def home(x):
        return exchange(x).reshape(GROUPS, KV_HEADS, SLOT, HALF)

    near, far = pack(group_of_row, query_rows, key_rows, token_values)
    near, far = lax.optimization_barrier((exchange(near), far))
    near = flat(near)
    far = flat(exchange(far))
    near_out = home(attend(doc_lengths, near, near))
    far_out = home(attend(doc_lengths, far, near))
    return unpack(group_of_row, near_out, far_out)


def solution(mesh):
    rows = P(("dp", "ctx"), None)
    return jax.shard_map(
        body,
        mesh=mesh,
        in_specs=(rows, rows, rows, rows, P("dp", None)),
        out_specs=rows,
        check_vma=False,
    )
```

time: 206 us -> 214 us (1.039)
  blocking collectives: 151 us -> 113 us
  Pallas kernels: 53 us -> 78.5 us
  starting transfers between devices: 0 us -> 20.4 us
    all_to_all x2, blocking collectives: 151 us -> 113 us  [exchange(): lax.all_to_all(x.reshape(devices, SLOT, x.shape[-1]), ('dp', 'ctx'), spli...]
    pallas_call x1 -> x2, Pallas kernels: 39.8 us -> 65.1 us  [attend(): pl.pallas_call(functools.partial(attend_kernel, heads), grid=(count // TQ...]
    all_to_all x0 -> x2, starting transfers between devices: none -> 20.4 us  [exchange(): lax.all_to_all(x.reshape(devices, SLOT, x.shape[-1]), ('dp', 'ctx'), spli...]
  transfers between devices with their start and end apart: 0 -> 2, of which waited for: 0 -> 0; matrix products, arithmetic and copies ran while one was open for 0% -> 0% of each run, Pallas kernels for 0% -> 31%
where the time goes in v2:
time: 214 us; the launch traced here: 213 us
  blocking collectives  113 us (53%)
  Pallas kernels  78.5 us (37%)
  starting transfers between devices  20.4 us (10%)
    all_to_all x2, blocking collectives, exchange(): lax.all_to_all(x.reshape(devices, SLOT, x.shape[-1]), ('dp', 'ctx'), spli...  113 us
    pallas_call x2, Pallas kernels, attend(): pl.pallas_call(functools.partial(attend_kernel, heads), grid=(count // TQ...  65.1 us
    all_to_all x2, starting transfers between devices, exchange(): lax.all_to_all(x.reshape(devices, SLOT, x.shape[-1]), ('dp', 'ctx'), spli...  20.4 us
    pallas_call x1, Pallas kernels, pack(): pl.pallas_call(pack_kernel, grid=(KV_HEADS,), in_specs=[pl.BlockSpec((row...  6.85 us
    pallas_call x1, Pallas kernels, unpack(): pl.pallas_call(unpack_kernel, grid=(KV_HEADS,), in_specs=[pl.BlockSpec((r...  6.52 us
  transfers between devices with their start and end apart: 2, of which 0 were waited for; matrix products, arithmetic and copies ran while one was open for 0% of the time, Pallas kernels for 31%

profile of v2, /device:TPU:1, one launch (start us, length us, event | category | flops | bytes accessed | tf_op | source)
XLA Modules:
  0.0 213.3 jit_solution(7680952999084597310)
XLA Ops:
  0.0 1.4 copy.7.group_ref
  1.4 6.9 %pack.1 = (bf16[32,8,8,512]{3,2,1,0:T(8,128)(2,1)}, bf16[32,8,8,256]{3,2,1,0:T(8,128)(2,1)}) custom-call(s32[128,1]{1,0:T(8,128)} %copy.7.group_ref, bf16[128,4096]{1,0:T(8,128)(2,1)} %q_ref.1, bf16[128,1024]{1,0:T(8,128)(2,1)} %k_ref.1, bf16[128,1024]{1,0:T(8,128)(2,1)} %v_ref.1), custom_call_target="tpu_custom_call" | custom-call | tf_op jit(solution)/shard_map/pack/pallas_call | solution.py:65
  8.2 68.6 %all_to_all.20 = bf16[256,8,512]{2,1,0:T(8,128)(2,1)} all-to-all(bf16[256,8,512]{2,1,0:T(8,128)(2,1)} %bitcast.15), channel_id=1, replica_groups=mesh['dp'=32,'ctx'=8] {'dp','ctx'}, dimensions={0} | all-to-all | bytes 4194304 | tf_op jit(solution)/shard_map/all_to_all | solution.py:215
  76.8 6.7 %all-to-all-start.2 = ((bf16[256,8,256]{2,1,0:T(8,128)(2,1)}), bf16[256,8,256]{2,1,0:T(8,128)(2,1)S(1)}, u32[]{:S(2)}, u32[]{:S(2)}) async-start(bf16[256,8,256]{2,1,0:T(8,128)(2,1)} %bitcast.4), calls=%async_computation.2 | async-start | bytes 2097152 | tf_op jit(solution)/shard_map/all_to_all | solution.py:215
  83.5 32.6 %attend.2 = bf16[2048,256]{1,0:T(8,128)(2,1)} custom-call(s32[1,2]{1,0:T(1,128)} %len_ref.3, bf16[2048,512]{1,0:T(8,128)(2,1)} %bitcast.10, bf16[2048,512]{1,0:T(8,128)(2,1)} %bitcast.11, bf16[2048,512]{1,0:T(8,128)(2,1)} %bitcast.12), custom_call_target="tpu_custom_call" | custom-call | flops 2147483648 | bytes 6291456 | tf_op jit(solution)/shard_map/attend/pallas_call | solution.py:188
  116.0 0.0 all-to-all-done.2
  116.0 0.0 copy-start.1
  116.0 13.7 %all-to-all-start.1 = ((bf16[256,8,256]{2,1,0:T(8,128)(2,1)}), bf16[256,8,256]{2,1,0:T(8,128)(2,1)S(1)}, u32[]{:S(2)}, u32[]{:S(2)}) async-start(bf16[256,8,256]{2,1,0:T(8,128)(2,1)} %bitcast.17), calls=%async_computation.1 | async-start | bytes 2097152 | tf_op jit(solution)/shard_map/all_to_all | solution.py:215
  129.8 0.0 copy-done.1
  129.8 32.6 %attend.3 = bf16[2048,256]{1,0:T(8,128)(2,1)} custom-call(s32[1,2]{1,0:T(1,128)} %len_ref.3, bf16[2048,256]{1,0:T(8,128)(2,1)} %bitcast.16, bf16[2048,512]{1,0:T(8,128)(2,1)} %bitcast.13, bf16[2048,512]{1,0:T(8,128)(2,1)} %bitcast.14), custom_call_target="tpu_custom_call" | custom-call | flops 2147483648 | bytes 3145728 | tf_op jit(solution)/shard_map/attend/pallas_call | solution.py:188
  162.4 0.0 all-to-all-done.1
  162.4 0.0 copy-start
  162.4 44.4 %all_to_all.21 = bf16[256,8,256]{2,1,0:T(8,128)(2,1)} all-to-all(bf16[256,8,256]{2,1,0:T(8,128)(2,1)} %bitcast.18), channel_id=1, replica_groups=mesh['dp'=32,'ctx'=8] {'dp','ctx'}, dimensions={0} | all-to-all | bytes 2097152 | tf_op jit(solution)/shard_map/all_to_all | solution.py:215
  206.8 0.0 copy-done
  206.8 6.5 %unpack.1 = bf16[128,4096]{1,0:T(8,128)(2,1)} custom-call(s32[128,1]{1,0:T(8,128)} %copy.7.group_ref, bf16[32,8,8,256]{3,2,1,0:T(8,128)(2,1)} %bitcast.8, bf16[32,8,8,256]{3,2,1,0:T(8,128)(2,1)} %bitcast.9), custom_call_target="tpu_custom_call" | custom-call | tf_op jit(solution)/shard_map/unpack/pallas_call | solution.py:104
Async XLA Ops:
  76.8 39.2 %all-to-all-start.2 = ((bf16[256,8,256]{2,1,0:T(8,128)(2,1)}), bf16[256,8,256]{2,1,0:T(8,128)(2,1)S(1)}, u32[]{:S(2)}, u32[]{:S(2)}) async-start(bf16[256,8,256]{2,1,0:T(8,128)(2,1)} %bitcast.4), calls=%async_computation.2 | async-start | bytes 2097152 | tf_op jit(solution)/shard_map/all_to_all | solution.py:215
  116.0 13.7 %copy-start.1 = (bf16[256,8,256]{2,1,0:T(8,128)(2,1)}, bf16[256,8,256]{2,1,0:T(8,128)(2,1)S(1)}, u32[]{:S(2)}) copy-start(bf16[256,8,256]{2,1,0:T(8,128)(2,1)S(1)} %all-to-all-done.2) | copy-start | bytes 3145732
  116.0 46.3 %all-to-all-start.1 = ((bf16[256,8,256]{2,1,0:T(8,128)(2,1)}), bf16[256,8,256]{2,1,0:T(8,128)(2,1)S(1)}, u32[]{:S(2)}, u32[]{:S(2)}) async-start(bf16[256,8,256]{2,1,0:T(8,128)(2,1)} %bitcast.17), calls=%async_computation.1 | async-start | bytes 2097152 | tf_op jit(solution)/shard_map/all_to_all | solution.py:215
  162.4 44.4 %copy-start = (bf16[256,8,256]{2,1,0:T(8,128)(2,1)}, bf16[256,8,256]{2,1,0:T(8,128)(2,1)S(1)}, u32[]{:S(2)}) copy-start(bf16[256,8,256]{2,1,0:T(8,128)(2,1)S(1)} %all-to-all-done.1) | copy-start | bytes 3145732

commit v3 on v2

v3 whole, which is shorter than its diff:
```python
import math

import jax
import jax.numpy as jnp
from jax import lax
from jax.experimental import pallas as pl
from jax.experimental.pallas import tpu as pltpu
from jax.sharding import PartitionSpec as P

KV_HEADS = 8
HEAD = 128
PER_KV = 4
GROUPS = 32
SLOT = 8
QW = PER_KV * HEAD
ROW_W = QW + 2 * HEAD
EMPTY = 64.0
FAR = 16384.0
TQ = 256
TK = 512
VALUE_ROWS = HEAD + 16
STEP = 2


def slot_targets(group_row):
    rows = group_row.shape[1]
    row = jnp.broadcast_to(group_row.astype(jnp.float32), (rows, rows))
    col = jnp.transpose(row)
    earlier = lax.broadcasted_iota(jnp.int32, (rows, rows), 0) < lax.broadcasted_iota(
        jnp.int32, (rows, rows), 1
    )
    same = jnp.where((col == row) & earlier, 1.0, 0.0)
    position = jnp.sum(same, axis=0, keepdims=True)
    return row[0:1, :] * float(SLOT) + position


def pack_kernel(group_ref, q_ref, k_ref, v_ref, out_ref, pick_ref):
    slots = GROUPS * SLOT
    rows = q_ref.shape[0]

    @pl.when(pl.program_id(0) == 0)
    def _():
        target = slot_targets(group_ref[...])
        slot = lax.broadcasted_iota(jnp.int32, (slots, rows), 0).astype(jnp.float32)
        pick_ref[...] = jnp.where(slot == target, 1.0, 0.0).astype(jnp.bfloat16)

    pick = pick_ref[...]

    def moved(x):
        return jnp.dot(pick, x, preferred_element_type=jnp.float32)

    def laid(x):
        return x.reshape(GROUPS, SLOT, x.shape[1]).astype(jnp.bfloat16)

    empty = (1.0 - jnp.sum(pick.astype(jnp.float32), axis=1, keepdims=True)) * EMPTY
    for j in range(STEP):
        head = slice(j * HEAD, (j + 1) * HEAD)
        out_ref[:, j, :, 0:QW] = laid(moved(q_ref[:, j * QW : (j + 1) * QW]))
        out_ref[:, j, :, QW : QW + HEAD] = laid(moved(k_ref[:, head]))
        out_ref[:, j, :, QW + HEAD :] = laid(moved(v_ref[:, head]) + empty)


def pack(group, q, k, v):
    rows = q.shape[0]
    return pl.pallas_call(
        pack_kernel,
        grid=(KV_HEADS // STEP,),
        in_specs=[
            pl.BlockSpec((1, rows), lambda j: (0, 0)),
            pl.BlockSpec((rows, STEP * QW), lambda j: (0, j)),
            pl.BlockSpec((rows, STEP * HEAD), lambda j: (0, j)),
            pl.BlockSpec((rows, STEP * HEAD), lambda j: (0, j)),
        ],
        out_specs=pl.BlockSpec((GROUPS, STEP, SLOT, ROW_W), lambda j: (0, j, 0, 0)),
        out_shape=jax.ShapeDtypeStruct((GROUPS, KV_HEADS, SLOT, ROW_W), jnp.bfloat16),
        scratch_shapes=[pltpu.VMEM((GROUPS * SLOT, rows), jnp.bfloat16)],
        name="pack",
    )(group, q, k, v)


def unpack_kernel(group_ref, o_ref, out_ref, pick_ref):
    slots = GROUPS * SLOT
    rows = out_ref.shape[0]

    @pl.when(pl.program_id(0) == 0)
    def _():
        target = slot_targets(group_ref[...])
        slot = lax.broadcasted_iota(jnp.int32, (slots, rows), 0).astype(jnp.float32)
        pick_ref[...] = jnp.transpose(jnp.where(slot == target, 1.0, 0.0)).astype(jnp.bfloat16)

    for j in range(STEP):
        x = o_ref[:, j].reshape(slots, QW)
        out_ref[:, j * QW : (j + 1) * QW] = jnp.dot(
            pick_ref[...], x, preferred_element_type=jnp.float32
        ).astype(jnp.bfloat16)


def unpack(group, o):
    rows = group.shape[1]
    return pl.pallas_call(
        unpack_kernel,
        grid=(KV_HEADS // STEP,),
        in_specs=[
            pl.BlockSpec((1, rows), lambda j: (0, 0)),
            pl.BlockSpec((GROUPS, STEP, SLOT, QW), lambda j: (0, j, 0, 0)),
        ],
        out_specs=pl.BlockSpec((rows, STEP * QW), lambda j: (0, j)),
        out_shape=jax.ShapeDtypeStruct((rows, KV_HEADS * QW), jnp.bfloat16),
        scratch_shapes=[pltpu.VMEM((rows, GROUPS * SLOT), jnp.bfloat16)],
        name="unpack",
    )(group, o)


def attend_kernel(len_ref, q_ref, k_ref, v_ref, o_ref, key_ref, vt_ref, mask_ref, acc_ref, s_ref, first_ref):
    count = k_ref.shape[0]
    block = pl.program_id(0)
    chunk = 128
    heads = PER_KV

    @pl.when(block == 0)
    def _():
        first_len = len_ref[0, 0].astype(jnp.float32)
        r = lax.broadcasted_iota(jnp.int32, (chunk, chunk), 0)
        l = lax.broadcasted_iota(jnp.int32, (chunk, chunk), 1)
        lower = jnp.where(r > l, 1.0, 0.0).astype(jnp.bfloat16)
        lane = l.astype(jnp.float32)
        row = r.astype(jnp.float32)
        seen = jnp.zeros((1, chunk), jnp.float32)
        first = jnp.full((1, chunk), float(count))
        ones = jnp.where(lax.broadcasted_iota(jnp.int32, (VALUE_ROWS - HEAD, chunk), 0) == 0, 1.0, 0.0).astype(jnp.bfloat16)
        for i in range(count // chunk):
            at = pl.ds(i * chunk, chunk)
            v = v_ref[at, :]
            vf = v.astype(jnp.float32)
            used = jnp.broadcast_to(jnp.where(vf[:, 0:1] < 0.5 * EMPTY, 1.0, 0.0), (chunk, chunk))
            rank = seen + jnp.dot(lower, used.astype(jnp.bfloat16), preferred_element_type=jnp.float32)
            code = jnp.where(used > 0.5, jnp.where(rank < first_len, 0.0, 1.0), 2.0)
            key_ref[at, 0:chunk] = k_ref[at, :]
            key_ref[at, chunk:] = jnp.where(lane == code, 1.0, 0.0).astype(jnp.bfloat16)
            mask_ref[at, :] = jnp.where((lane < 2.5) & (lane != code), -FAR, 0.0).astype(jnp.bfloat16)
            vt_ref[0:HEAD, at] = jnp.transpose(vf).astype(jnp.bfloat16)
            vt_ref[HEAD:, at] = ones
            place = jnp.where(code == 1.0, row + float(i * chunk), float(count))
            seen = seen + jnp.sum(used, axis=0, keepdims=True)
            first = jnp.minimum(first, jnp.min(place, axis=0, keepdims=True))
        first_ref[0] = jnp.min(first).astype(jnp.int32)
    first = first_ref[0]
    q_start = block * TQ
    scale = math.log2(math.e) / math.sqrt(HEAD)
    mask = mask_ref[pl.ds(pl.multiple_of(q_start, TQ), TQ), :]
    qs = [jnp.concatenate([q_ref[:, h*HEAD:(h+1)*HEAD], mask], axis=1) for h in range(heads)]
    def step(b, ms, kind):
        at = pl.ds(pl.multiple_of(b * TK, TK), TK)
        key = key_ref[at, :]
        vt = vt_ref[:, at]
        new = []
        if kind == "diag":
            t = q_start + lax.broadcasted_iota(jnp.int32, (TK, TQ), 1)
            u = b * TK + lax.broadcasted_iota(jnp.int32, (TK, TQ), 0)
            bias = jnp.where(u <= t, 0.0, -2.0 * FAR)
        for h in range(heads):
            s_ref[h] = lax.dot_general(key, qs[h], (((1,), (1,)), ((), ())), preferred_element_type=jnp.float32)
        for h in range(heads):
            s = s_ref[h]
            if kind == "diag":
                s = s + bias
            m_new = jnp.maximum(ms[h], jnp.max(s, axis=0, keepdims=True))
            w = jnp.exp2((s - m_new) * scale).astype(jnp.bfloat16)
            fade = jnp.exp2((ms[h] - m_new) * scale)
            acc_ref[h] = acc_ref[h] * fade + jnp.dot(vt, w, preferred_element_type=jnp.float32)
            new.append(m_new)
        return tuple(new)
    acc_ref[...] = jnp.zeros_like(acc_ref)
    lowest = jnp.where(q_start >= first, first // TK, 0)
    last = (q_start + TQ - 1) // TK
    ms = tuple(jnp.full((1, TQ), -4.0 * FAR, jnp.float32) for _ in range(heads))
    full = q_start // TK
    ms = lax.fori_loop(lowest, full, lambda b, c: step(b, c, "full"), ms)
    ndiag = max(TQ // TK, 1)
    for d in range(ndiag):
        ms = step(full + d, ms, "diag")
    for h in range(heads):
        acc = acc_ref[h]
        o = acc[0:HEAD] * (1.0 / acc[HEAD:HEAD+1])
        o_ref[:, h*HEAD:(h+1)*HEAD] = jnp.transpose(o).astype(jnp.bfloat16)


def attend(lengths, rows):
    count = rows.shape[0]
    return pl.pallas_call(
        attend_kernel,
        grid=(count // TQ,),
        in_specs=[
            pl.BlockSpec(memory_space=pltpu.SMEM),
            pl.BlockSpec((TQ, QW), lambda i: (i, 0)),
            pl.BlockSpec((count, HEAD), lambda i: (0, PER_KV)),
            pl.BlockSpec((count, HEAD), lambda i: (0, PER_KV + 1)),
        ],
        out_specs=pl.BlockSpec((TQ, QW), lambda i: (i, 0)),
        out_shape=jax.ShapeDtypeStruct((count, QW), jnp.bfloat16),
        scratch_shapes=[
            pltpu.VMEM((count, 2 * HEAD), jnp.bfloat16),
            pltpu.VMEM((VALUE_ROWS, count), jnp.bfloat16),
            pltpu.VMEM((count, HEAD), jnp.bfloat16),
            pltpu.VMEM((PER_KV, VALUE_ROWS, TQ), jnp.float32),
            pltpu.VMEM((PER_KV, TK, TQ), jnp.float32),
            pltpu.SMEM((1,), jnp.int32),
        ],
        name="attend",
    )(lengths, rows, rows, rows)


def body(query_rows, key_rows, token_values, group_of_row, doc_lengths):
    devices = lax.axis_size("dp") * lax.axis_size("ctx")
    group = group_of_row.reshape(1, group_of_row.shape[0])
    packed = pack(group, query_rows, key_rows, token_values)
    arrived = lax.all_to_all(
        packed.reshape(devices, SLOT, ROW_W), ("dp", "ctx"), split_axis=0, concat_axis=0, tiled=True
    )
    result = attend(doc_lengths, arrived.reshape(devices * SLOT, ROW_W))
    returned = lax.all_to_all(
        result.reshape(devices, SLOT, QW), ("dp", "ctx"), split_axis=0, concat_axis=0, tiled=True
    )
    return unpack(group, returned.reshape(GROUPS, KV_HEADS, SLOT, QW))


def solution(mesh):
    rows = P(("dp", "ctx"), None)
    return jax.shard_map(
        body,
        mesh=mesh,
        in_specs=(rows, rows, rows, rows, P("dp", None)),
        out_specs=rows,
        check_vma=False,
    )
```

time: 214 us -> 183 us (0.86)
  Pallas kernels: 78.5 us -> 32.1 us
  blocking collectives: 113 us -> 152 us
  starting transfers between devices: 20.4 us -> 0 us
    pallas_call x4 -> x3, Pallas kernels: 78.5 us -> 32.1 us  [the longest x1 23.2 us: attend(): pl.pallas_call(attend_kernel, grid=(count // TQ,), in_specs=[pl.BlockSpec...]
    all_to_all x2, blocking collectives: 113 us -> 152 us  [the longest x1 90.5 us: body(): lax.all_to_all(packed.reshape(devices, SLOT, ROW_W), ('dp', 'ctx'), split...]
    all_to_all x2 -> x0, starting transfers between devices: 20.4 us -> none  [exchange(): lax.all_to_all(x.reshape(devices, SLOT, x.shape[-1]), ('dp', 'ctx'), spli...]
  transfers between devices with their start and end apart: 2 -> 0, of which waited for: 0 -> 0; matrix products, arithmetic and copies ran while one was open for 0% -> 0% of each run, Pallas kernels for 31% -> 0%
where the time goes in v3:
time: 183 us; the launch traced here: 184 us
  blocking collectives  152 us (83%)
  Pallas kernels  32.1 us (18%)
    all_to_all x1, blocking collectives, body(): lax.all_to_all(packed.reshape(devices, SLOT, ROW_W), ('dp', 'ctx'), split...  90.5 us
    all_to_all x1, blocking collectives, body(): lax.all_to_all(result.reshape(devices, SLOT, QW), ('dp', 'ctx'), split_ax...  61 us
    pallas_call x1, Pallas kernels, attend(): pl.pallas_call(attend_kernel, grid=(count // TQ,), in_specs=[pl.BlockSpec...  23.2 us
    pallas_call x1, Pallas kernels, pack(): pl.pallas_call(pack_kernel, grid=(KV_HEADS // STEP,), in_specs=[pl.BlockS...  4.68 us
    pallas_call x1, Pallas kernels, unpack(): pl.pallas_call(unpack_kernel, grid=(KV_HEADS // STEP,), in_specs=[pl.Bloc...  4.22 us

profile of v3, /device:TPU:1, one launch (start us, length us, event | category | flops | bytes accessed | tf_op | source)
XLA Modules:
  0.0 183.6 jit_solution(10265729542328754085)
XLA Ops:
  0.0 4.7 %pack.1 = bf16[32,8,8,768]{3,2,1,0:T(8,128)(2,1)} custom-call(s32[1,128]{1,0:T(1,128)} %bitcast.11, bf16[128,4096]{1,0:T(8,128)(2,1)} %q_ref.1, bf16[128,1024]{1,0:T(8,128)(2,1)} %k_ref.1, bf16[128,1024]{1,0:T(8,128)(2,1)} %v_ref.1), custom_call_target="tpu_custom_call" | custom-call | tf_op jit(solution)/shard_map/pack/pallas_call | solution.py:65
  4.7 90.5 %all_to_all.10 = bf16[256,8,768]{2,1,0:T(8,128)(2,1)} all-to-all(bf16[256,8,768]{2,1,0:T(8,128)(2,1)} %bitcast.8), channel_id=1, replica_groups=mesh['dp'=32,'ctx'=8] {'dp','ctx'}, dimensions={0} | all-to-all | bytes 6291456 | tf_op jit(solution)/shard_map/all_to_all | solution.py:217
  95.2 23.2 %attend.1 = bf16[2048,512]{1,0:T(8,128)(2,1)} custom-call(s32[1,2]{1,0:T(1,128)} %len_ref.1, bf16[2048,768]{1,0:T(8,128)(2,1)} %bitcast.5, bf16[2048,768]{1,0:T(8,128)(2,1)} %bitcast.6, bf16[2048,768]{1,0:T(8,128)(2,1)} %bitcast.7), custom_call_target="tpu_custom_call" | custom-call | tf_op jit(solution)/shard_map/attend/pallas_call | solution.py:190
  118.4 61.0 %all_to_all.11 = bf16[256,8,512]{2,1,0:T(8,128)(2,1)} all-to-all(bf16[256,8,512]{2,1,0:T(8,128)(2,1)} %bitcast.10), channel_id=1, replica_groups=mesh['dp'=32,'ctx'=8] {'dp','ctx'}, dimensions={0} | all-to-all | bytes 4194304 | tf_op jit(solution)/shard_map/all_to_all | solution.py:221
  179.4 4.2 %unpack.1 = bf16[128,4096]{1,0:T(8,128)(2,1)} custom-call(s32[1,128]{1,0:T(1,128)} %bitcast.12, bf16[32,8,8,512]{3,2,1,0:T(8,128)(2,1)} %bitcast.9), custom_call_target="tpu_custom_call" | custom-call | tf_op jit(solution)/shard_map/unpack/pallas_call | solution.py:100

commit v4 on v3

v4 whole, which is shorter than its diff:
```python
import math

import jax
import jax.numpy as jnp
from jax import lax
from jax.experimental import pallas as pl
from jax.experimental.pallas import tpu as pltpu
from jax.sharding import PartitionSpec as P

KV_HEADS = 8
HEAD = 128
PER_KV = 4
GROUPS = 32
SLOT = 8
CTX = 8
QW = PER_KV * HEAD
EMPTY = 64.0
FAR = 16384.0
SPAN = 8
BLOCKS = GROUPS // SPAN
KEYS = CTX * SPAN * SLOT
ROWS = SPAN * SLOT
LANES = PER_KV * ROWS
VALUE_ROWS = HEAD + 16
PARTS = 2
HEADS = KV_HEADS // PARTS


def slot_targets(group_row):
    rows = group_row.shape[1]
    row = jnp.broadcast_to(group_row.astype(jnp.float32), (rows, rows))
    col = jnp.transpose(row)
    earlier = lax.broadcasted_iota(jnp.int32, (rows, rows), 0) < lax.broadcasted_iota(
        jnp.int32, (rows, rows), 1
    )
    same = jnp.where((col == row) & earlier, 1.0, 0.0)
    position = jnp.sum(same, axis=0, keepdims=True)
    return row[0:1, :] * float(SLOT) + position


def selection(group_row):
    slots, rows = GROUPS * SLOT, group_row.shape[1]
    slot = lax.broadcasted_iota(jnp.int32, (slots, rows), 0).astype(jnp.float32)
    return jnp.where(slot == slot_targets(group_row), 1.0, 0.0)


def laid(x):
    return x.reshape(GROUPS, SLOT, x.shape[1]).astype(jnp.bfloat16)


def pack_kv_kernel(group_ref, k_ref, v_ref, out_ref):
    pick = selection(group_ref[...])
    empty = (1.0 - jnp.sum(pick, axis=1, keepdims=True)) * EMPTY
    pick = pick.astype(jnp.bfloat16)
    width = k_ref.shape[1]
    out_ref[:, :, 0:width] = laid(jnp.dot(pick, k_ref[...], preferred_element_type=jnp.float32))
    out_ref[:, :, width:] = laid(
        jnp.dot(pick, v_ref[...], preferred_element_type=jnp.float32) + empty
    )


def pack_kv(group, k, v):
    return pl.pallas_call(
        pack_kv_kernel,
        out_shape=jax.ShapeDtypeStruct((GROUPS, SLOT, 2 * k.shape[1]), jnp.bfloat16),
        name="pack_kv",
    )(group, k, v)


def pack_q_kernel(group_ref, q_ref, *refs):
    outs, pick_ref = refs[:-1], refs[-1]
    step = pl.program_id(0)

    @pl.when(step == 0)
    def _():
        pick_ref[...] = selection(group_ref[...]).astype(jnp.bfloat16)

    for part, out_ref in enumerate(outs):

        @pl.when(step == part)
        def _(out_ref=out_ref):
            out_ref[...] = laid(
                jnp.dot(pick_ref[...], q_ref[...], preferred_element_type=jnp.float32)
            )


def pack_q(group, q):
    rows, width = q.shape
    part = width // PARTS
    shape = (GROUPS, SLOT, part)
    return pl.pallas_call(
        pack_q_kernel,
        grid=(PARTS,),
        in_specs=[
            pl.BlockSpec((1, rows), lambda i: (0, 0)),
            pl.BlockSpec((rows, part), lambda i: (0, i)),
        ],
        out_specs=[pl.BlockSpec(shape, lambda i: (0, 0, 0))] * PARTS,
        out_shape=[jax.ShapeDtypeStruct(shape, jnp.bfloat16)] * PARTS,
        scratch_shapes=[pltpu.VMEM((GROUPS * SLOT, rows), jnp.bfloat16)],
        name="pack_q",
    )(group, q)


def unpack_kernel(group_ref, *refs):
    parts, out_ref = refs[:-1], refs[-1]
    pick = jnp.transpose(selection(group_ref[...])).astype(jnp.bfloat16)
    for i, ref in enumerate(parts):
        width = ref.shape[2]
        out_ref[:, i * width : (i + 1) * width] = jnp.dot(
            pick, ref[...].reshape(GROUPS * SLOT, width), preferred_element_type=jnp.float32
        ).astype(jnp.bfloat16)


def unpack(group, parts):
    return pl.pallas_call(
        unpack_kernel,
        out_shape=jax.ShapeDtypeStruct(
            (group.shape[1], sum(p.shape[2] for p in parts)), jnp.bfloat16
        ),
        name="unpack",
    )(group, *parts)


def attend_kernel(
    len_ref, me_ref, q_ref, k_ref, v_ref, o_ref, feat_ref, mask_ref, bias_ref, vt_ref, s_ref
):
    @pl.when(pl.program_id(0) == 0)
    def _():
        me = me_ref[0, 0]
        first_len = len_ref[0, 0].astype(jnp.float32)
        shape = (GROUPS, SLOT, HEAD)
        lane = lax.broadcasted_iota(jnp.int32, shape, 2).astype(jnp.float32)
        slot = lax.broadcasted_iota(jnp.int32, shape, 1).astype(jnp.float32)
        used = [
            jnp.broadcast_to(
                jnp.where(v_ref[c].astype(jnp.float32)[:, :, 0:1] < 0.5 * EMPTY, 1.0, 0.0), shape
            )
            for c in range(CTX)
        ]
        number = [jnp.sum(u, axis=1) for u in used]
        before = jnp.where(
            lax.broadcasted_iota(jnp.int32, (GROUPS, GROUPS), 0)
            > lax.broadcasted_iota(jnp.int32, (GROUPS, GROUPS), 1),
            1.0,
            0.0,
        )
        base = jnp.dot(
            before.astype(jnp.bfloat16),
            sum(number).astype(jnp.bfloat16),
            preferred_element_type=jnp.float32,
        )
        own = jnp.zeros(shape, jnp.float32)
        for c in range(CTX):
            rank = base[:, None, :] + slot
            base = base + number[c]
            code = jnp.where(used[c] > 0.5, jnp.where(rank < first_len, 0.0, 1.0), 2.0)
            own = own + jnp.where(me == c, code, 0.0)
            feat = jnp.where(lane == code, 1.0, 0.0)
            for b in range(BLOCKS):
                feat_ref[b, c * ROWS : (c + 1) * ROWS, :] = (
                    feat[b * SPAN : (b + 1) * SPAN].reshape(ROWS, HEAD).astype(jnp.bfloat16)
                )
        mask_ref[...] = (
            jnp.where(lane == own, 0.0, -FAR).reshape(GROUPS * SLOT, HEAD).astype(jnp.bfloat16)
        )
        u = lax.broadcasted_iota(jnp.int32, (KEYS, LANES), 0)
        t = lax.broadcasted_iota(jnp.int32, (KEYS, LANES), 1) % ROWS
        u_order = (u % ROWS) // SLOT * (CTX * SLOT) + u // ROWS * SLOT + u % SLOT
        t_order = t // SLOT * (CTX * SLOT) + me * SLOT + t % SLOT
        bias_ref[...] = jnp.where(u_order <= t_order, 0.0, -2.0 * FAR)
        vt_ref[HEAD:, :] = jnp.where(
            lax.broadcasted_iota(jnp.int32, (VALUE_ROWS - HEAD, BLOCKS * KEYS), 0) == 0, 1.0, 0.0
        ).astype(jnp.bfloat16)

    scale = math.log2(math.e) / math.sqrt(HEAD)
    queries = []
    for i in range(BLOCKS):
        at = slice(i * ROWS, (i + 1) * ROWS)
        mask = mask_ref[at, :]
        queries.append(
            jnp.concatenate(
                [
                    jnp.concatenate([q_ref[at, h * HEAD : (h + 1) * HEAD], mask], axis=1)
                    for h in range(PER_KV)
                ],
                axis=0,
            )
        )
    for b in range(BLOCKS):
        span = slice(b * SPAN, (b + 1) * SPAN)
        key = jnp.concatenate([k_ref[:, span].reshape(KEYS, HEAD), feat_ref[b]], axis=1)
        vt_ref[0:HEAD, b * KEYS : (b + 1) * KEYS] = jnp.transpose(
            v_ref[:, span].reshape(KEYS, HEAD).astype(jnp.float32)
        ).astype(jnp.bfloat16)
        for i in range(b, BLOCKS):
            s = lax.dot_general(
                key, queries[i], (((1,), (1,)), ((), ())), preferred_element_type=jnp.float32
            )
            s_ref[i, b] = s + bias_ref[...] if i == b else s
    for i in range(BLOCKS):
        top = jnp.max(s_ref[i, 0], axis=0, keepdims=True)
        for b in range(1, i + 1):
            top = jnp.maximum(top, jnp.max(s_ref[i, b], axis=0, keepdims=True))
        acc = None
        for b in range(i + 1):
            w = jnp.exp2((s_ref[i, b] - top) * scale).astype(jnp.bfloat16)
            part = jnp.dot(
                vt_ref[:, b * KEYS : (b + 1) * KEYS], w, preferred_element_type=jnp.float32
            )
            acc = part if acc is None else acc + part
        out = jnp.transpose(acc[0:HEAD] * (1.0 / acc[HEAD : HEAD + 1])).astype(jnp.bfloat16)
        for h in range(PER_KV):
            o_ref[i * ROWS : (i + 1) * ROWS, h * HEAD : (h + 1) * HEAD] = out[
                h * ROWS : (h + 1) * ROWS
            ]


def attend(lengths, me, q, kv, part):
    count = GROUPS * SLOT
    block = (CTX, GROUPS, SLOT, HEAD)
    low = part * HEADS
    return pl.pallas_call(
        attend_kernel,
        grid=(HEADS,),
        in_specs=[
            pl.BlockSpec(memory_space=pltpu.SMEM),
            pl.BlockSpec(memory_space=pltpu.SMEM),
            pl.BlockSpec((count, QW), lambda j: (0, j)),
            pl.BlockSpec(block, lambda j: (0, 0, 0, low + j)),
            pl.BlockSpec(block, lambda j: (0, 0, 0, KV_HEADS + low + j)),
        ],
        out_specs=pl.BlockSpec((count, QW), lambda j: (0, j)),
        out_shape=jax.ShapeDtypeStruct((count, HEADS * QW), jnp.bfloat16),
        scratch_shapes=[
            pltpu.VMEM((BLOCKS, KEYS, HEAD), jnp.bfloat16),
            pltpu.VMEM((count, HEAD), jnp.bfloat16),
            pltpu.VMEM((KEYS, LANES), jnp.float32),
            pltpu.VMEM((VALUE_ROWS, BLOCKS * KEYS), jnp.bfloat16),
            pltpu.VMEM((BLOCKS, BLOCKS, KEYS, LANES), jnp.float32),
        ],
        cost_estimate=pl.CostEstimate(
            flops=5 * 10**9, transcendentals=2 * 10**7, bytes_accessed=8 * 10**6
        ),
        name="attend",
    )(lengths, me, q, kv, kv)


def exchange(x):
    return lax.all_to_all(x, "dp", split_axis=0, concat_axis=0, tiled=True)


def gather(kv):
    return lax.all_gather(kv, "ctx", axis=0)


def body(query_rows, key_rows, token_values, group_of_row, doc_lengths):
    group = group_of_row.reshape(1, group_of_row.shape[0])
    me = lax.axis_index("ctx").astype(jnp.int32).reshape(1, 1)
    sent = pack_kv(group, key_rows, token_values)
    queries = pack_q(group, query_rows)
    kv, queries = lax.optimization_barrier((exchange(sent), queries))
    everyone = gather(kv)
    outs = []
    for part in range(PARTS):
        arrived = exchange(queries[part])
        if part + 1 < PARTS:
            arrived, queries = lax.optimization_barrier((arrived, queries))
        out = attend(doc_lengths, me, arrived.reshape(GROUPS * SLOT, HEADS * QW), everyone, part)
        outs.append(exchange(out.reshape(GROUPS, SLOT, HEADS * QW)))
    return unpack(group, outs)


def solution(mesh):
    rows = P(("dp", "ctx"), None)
    return jax.shard_map(
        body,
        mesh=mesh,
        in_specs=(rows, rows, rows, rows, P("dp", None)),
        out_specs=rows,
        check_vma=False,
    )
```

time: 183 us -> 193 us (1.055); the launches traced: 184 us -> 190 us
  blocking collectives: 152 us -> 63.3 us
  waiting for transfers between devices: 0 us -> 51 us
  starting transfers between devices: 0 us -> 28.4 us
  between operations: 0.01 us -> 13.4 us
    all_to_all x2, blocking collectives: 152 us -> 63.3 us  [exchange(): return lax.all_to_all(x, 'dp', split_axis=0, concat_axis=0, tiled=True)]
    all_to_all x0 -> x3, waiting for transfers between devices: none -> 37.7 us  [exchange(): return lax.all_to_all(x, 'dp', split_axis=0, concat_axis=0, tiled=True)]
    all_to_all x0 -> x3, starting transfers between devices: none -> 28.4 us  [exchange(): return lax.all_to_all(x, 'dp', split_axis=0, concat_axis=0, tiled=True)]
    all_gather x0 -> x1, waiting for transfers between devices: none -> 13.2 us  [gather(): return lax.all_gather(kv, 'ctx', axis=0)]
    pallas_call x3 -> x5, Pallas kernels: 32.1 us -> 32.9 us  [the longest x2 23.8 us: attend(): pl.pallas_call(attend_kernel, grid=(HEADS,), in_specs=[pl.BlockSpec(memor...]
  transfers between devices with their start and end apart: 0 -> 4, of which waited for: 0 -> 3; matrix products, arithmetic and copies ran while one was open for 0% -> 0% of each run, Pallas kernels for 0% -> 14%
where the time goes in v4:
time: 193 us; the launch traced here: 190 us
  blocking collectives  63.3 us (33%)
  waiting for transfers between devices  51 us (26%)
  Pallas kernels  32.9 us (17%)
  starting transfers between devices  28.4 us (15%)
  between operations  13.4 us (7%)
    all_to_all x2, blocking collectives, exchange(): return lax.all_to_all(x, 'dp', split_axis=0, concat_axis=0, tiled=True)  63.3 us
    all_to_all x3, waiting for transfers between devices, exchange(): return lax.all_to_all(x, 'dp', split_axis=0, concat_axis=0, tiled=True)  37.7 us
    all_to_all x3, starting transfers between devices, exchange(): return lax.all_to_all(x, 'dp', split_axis=0, concat_axis=0, tiled=True)  28.4 us
    pallas_call x2, Pallas kernels, attend(): pl.pallas_call(attend_kernel, grid=(HEADS,), in_specs=[pl.BlockSpec(memor...  23.8 us
    all_gather x1, waiting for transfers between devices, gather(): return lax.all_gather(kv, 'ctx', axis=0)  13.2 us
  transfers between devices with their start and end apart: 4, of which 3 were waited for; matrix products, arithmetic and copies ran while one was open for 0% of the time, Pallas kernels for 14%

profile of v4, /device:TPU:1, one launch (start us, length us, event | category | flops | bytes accessed | tf_op | source)
XLA Modules:
  0.0 190.0 jit_solution(6250271346306223930)
XLA Ops:
  6.5 2.5 %pack_kv.1 = bf16[32,8,2048]{2,1,0:T(8,128)(2,1)} custom-call(s32[1,128]{1,0:T(1,128)} %bitcast.11, bf16[128,1024]{1,0:T(8,128)(2,1)} %k_ref.1, bf16[128,1024]{1,0:T(8,128)(2,1)} %v_ref.1), custom_call_target="tpu_custom_call" | custom-call | tf_op jit(solution)/shard_map/pack_kv/pallas_call | solution.py:63
  9.1 12.0 %all-to-all-start = ((bf16[32,8,2048]{2,1,0:T(8,128)(2,1)}), bf16[32,8,2048]{2,1,0:T(8,128)(2,1)S(1)}, u32[]{:S(2)}, u32[]{:S(2)}) async-start(bf16[32,8,2048]{2,1,0:T(8,128)(2,1)} %pack_kv.1), calls=%async_computation | async-start | bytes 2097152 | tf_op jit(solution)/shard_map/all_to_all | solution.py:250
  21.1 0.0 all-gather.3.cloned.1.call-start
  21.2 3.4 %pack_q.1 = (bf16[32,8,2048]{2,1,0:T(8,128)(2,1)}, bf16[32,8,2048]{2,1,0:T(8,128)(2,1)}) custom-call(s32[1,128]{1,0:T(1,128)} %bitcast.12, bf16[128,4096]{1,0:T(8,128)(2,1)} %q_ref.1), custom_call_target="tpu_custom_call" | custom-call | tf_op jit(solution)/shard_map/pack_q/pallas_call | solution.py:91
  24.6 22.7 %all-to-all-done = bf16[32,8,2048]{2,1,0:T(8,128)(2,1)S(1)} async-done(((bf16[32,8,2048]{2,1,0:T(8,128)(2,1)}), bf16[32,8,2048]{2,1,0:T(8,128)(2,1)S(1)}, u32[]{:S(2)}, u32[]{:S(2)}) %all-to-all-start) | async-done | bytes 1048608 | tf_op jit(solution)/shard_map/all_to_all | solution.py:250
  47.3 0.0 copy-start
  47.3 1.0 copy-done
  48.3 0.0 all-gather.3.cloned.1.call-update
  48.3 31.9 %all_to_all.25 = bf16[32,8,2048]{2,1,0:T(8,128)(2,1)} all-to-all(bf16[32,8,2048]{2,1,0:T(8,128)(2,1)} %get-tuple-element.14), channel_id=1, replica_groups=mesh['dp'=32,'ctx'=8] {'dp'}, dimensions={0} | all-to-all | bytes 2097152 | tf_op jit(solution)/shard_map/all_to_all | solution.py:250
  80.2 6.8 %all-to-all-start.3 = ((bf16[32,8,2048]{2,1,0:T(8,128)(2,1)}), bf16[32,8,2048]{2,1,0:T(8,128)(2,1)S(1)}, u32[]{:S(2)}, u32[]{:S(2)}) async-start(bf16[32,8,2048]{2,1,0:T(8,128)(2,1)} %get-tuple-element.18), calls=%async_computation.3 | async-start | bytes 2097152 | tf_op jit(solution)/shard_map/all_to_all | solution.py:250
  87.0 13.2 %all-gather.3.cloned.1.call-done = bf16[256,8,2048]{2,1,0:T(8,128)(2,1)} async-done(((bf16[32,8,2048]{2,1,0:T(8,128)(2,1)}), bf16[256,8,2048]{2,1,0:T(8,128)(2,1)}) %all-gather.3.cloned.1.call-update) | async-done | bytes 8388624 | tf_op jit(solution)/shard_map/all_gather | solution.py:254
  100.2 11.9 %attend.2 = bf16[256,2048]{1,0:T(8,128)(2,1)} custom-call(s32[1,2]{1,0:T(1,128)} %len_ref.3, s32[1,1]{1,0:T(1,128)} %bitcast.1.me_ref, bf16[256,2048]{1,0:T(8,128)(2,1)} %bitcast.8, bf16[8,32,8,2048]{3,2,1,0:T(8,128)(2,1)} %bitcast.14, bf16[8,32,8,2048]{3,2,1,0:T(8,128)(2,1)} %bitcast.15), custom_call_target="tpu_custom_call" | custom-call | flops 5000000000 | bytes 8000000 | tf_op jit(solution)/shard_map/attend/pallas_call | solution.py:223
  112.1 0.0 all-to-all-done.3
  112.1 0.0 copy-start.2
  112.1 9.6 %all-to-all-start.2 = ((bf16[32,8,2048]{2,1,0:T(8,128)(2,1)}), bf16[32,8,2048]{2,1,0:T(8,128)(2,1)S(1)}, u32[]{:S(2)}, u32[]{:S(2)}) async-start(bf16[32,8,2048]{2,1,0:T(8,128)(2,1)} %bitcast.9), calls=%async_computation.2 | async-start | bytes 2097152 | tf_op jit(solution)/shard_map/all_to_all | solution.py:250
  121.7 0.0 copy-done.2
  121.7 11.9 %attend.3 = bf16[256,2048]{1,0:T(8,128)(2,1)} custom-call(s32[1,2]{1,0:T(1,128)} %len_ref.3, s32[1,1]{1,0:T(1,128)} %bitcast.1.me_ref, bf16[256,2048]{1,0:T(8,128)(2,1)} %bitcast.7, bf16[8,32,8,2048]{3,2,1,0:T(8,128)(2,1)} %bitcast.16, bf16[8,32,8,2048]{3,2,1,0:T(8,128)(2,1)} %bitcast.17), custom_call_target="tpu_custom_call" | custom-call | flops 5000000000 | bytes 8000000 | tf_op jit(solution)/shard_map/attend/pallas_call | solution.py:223
  133.6 15.0 %all-to-all-done.2.refs_0_ = bf16[32,8,2048]{2,1,0:T(8,128)(2,1)S(1)} async-done(((bf16[32,8,2048]{2,1,0:T(8,128)(2,1)}), bf16[32,8,2048]{2,1,0:T(8,128)(2,1)S(1)}, u32[]{:S(2)}, u32[]{:S(2)}) %all-to-all-start.2) | async-done | bytes 1048608 | tf_op jit(solution)/shard_map/all_to_all | solution.py:250
  148.6 0.0 copy-start.1
  148.6 31.4 %all_to_all.26.refs_1_ = bf16[32,8,2048]{2,1,0:T(8,128)(2,1)} all-to-all(bf16[32,8,2048]{2,1,0:T(8,128)(2,1)} %bitcast.10), channel_id=1, replica_groups=mesh['dp'=32,'ctx'=8] {'dp'}, dimensions={0} | all-to-all | bytes 2097152 | tf_op jit(solution)/shard_map/all_to_all | solution.py:250
  180.0 0.0 copy-done.1
  180.0 3.1 %unpack.1 = bf16[128,4096]{1,0:T(8,128)(2,1)} custom-call(s32[1,128]{1,0:T(1,128)} %bitcast.13, bf16[32,8,2048]{2,1,0:T(8,128)(2,1)} %copy-done.1, bf16[32,8,2048]{2,1,0:T(8,128)(2,1)} %all_to_all.26.refs_1_), custom_call_target="tpu_custom_call" | custom-call | tf_op jit(solution)/shard_map/unpack/pallas_call | solution.py:116
Async XLA Ops:
  9.1 38.2 %all-to-all-start = ((bf16[32,8,2048]{2,1,0:T(8,128)(2,1)}), bf16[32,8,2048]{2,1,0:T(8,128)(2,1)S(1)}, u32[]{:S(2)}, u32[]{:S(2)}) async-start(bf16[32,8,2048]{2,1,0:T(8,128)(2,1)} %pack_kv.1), calls=%async_computation | async-start | bytes 2097152 | tf_op jit(solution)/shard_map/all_to_all | solution.py:250
  21.1 79.1 %all-gather.3.cloned.1.call-start = ((), (), s32[]{:S(2)}) async-start(), calls=%async_computation.5 | async-start | bytes 9437184 | tf_op jit(solution)/shard_map/all_gather | solution.py:254
  47.3 1.0 copy-start
  80.2 31.9 %all-to-all-start.3 = ((bf16[32,8,2048]{2,1,0:T(8,128)(2,1)}), bf16[32,8,2048]{2,1,0:T(8,128)(2,1)S(1)}, u32[]{:S(2)}, u32[]{:S(2)}) async-start(bf16[32,8,2048]{2,1,0:T(8,128)(2,1)} %get-tuple-element.18), calls=%async_computation.3 | async-start | bytes 2097152 | tf_op jit(solution)/shard_map/all_to_all | solution.py:250
  112.1 9.6 %copy-start.2 = (bf16[32,8,2048]{2,1,0:T(8,128)(2,1)}, bf16[32,8,2048]{2,1,0:T(8,128)(2,1)S(1)}, u32[]{:S(2)}) copy-start(bf16[32,8,2048]{2,1,0:T(8,128)(2,1)S(1)} %all-to-all-done.3) | copy-start | bytes 3145732
  112.1 36.5 %all-to-all-start.2 = ((bf16[32,8,2048]{2,1,0:T(8,128)(2,1)}), bf16[32,8,2048]{2,1,0:T(8,128)(2,1)S(1)}, u32[]{:S(2)}, u32[]{:S(2)}) async-start(bf16[32,8,2048]{2,1,0:T(8,128)(2,1)} %bitcast.9), calls=%async_computation.2 | async-start | bytes 2097152 | tf_op jit(solution)/shard_map/all_to_all | solution.py:250
  148.6 31.4 %copy-start.1 = (bf16[32,8,2048]{2,1,0:T(8,128)(2,1)}, bf16[32,8,2048]{2,1,0:T(8,128)(2,1)S(1)}, u32[]{:S(2)}) copy-start(bf16[32,8,2048]{2,1,0:T(8,128)(2,1)S(1)} %all-to-all-done.2.refs_0_) | copy-start | bytes 3145732
Sparse Core Ops, SparseCore 0:
  48.4 51.7 all-gather.2

commit v5 on v4

--- a/solution.py
+++ b/solution.py
@@ -22,7 +22,7 @@
 ROWS = SPAN * SLOT
 LANES = PER_KV * ROWS
 VALUE_ROWS = HEAD + 16
-PARTS = 2
+PARTS = 1
 HEADS = KV_HEADS // PARTS
 
 
@@ -122,19 +122,20 @@
     )(group, *parts)
 
 
-def attend_kernel(
-    len_ref, me_ref, q_ref, k_ref, v_ref, o_ref, feat_ref, mask_ref, bias_ref, vt_ref, s_ref
-):
+def attend_kernel(len_ref, who_ref, q_ref, *refs):
+    k_refs, v_refs = refs[:CTX], refs[CTX : 2 * CTX]
+    o_ref, feat_ref, mask_ref, bias_ref, vt_ref, s_ref = refs[2 * CTX :]
+
     @pl.when(pl.program_id(0) == 0)
     def _():
-        me = me_ref[0, 0]
+        who = [who_ref[0, c] for c in range(CTX)]
         first_len = len_ref[0, 0].astype(jnp.float32)
         shape = (GROUPS, SLOT, HEAD)
         lane = lax.broadcasted_iota(jnp.int32, shape, 2).astype(jnp.float32)
         slot = lax.broadcasted_iota(jnp.int32, shape, 1).astype(jnp.float32)
         used = [
             jnp.broadcast_to(
-                jnp.where(v_ref[c].astype(jnp.float32)[:, :, 0:1] < 0.5 * EMPTY, 1.0, 0.0), shape
+                jnp.where(v_refs[c][...].astype(jnp.float32)[:, :, 0:1] < 0.5 * EMPTY, 1.0, 0.0), shape
             )
             for c in range(CTX)
         ]
@@ -150,28 +151,35 @@
             sum(number).astype(jnp.bfloat16),
             preferred_element_type=jnp.float32,
         )
-        own = jnp.zeros(shape, jnp.float32)
         for c in range(CTX):
-            rank = base[:, None, :] + slot
-            base = base + number[c]
+            earlier = sum(jnp.where(who[d] < who[c], number[d], 0.0) for d in range(CTX))
+            rank = (base + earlier)[:, None, :] + slot
             code = jnp.where(used[c] > 0.5, jnp.where(rank < first_len, 0.0, 1.0), 2.0)
-            own = own + jnp.where(me == c, code, 0.0)
+            if c == 0:
+                mask_ref[...] = (
+                    jnp.where(lane == code, 0.0, -FAR)
+                    .reshape(GROUPS * SLOT, HEAD)
+                    .astype(jnp.bfloat16)
+                )
             feat = jnp.where(lane == code, 1.0, 0.0)
             for b in range(BLOCKS):
                 feat_ref[b, c * ROWS : (c + 1) * ROWS, :] = (
                     feat[b * SPAN : (b + 1) * SPAN].reshape(ROWS, HEAD).astype(jnp.bfloat16)
                 )
-        mask_ref[...] = (
-            jnp.where(lane == own, 0.0, -FAR).reshape(GROUPS * SLOT, HEAD).astype(jnp.bfloat16)
-        )
-        u = lax.broadcasted_iota(jnp.int32, (KEYS, LANES), 0)
-        t = lax.broadcasted_iota(jnp.int32, (KEYS, LANES), 1) % ROWS
-        u_order = (u % ROWS) // SLOT * (CTX * SLOT) + u // ROWS * SLOT + u % SLOT
-        t_order = t // SLOT * (CTX * SLOT) + me * SLOT + t % SLOT
-        bias_ref[...] = jnp.where(u_order <= t_order, 0.0, -2.0 * FAR)
+        u = lax.broadcasted_iota(jnp.int32, (ROWS, LANES), 0)
+        t = lax.broadcasted_iota(jnp.int32, (ROWS, LANES), 1) % ROWS
+        u_order = u // SLOT * (CTX * SLOT) + u % SLOT
+        t_order = t // SLOT * (CTX * SLOT) + who[0] * SLOT + t % SLOT
+        for c in range(CTX):
+            bias_ref[c * ROWS : (c + 1) * ROWS, :] = jnp.where(
+                u_order + who[c] * SLOT <= t_order, 0.0, -2.0 * FAR
+            )
         vt_ref[HEAD:, :] = jnp.where(
             lax.broadcasted_iota(jnp.int32, (VALUE_ROWS - HEAD, BLOCKS * KEYS), 0) == 0, 1.0, 0.0
         ).astype(jnp.bfloat16)
+
+    def joined(refs, span):
+        return jnp.concatenate([ref[span].reshape(ROWS, HEAD) for ref in refs], axis=0)
 
     scale = math.log2(math.e) / math.sqrt(HEAD)
     queries = []
@@ -189,9 +197,9 @@
         )
     for b in range(BLOCKS):
         span = slice(b * SPAN, (b + 1) * SPAN)
-        key = jnp.concatenate([k_ref[:, span].reshape(KEYS, HEAD), feat_ref[b]], axis=1)
+        key = jnp.concatenate([joined(k_refs, span), feat_ref[b]], axis=1)
         vt_ref[0:HEAD, b * KEYS : (b + 1) * KEYS] = jnp.transpose(
-            v_ref[:, span].reshape(KEYS, HEAD).astype(jnp.float32)
+            joined(v_refs, span).astype(jnp.float32)
         ).astype(jnp.bfloat16)
         for i in range(b, BLOCKS):
             s = lax.dot_general(
@@ -216,10 +224,13 @@
             ]
 
 
-def attend(lengths, me, q, kv, part):
+def attend(lengths, who, q, keys, values):
     count = GROUPS * SLOT
-    block = (CTX, GROUPS, SLOT, HEAD)
-    low = part * HEADS
+
+    def heads(first):
+        return pl.BlockSpec((GROUPS, SLOT, HEAD), lambda j: (0, 0, first + j))
+
+    blocks = keys + values
     return pl.pallas_call(
         attend_kernel,
         grid=(HEADS,),
@@ -227,8 +238,7 @@
             pl.BlockSpec(memory_space=pltpu.SMEM),
             pl.BlockSpec(memory_space=pltpu.SMEM),
             pl.BlockSpec((count, QW), lambda j: (0, j)),
-            pl.BlockSpec(block, lambda j: (0, 0, 0, low + j)),
-            pl.BlockSpec(block, lambda j: (0, 0, 0, KV_HEADS + low + j)),
+            *(heads(first) for _, first in blocks),
         ],
         out_specs=pl.BlockSpec((count, QW), lambda j: (0, j)),
         out_shape=jax.ShapeDtypeStruct((count, HEADS * QW), jnp.bfloat16),
@@ -240,10 +250,10 @@
             pltpu.VMEM((BLOCKS, BLOCKS, KEYS, LANES), jnp.float32),
         ],
         cost_estimate=pl.CostEstimate(
-            flops=5 * 10**9, transcendentals=2 * 10**7, bytes_accessed=8 * 10**6
+            flops=10**10, transcendentals=4 * 10**7, bytes_accessed=16 * 10**6
         ),
         name="attend",
-    )(lengths, me, q, kv, kv)
+    )(lengths, who, q, *(array for array, _ in blocks))
 
 
 def exchange(x):
@@ -251,24 +261,35 @@
 
 
 def gather(kv):
-    return lax.all_gather(kv, "ctx", axis=0)
+    me = lax.axis_index("ctx").astype(jnp.int32)
+    right = [(i, (i + 2) % CTX) for i in range(CTX)]
+    left = [(i, (i - 2) % CTX) for i in range(CTX)]
+    across = [(i, i ^ 1) for i in range(CTX)]
+    half = kv.shape[2] // 2
+    before = lax.ppermute(kv, "ctx", right)
+    after = lax.ppermute(kv, "ctx", left)
+    far_keys = lax.ppermute(before[:, :, 0:half], "ctx", right)
+    far_values = lax.ppermute(after[:, :, half:], "ctx", left)
+    mine = (kv, before, after, far_keys, far_values)
+    keys, values = [], []
+    for side in (mine, tuple(lax.ppermute(x, "ctx", across) for x in mine)):
+        keys += [(x, 0) for x in side[:4]]
+        values += [(x, KV_HEADS) for x in side[:3]] + [(side[4], 0)]
+    chip, core = me // 2, me % 2
+    who = [(chip + d) % (CTX // 2) * 2 + core for d in (0, 3, 1, 2)]
+    who = jnp.stack(who + [w + 1 - 2 * core for w in who]).reshape(1, CTX)
+    return keys, values, who
 
 
 def body(query_rows, key_rows, token_values, group_of_row, doc_lengths):
     group = group_of_row.reshape(1, group_of_row.shape[0])
-    me = lax.axis_index("ctx").astype(jnp.int32).reshape(1, 1)
     sent = pack_kv(group, key_rows, token_values)
-    queries = pack_q(group, query_rows)
+    (queries,) = pack_q(group, query_rows)
     kv, queries = lax.optimization_barrier((exchange(sent), queries))
-    everyone = gather(kv)
-    outs = []
-    for part in range(PARTS):
-        arrived = exchange(queries[part])
-        if part + 1 < PARTS:
-            arrived, queries = lax.optimization_barrier((arrived, queries))
-        out = attend(doc_lengths, me, arrived.reshape(GROUPS * SLOT, HEADS * QW), everyone, part)
-        outs.append(exchange(out.reshape(GROUPS, SLOT, HEADS * QW)))
-    return unpack(group, outs)
+    keys, values, who = gather(kv)
+    arrived = exchange(queries).reshape(GROUPS * SLOT, HEADS * QW)
+    out = attend(doc_lengths, who, arrived, keys, values)
+    return unpack(group, [exchange(out.reshape(GROUPS, SLOT, HEADS * QW))])
 
 
 def solution(mesh):

time: 193 us -> 179 us (0.927)
  between operations: 13.4 us -> 0.06 us
  starting transfers between devices: 28.4 us -> 38 us
  blocking collectives: 63.3 us -> 56.6 us
  waiting for transfers between devices: 51 us -> 47.6 us
  local copies, waits for them, and re-layouts: 0.97 us -> 4.16 us
  Pallas kernels: 32.9 us -> 30.5 us
    ppermute x0 -> x9, waiting for transfers between devices: none -> 24 us  [the longest x1 18.2 us: gather(): after = lax.ppermute(kv, 'ctx', left)]
    ppermute x0 -> x9, starting transfers between devices: none -> 19.6 us  [the longest x5 13.3 us: gather(): lax.ppermute(x, 'ctx', across)]
    all_to_all x3 -> x2, waiting for transfers between devices: 37.7 us -> 23.6 us  [exchange(): return lax.all_to_all(x, 'dp', split_axis=0, concat_axis=0, tiled=True)]
    all_gather x1 -> x0, waiting for transfers between devices: 13.2 us -> none  [gather(): return lax.all_gather(kv, 'ctx', axis=0)]
    all_to_all x3 -> x2, starting transfers between devices: 28.4 us -> 18.4 us  [exchange(): return lax.all_to_all(x, 'dp', split_axis=0, concat_axis=0, tiled=True)]
    all_to_all x2 -> x1, blocking collectives: 63.3 us -> 56.6 us  [exchange(): return lax.all_to_all(x, 'dp', split_axis=0, concat_axis=0, tiled=True)]
    pallas_call x2 -> x1, Pallas kernels: 23.8 us -> 21.4 us  [attend(): pl.pallas_call(attend_kernel, grid=(HEADS,), in_specs=[pl.BlockSpec(memor...]
    slice x0 -> x2, local copies, waits for them, and re-layouts: none -> 2.15 us  [the longest x1 1.08 us: gather(): far_keys = lax.ppermute(before[:, :, 0:half], 'ctx', right)]
  transfers between devices with their start and end apart: 4 -> 11, of which waited for: 3 -> 6; matrix products, arithmetic and copies ran while one was open for 0% -> 2% of each run, Pallas kernels for 14% -> 2%
where the time goes in v5:
time: 179 us; the launch traced here: 177 us
  blocking collectives  56.6 us (32%)
  waiting for transfers between devices  47.6 us (27%)
  starting transfers between devices  38 us (21%)
  Pallas kernels  30.5 us (17%)
  local copies, waits for them, and re-layouts  4.16 us (2%)
    all_to_all x1, blocking collectives, exchange(): return lax.all_to_all(x, 'dp', split_axis=0, concat_axis=0, tiled=True)  56.6 us
    all_to_all x2, waiting for transfers between devices, exchange(): return lax.all_to_all(x, 'dp', split_axis=0, concat_axis=0, tiled=True)  23.6 us
    pallas_call x1, Pallas kernels, attend(): pl.pallas_call(attend_kernel, grid=(HEADS,), in_specs=[pl.BlockSpec(memor...  21.4 us
    all_to_all x2, starting transfers between devices, exchange(): return lax.all_to_all(x, 'dp', split_axis=0, concat_axis=0, tiled=True)  18.4 us
    ppermute x1, waiting for transfers between devices, gather(): after = lax.ppermute(kv, 'ctx', left)  18.2 us
    ppermute x5, starting transfers between devices, gather(): lax.ppermute(x, 'ctx', across)  13.3 us
    ppermute x1, waiting for transfers between devices, gather(): far_values = lax.ppermute(after[:, :, half:], 'ctx', left)  3.91 us
    ppermute x1, starting transfers between devices, gather(): far_values = lax.ppermute(after[:, :, half:], 'ctx', left)  3.59 us
  transfers between devices with their start and end apart: 11, of which 6 were waited for; matrix products, arithmetic and copies ran while one was open for 2% of the time, Pallas kernels for 2%

profile of v5, /device:TPU:1, one launch (start us, length us, event | category | flops | bytes accessed | tf_op | source)
XLA Modules:
  0.0 176.8 jit_solution(3965121935795261668)
XLA Ops:
  0.0 2.5 %pack_kv.1 = bf16[32,8,2048]{2,1,0:T(8,128)(2,1)} custom-call(s32[1,128]{1,0:T(1,128)} %bitcast.14, bf16[128,1024]{1,0:T(8,128)(2,1)} %k_ref.1, bf16[128,1024]{1,0:T(8,128)(2,1)} %v_ref.1), custom_call_target="tpu_custom_call" | custom-call | tf_op jit(solution)/shard_map/pack_kv/pallas_call | solution.py:63
  2.5 12.0 %all-to-all-start = ((bf16[32,8,2048]{2,1,0:T(8,128)(2,1)}), bf16[32,8,2048]{2,1,0:T(8,128)(2,1)S(1)}, u32[]{:S(2)}, u32[]{:S(2)}) async-start(bf16[32,8,2048]{2,1,0:T(8,128)(2,1)} %pack_kv.1), calls=%async_computation | async-start | bytes 2097152 | tf_op jit(solution)/shard_map/all_to_all | solution.py:260
  14.6 3.4 %pack_q.1 = bf16[32,8,4096]{2,1,0:T(8,128)(2,1)} custom-call(s32[1,128]{1,0:T(1,128)} %bitcast.15, bf16[128,4096]{1,0:T(8,128)(2,1)} %q_ref.1), custom_call_target="tpu_custom_call" | custom-call | tf_op jit(solution)/shard_map/pack_q/pallas_call | solution.py:91
  17.9 22.8 %all-to-all-done.refs_0_.refs_8_ = bf16[32,8,2048]{2,1,0:T(8,128)(2,1)S(1)} async-done(((bf16[32,8,2048]{2,1,0:T(8,128)(2,1)}), bf16[32,8,2048]{2,1,0:T(8,128)(2,1)S(1)}, u32[]{:S(2)}, u32[]{:S(2)}) %all-to-all-start) | async-done | bytes 1048608 | tf_op jit(solution)/shard_map/all_to_all | solution.py:260
  40.8 6.4 %all-to-all-start.1 = ((bf16[32,8,4096]{2,1,0:T(8,128)(2,1)}), bf16[32,8,4096]{2,1,0:T(8,128)(2,1)S(1)}, u32[]{:S(2)}, u32[]{:S(2)}) async-start(bf16[32,8,4096]{2,1,0:T(8,128)(2,1)} %pack_q.1), calls=%async_computation.1 | async-start | bytes 4194304 | tf_op jit(solution)/shard_map/all_to_all | solution.py:260
  47.1 2.6 %collective-permute-start.1 = (bf16[32,8,2048]{2,1,0:T(8,128)(2,1)S(1)}, bf16[32,8,2048]{2,1,0:T(8,128)(2,1)}, u32[]{:S(2)}, u32[]{:S(2)}) collective-permute-start(bf16[32,8,2048]{2,1,0:T(8,128)(2,1)S(1)} %all-to-all-done.refs_0_.refs_8_), channel_id=1, source_target_pairs={{0,6},{1,7},{2,0},{3,1},{4,2},{5,3},{6,4},{7,5},{8,14},{9,15},{10,... | collective-permute-start | bytes 3145736 | tf_op jit(solution)/shard_map/ppermute | solution.py:270
  49.7 2.3 %collective-permute-start.3 = (bf16[32,8,2048]{2,1,0:T(8,128)(2,1)S(1)}, bf16[32,8,2048]{2,1,0:T(8,128)(2,1)}, u32[]{:S(2)}, u32[]{:S(2)}) collective-permute-start(bf16[32,8,2048]{2,1,0:T(8,128)(2,1)S(1)} %all-to-all-done.refs_0_.refs_8_), channel_id=1, source_target_pairs={{0,1},{1,0},{2,3},{3,2},{4,5},{5,4},{6,7},{7,6},{8,9},{9,8},{10,11... | collective-permute-start | bytes 3145736 | tf_op jit(solution)/shard_map/ppermute | solution.py:275
  52.0 18.2 %collective-permute-done.1.refs_2_.refs_10_ = bf16[32,8,2048]{2,1,0:T(8,128)(2,1)} collective-permute-done((bf16[32,8,2048]{2,1,0:T(8,128)(2,1)S(1)}, bf16[32,8,2048]{2,1,0:T(8,128)(2,1)}, u32[]{:S(2)}, u32[]{:S(2)}) %collective-permute-start.1) | collective-permute-done | bytes 1048608 | tf_op jit(solution)/shard_map/ppermute | solution.py:270
  70.2 1.1 slice.9
  71.3 3.6 %collective-permute-start.7 = (bf16[32,8,1024]{2,1,0:T(8,128)(2,1)S(1)}, bf16[32,8,1024]{2,1,0:T(8,128)(2,1)}, u32[]{:S(2)}, u32[]{:S(2)}) collective-permute-start(bf16[32,8,1024]{2,1,0:T(8,128)(2,1)S(1)} %slice.9), channel_id=1, source_target_pairs={{0,6},{1,7},{2,0},{3,1},{4,2},{5,3},{6,4},{7,5},{8,14},{9,15},{10,... | collective-permute-start | bytes 1572872 | tf_op jit(solution)/shard_map/ppermute | solution.py:272
  74.9 1.1 slice.8
  76.1 3.2 %collective-permute-start.5 = (bf16[32,8,2048]{2,1,0:T(8,128)(2,1)}, bf16[32,8,2048]{2,1,0:T(8,128)(2,1)}, u32[]{:S(2)}, u32[]{:S(2)}) collective-permute-start(bf16[32,8,2048]{2,1,0:T(8,128)(2,1)} %collective-permute-done.1.refs_2_.refs_10_), channel_id=1, source_target_pairs={{0,1},{1,0},{2,3},{3,2},{4,5},{5,4},{6,7},{7,6},{8,9},{9,8},{10,11... | collective-permute-start | bytes 3145736 | tf_op jit(solution)/shard_map/ppermute | solution.py:275
  79.3 0.1 collective-permute-start.4
  79.4 3.9 %collective-permute-done.7.refs_11_ = bf16[32,8,1024]{2,1,0:T(8,128)(2,1)} collective-permute-done((bf16[32,8,1024]{2,1,0:T(8,128)(2,1)S(1)}, bf16[32,8,1024]{2,1,0:T(8,128)(2,1)}, u32[]{:S(2)}, u32[]{:S(2)}) %collective-permute-start.7) | collective-permute-done | bytes 524320 | tf_op jit(solution)/shard_map/ppermute | solution.py:272
  83.3 3.7 %collective-permute-start.8 = (bf16[32,8,1024]{2,1,0:T(8,128)(2,1)}, bf16[32,8,1024]{2,1,0:T(8,128)(2,1)}, u32[]{:S(2)}, u32[]{:S(2)}) collective-permute-start(bf16[32,8,1024]{2,1,0:T(8,128)(2,1)} %collective-permute-done.7.refs_11_), channel_id=1, source_target_pairs={{0,1},{1,0},{2,3},{3,2},{4,5},{5,4},{6,7},{7,6},{8,9},{9,8},{10,11... | collective-permute-start | bytes 1572872 | tf_op jit(solution)/shard_map/ppermute | solution.py:275
  87.0 0.7 collective-permute-done.2.refs_3_
  87.7 4.0 %collective-permute-start.6 = (bf16[32,8,1024]{2,1,0:T(8,128)(2,1)}, bf16[32,8,1024]{2,1,0:T(8,128)(2,1)}, u32[]{:S(2)}, u32[]{:S(2)}) collective-permute-start(bf16[32,8,1024]{2,1,0:T(8,128)(2,1)} %collective-permute-done.2.refs_3_), channel_id=1, source_target_pairs={{0,1},{1,0},{2,3},{3,2},{4,5},{5,4},{6,7},{7,6},{8,9},{9,8},{10,11... | collective-permute-start | bytes 1572872 | tf_op jit(solution)/shard_map/ppermute | solution.py:275
  91.7 0.7 stack.35
  92.4 1.2 collective-permute-done.6.refs_7_
  93.6 0.7 all-to-all-done.1
  94.4 1.3 copy-done
  95.7 21.4 %attend.1 = bf16[256,4096]{1,0:T(8,128)(2,1)} custom-call(s32[1,2]{1,0:T(1,128)} %len_ref.1, s32[1,8]{1,0:T(1,128)} %bitcast.17, bf16[256,4096]{1,0:T(8,128)(2,1)} %bitcast.12, bf16[32,8,2048]{2,1,0:T(8,128)(2,1)} %copy-done.1, bf16[32,8,2048]{2,1,0:T(8,128)(2,1)} %collective-permute-done.refs_1_.refs_9_, ...), custom_call_target="tpu_custom_call" | custom-call | flops 10000000000 | bytes 16000000 | tf_op jit(solution)/shard_map/attend/pallas_call | solution.py:234
  117.0 56.6 %all_to_all.15.refs_0_ = bf16[32,8,4096]{2,1,0:T(8,128)(2,1)} all-to-all(bf16[32,8,4096]{2,1,0:T(8,128)(2,1)} %bitcast.13), channel_id=1, replica_groups=mesh['dp'=32,'ctx'=8] {'dp'}, dimensions={0} | all-to-all | bytes 4194304 | tf_op jit(solution)/shard_map/all_to_all | solution.py:260
  173.6 3.2 %unpack.1 = bf16[128,4096]{1,0:T(8,128)(2,1)} custom-call(s32[1,128]{1,0:T(1,128)} %bitcast.16, bf16[32,8,4096]{2,1,0:T(8,128)(2,1)} %all_to_all.15.refs_0_), custom_call_target="tpu_custom_call" | custom-call | tf_op jit(solution)/shard_map/unpack/pallas_call | solution.py:116
  (10 shorter events, 0.1 us)
Async XLA Ops:
  2.5 38.2 %all-to-all-start = ((bf16[32,8,2048]{2,1,0:T(8,128)(2,1)}), bf16[32,8,2048]{2,1,0:T(8,128)(2,1)S(1)}, u32[]{:S(2)}, u32[]{:S(2)}) async-start(bf16[32,8,2048]{2,1,0:T(8,128)(2,1)} %pack_kv.1), calls=%async_computation | async-start | bytes 2097152 | tf_op jit(solution)/shard_map/all_to_all | solution.py:260
  40.8 30.5 %copy-start.1 = (bf16[32,8,2048]{2,1,0:T(8,128)(2,1)}, bf16[32,8,2048]{2,1,0:T(8,128)(2,1)S(1)}, u32[]{:S(2)}) copy-start(bf16[32,8,2048]{2,1,0:T(8,128)(2,1)S(1)} %all-to-all-done.refs_0_.refs_8_) | copy-start | bytes 3145732
  40.8 53.6 %all-to-all-start.1 = ((bf16[32,8,4096]{2,1,0:T(8,128)(2,1)}), bf16[32,8,4096]{2,1,0:T(8,128)(2,1)S(1)}, u32[]{:S(2)}, u32[]{:S(2)}) async-start(bf16[32,8,4096]{2,1,0:T(8,128)(2,1)} %pack_q.1), calls=%async_computation.1 | async-start | bytes 4194304 | tf_op jit(solution)/shard_map/all_to_all | solution.py:260
  47.1 23.1 %collective-permute-start.1 = (bf16[32,8,2048]{2,1,0:T(8,128)(2,1)S(1)}, bf16[32,8,2048]{2,1,0:T(8,128)(2,1)}, u32[]{:S(2)}, u32[]{:S(2)}) collective-permute-start(bf16[32,8,2048]{2,1,0:T(8,128)(2,1)S(1)} %all-to-all-done.refs_0_.refs_8_), channel_id=1, source_target_pairs={{0,6},{1,7},{2,0},{3,1},{4,2},{5,3},{6,4},{7,5},{8,14},{9,15},{10,... | collective-permute-start | bytes 3145736 | tf_op jit(solution)/shard_map/ppermute | solution.py:270
  49.7 25.2 %collective-permute-start = (bf16[32,8,2048]{2,1,0:T(8,128)(2,1)S(1)}, bf16[32,8,2048]{2,1,0:T(8,128)(2,1)}, u32[]{:S(2)}, u32[]{:S(2)}) collective-permute-start(bf16[32,8,2048]{2,1,0:T(8,128)(2,1)S(1)} %all-to-all-done.refs_0_.refs_8_), channel_id=1, source_target_pairs={{0,2},{1,3},{2,4},{3,5},{4,6},{5,7},{6,0},{7,1},{8,10},{9,11},{10,... | collective-permute-start | bytes 3145736 | tf_op jit(solution)/shard_map/ppermute | solution.py:269
  49.7 42.7 %collective-permute-start.3 = (bf16[32,8,2048]{2,1,0:T(8,128)(2,1)S(1)}, bf16[32,8,2048]{2,1,0:T(8,128)(2,1)}, u32[]{:S(2)}, u32[]{:S(2)}) collective-permute-start(bf16[32,8,2048]{2,1,0:T(8,128)(2,1)S(1)} %all-to-all-done.refs_0_.refs_8_), channel_id=1, source_target_pairs={{0,1},{1,0},{2,3},{3,2},{4,5},{5,4},{6,7},{7,6},{8,9},{9,8},{10,11... | collective-permute-start | bytes 3145736 | tf_op jit(solution)/shard_map/ppermute | solution.py:275
  71.3 12.0 %collective-permute-start.7 = (bf16[32,8,1024]{2,1,0:T(8,128)(2,1)S(1)}, bf16[32,8,1024]{2,1,0:T(8,128)(2,1)}, u32[]{:S(2)}, u32[]{:S(2)}) collective-permute-start(bf16[32,8,1024]{2,1,0:T(8,128)(2,1)S(1)} %slice.9), channel_id=1, source_target_pairs={{0,6},{1,7},{2,0},{3,1},{4,2},{5,3},{6,4},{7,5},{8,14},{9,15},{10,... | collective-permute-start | bytes 1572872 | tf_op jit(solution)/shard_map/ppermute | solution.py:272
  76.0 11.7 %collective-permute-start.2 = (bf16[32,8,1024]{2,1,0:T(8,128)(2,1)S(1)}, bf16[32,8,1024]{2,1,0:T(8,128)(2,1)}, u32[]{:S(2)}, u32[]{:S(2)}) collective-permute-start(bf16[32,8,1024]{2,1,0:T(8,128)(2,1)S(1)} %slice.8), channel_id=1, source_target_pairs={{0,2},{1,3},{2,4},{3,5},{4,6},{5,7},{6,0},{7,1},{8,10},{9,11},{10,... | collective-permute-start | bytes 1572872 | tf_op jit(solution)/shard_map/ppermute | solution.py:271
  76.1 17.5 %collective-permute-start.5 = (bf16[32,8,2048]{2,1,0:T(8,128)(2,1)}, bf16[32,8,2048]{2,1,0:T(8,128)(2,1)}, u32[]{:S(2)}, u32[]{:S(2)}) collective-permute-start(bf16[32,8,2048]{2,1,0:T(8,128)(2,1)} %collective-permute-done.1.refs_2_.refs_10_), channel_id=1, source_target_pairs={{0,1},{1,0},{2,3},{3,2},{4,5},{5,4},{6,7},{7,6},{8,9},{9,8},{10,11... | collective-permute-start | bytes 3145736 | tf_op jit(solution)/shard_map/ppermute | solution.py:275
  79.3 14.3 %collective-permute-start.4 = (bf16[32,8,2048]{2,1,0:T(8,128)(2,1)}, bf16[32,8,2048]{2,1,0:T(8,128)(2,1)}, u32[]{:S(2)}, u32[]{:S(2)}) collective-permute-start(bf16[32,8,2048]{2,1,0:T(8,128)(2,1)} %collective-permute-done.refs_1_.refs_9_), channel_id=1, source_target_pairs={{0,1},{1,0},{2,3},{3,2},{4,5},{5,4},{6,7},{7,6},{8,9},{9,8},{10,11... | collective-permute-start | bytes 3145736 | tf_op jit(solution)/shard_map/ppermute | solution.py:275
  83.3 9.1 %collective-permute-start.8 = (bf16[32,8,1024]{2,1,0:T(8,128)(2,1)}, bf16[32,8,1024]{2,1,0:T(8,128)(2,1)}, u32[]{:S(2)}, u32[]{:S(2)}) collective-permute-start(bf16[32,8,1024]{2,1,0:T(8,128)(2,1)} %collective-permute-done.7.refs_11_), channel_id=1, source_target_pairs={{0,1},{1,0},{2,3},{3,2},{4,5},{5,4},{6,7},{7,6},{8,9},{9,8},{10,11... | collective-permute-start | bytes 1572872 | tf_op jit(solution)/shard_map/ppermute | solution.py:275
  87.7 5.9 %collective-permute-start.6 = (bf16[32,8,1024]{2,1,0:T(8,128)(2,1)}, bf16[32,8,1024]{2,1,0:T(8,128)(2,1)}, u32[]{:S(2)}, u32[]{:S(2)}) collective-permute-start(bf16[32,8,1024]{2,1,0:T(8,128)(2,1)} %collective-permute-done.2.refs_3_), channel_id=1, source_target_pairs={{0,1},{1,0},{2,3},{3,2},{4,5},{5,4},{6,7},{7,6},{8,9},{9,8},{10,11... | collective-permute-start | bytes 1572872 | tf_op jit(solution)/shard_map/ppermute | solution.py:275
  94.4 1.3 copy-start

commit v6 on v3

v6 whole, which is shorter than its diff:
```python
import math

import jax
import jax.numpy as jnp
from jax import lax
from jax.experimental import pallas as pl
from jax.experimental.pallas import tpu as pltpu
from jax.sharding import PartitionSpec as P

KV_HEADS = 8
HEAD = 128
PER_KV = 4
GROUPS = 32
SLOT = 8
QW = PER_KV * HEAD
ROW_W = QW + 2 * HEAD
EMPTY = 64.0
FAR = 16384.0
BLOCKS = 4
KEYS = 512
ROWS = 64
LANES = PER_KV * ROWS
GRANT = 24 << 20
VALUE_ROWS = HEAD + 16
STEP = 2


def slot_targets(group_row):
    rows = group_row.shape[1]
    row = jnp.broadcast_to(group_row.astype(jnp.float32), (rows, rows))
    col = jnp.transpose(row)
    earlier = lax.broadcasted_iota(jnp.int32, (rows, rows), 0) < lax.broadcasted_iota(
        jnp.int32, (rows, rows), 1
    )
    same = jnp.where((col == row) & earlier, 1.0, 0.0)
    position = jnp.sum(same, axis=0, keepdims=True)
    return row[0:1, :] * float(SLOT) + position


def pack_kernel(group_ref, q_ref, k_ref, v_ref, out_ref, pick_ref):
    slots = GROUPS * SLOT
    rows = q_ref.shape[0]

    @pl.when(pl.program_id(0) == 0)
    def _():
        target = slot_targets(group_ref[...])
        slot = lax.broadcasted_iota(jnp.int32, (slots, rows), 0).astype(jnp.float32)
        pick_ref[...] = jnp.where(slot == target, 1.0, 0.0).astype(jnp.bfloat16)

    pick = pick_ref[...]

    def moved(x):
        return jnp.dot(pick, x, preferred_element_type=jnp.float32)

    def laid(x):
        return x.reshape(GROUPS, SLOT, x.shape[1]).astype(jnp.bfloat16)

    empty = (1.0 - jnp.sum(pick.astype(jnp.float32), axis=1, keepdims=True)) * EMPTY
    for j in range(STEP):
        head = slice(j * HEAD, (j + 1) * HEAD)
        out_ref[:, j, :, 0:QW] = laid(moved(q_ref[:, j * QW : (j + 1) * QW]))
        out_ref[:, j, :, QW : QW + HEAD] = laid(moved(k_ref[:, head]))
        out_ref[:, j, :, QW + HEAD :] = laid(moved(v_ref[:, head]) + empty)


def pack(group, q, k, v):
    rows = q.shape[0]
    return pl.pallas_call(
        pack_kernel,
        grid=(KV_HEADS // STEP,),
        in_specs=[
            pl.BlockSpec((1, rows), lambda j: (0, 0)),
            pl.BlockSpec((rows, STEP * QW), lambda j: (0, j)),
            pl.BlockSpec((rows, STEP * HEAD), lambda j: (0, j)),
            pl.BlockSpec((rows, STEP * HEAD), lambda j: (0, j)),
        ],
        out_specs=pl.BlockSpec((GROUPS, STEP, SLOT, ROW_W), lambda j: (0, j, 0, 0)),
        out_shape=jax.ShapeDtypeStruct((GROUPS, KV_HEADS, SLOT, ROW_W), jnp.bfloat16),
        scratch_shapes=[pltpu.VMEM((GROUPS * SLOT, rows), jnp.bfloat16)],
        compiler_params=pltpu.CompilerParams(vmem_limit_bytes=GRANT),
        name="pack",
    )(group, q, k, v)


def unpack_kernel(group_ref, o_ref, out_ref, pick_ref):
    slots = GROUPS * SLOT
    rows = out_ref.shape[0]

    @pl.when(pl.program_id(0) == 0)
    def _():
        target = slot_targets(group_ref[...])
        slot = lax.broadcasted_iota(jnp.int32, (slots, rows), 0).astype(jnp.float32)
        pick_ref[...] = jnp.transpose(jnp.where(slot == target, 1.0, 0.0)).astype(jnp.bfloat16)

    for j in range(STEP):
        x = o_ref[:, j].reshape(slots, QW)
        out_ref[:, j * QW : (j + 1) * QW] = jnp.dot(
            pick_ref[...], x, preferred_element_type=jnp.float32
        ).astype(jnp.bfloat16)


def unpack(group, o):
    rows = group.shape[1]
    return pl.pallas_call(
        unpack_kernel,
        grid=(KV_HEADS // STEP,),
        in_specs=[
            pl.BlockSpec((1, rows), lambda j: (0, 0)),
            pl.BlockSpec((GROUPS, STEP, SLOT, QW), lambda j: (0, j, 0, 0)),
        ],
        out_specs=pl.BlockSpec((rows, STEP * QW), lambda j: (0, j)),
        out_shape=jax.ShapeDtypeStruct((rows, KV_HEADS * QW), jnp.bfloat16),
        scratch_shapes=[pltpu.VMEM((rows, GROUPS * SLOT), jnp.bfloat16)],
        compiler_params=pltpu.CompilerParams(vmem_limit_bytes=GRANT),
        name="unpack",
    )(group, o)


def attend_kernel(len_ref, q_ref, k_ref, v_ref, o_ref, feat_ref, mask_ref, ahead_ref, vt_ref, s_ref):
    count = k_ref.shape[0]
    step = pl.program_id(0)

    @pl.when(step == 0)
    def _():
        first_len = len_ref[0, 0].astype(jnp.float32)
        sources = count // SLOT
        shape = (sources, SLOT, HEAD)
        lane = lax.broadcasted_iota(jnp.int32, shape, 2).astype(jnp.float32)
        slot = lax.broadcasted_iota(jnp.int32, shape, 1).astype(jnp.float32)
        value = v_ref[...].astype(jnp.float32)
        used = jnp.broadcast_to(
            jnp.where(value.reshape(shape)[:, :, 0:1] < 0.5 * EMPTY, 1.0, 0.0), shape
        )
        before = jnp.where(
            lax.broadcasted_iota(jnp.int32, (sources, sources), 0)
            > lax.broadcasted_iota(jnp.int32, (sources, sources), 1),
            1.0,
            0.0,
        )
        base = jnp.dot(
            before.astype(jnp.bfloat16),
            jnp.sum(used, axis=1).astype(jnp.bfloat16),
            preferred_element_type=jnp.float32,
        )
        rank = base[:, None, :] + slot
        code = jnp.where(used > 0.5, jnp.where(rank < first_len, 0.0, 1.0), 2.0)
        hit = lane == code
        feat_ref[...] = jnp.where(hit, 1.0, 0.0).reshape(count, HEAD).astype(jnp.bfloat16)
        mask_ref[...] = jnp.where(hit, 0.0, -FAR).reshape(mask_ref.shape).astype(jnp.bfloat16)
        ahead_ref[...] = (
            lax.broadcasted_iota(jnp.int32, (KEYS, LANES), 0)
            - lax.broadcasted_iota(jnp.int32, (KEYS, LANES), 1) % ROWS
        ).astype(jnp.float32)
        vt_ref[0:HEAD, :] = jnp.transpose(value).astype(jnp.bfloat16)
        vt_ref[HEAD:, :] = jnp.where(
            lax.broadcasted_iota(jnp.int32, (VALUE_ROWS - HEAD, count), 0) == 0, 1.0, 0.0
        ).astype(jnp.bfloat16)

    scale = math.log2(math.e) / math.sqrt(HEAD)
    offset = pl.multiple_of(step * ROWS, ROWS)
    bias = jnp.where(ahead_ref[...] <= offset.astype(jnp.float32), 0.0, -2.0 * FAR)
    queries = []
    for i in range(BLOCKS):
        mask = mask_ref[i, pl.ds(offset, ROWS), :]
        queries.append(
            jnp.concatenate(
                [
                    jnp.concatenate([q_ref[i, :, h * HEAD : (h + 1) * HEAD], mask], axis=1)
                    for h in range(PER_KV)
                ],
                axis=0,
            )
        )
    for b in range(BLOCKS):
        at = slice(b * KEYS, (b + 1) * KEYS)
        key = jnp.concatenate([k_ref[at, :], feat_ref[at, :]], axis=1)
        for i in range(b, BLOCKS):
            s = lax.dot_general(
                key, queries[i], (((1,), (1,)), ((), ())), preferred_element_type=jnp.float32
            )
            s_ref[i * (i + 1) // 2 + b] = s + bias if i == b else s
    for i in range(BLOCKS):
        low = i * (i + 1) // 2
        top = jnp.max(s_ref[low], axis=0, keepdims=True)
        for b in range(1, i + 1):
            top = jnp.maximum(top, jnp.max(s_ref[low + b], axis=0, keepdims=True))
        acc = None
        for b in range(i + 1):
            w = jnp.exp2((s_ref[low + b] - top) * scale).astype(jnp.bfloat16)
            part = jnp.dot(
                vt_ref[:, b * KEYS : (b + 1) * KEYS], w, preferred_element_type=jnp.float32
            )
            acc = part if acc is None else acc + part
        out = jnp.transpose(acc[0:HEAD] * (1.0 / acc[HEAD : HEAD + 1])).astype(jnp.bfloat16)
        for h in range(PER_KV):
            o_ref[i, :, h * HEAD : (h + 1) * HEAD] = out[h * ROWS : (h + 1) * ROWS]


def attend(lengths, rows):
    count = rows.shape[0]
    tile = pl.BlockSpec((BLOCKS, ROWS, QW), lambda i: (0, i, 0))
    out = pl.pallas_call(
        attend_kernel,
        grid=(KEYS // ROWS,),
        in_specs=[
            pl.BlockSpec(memory_space=pltpu.SMEM),
            tile,
            pl.BlockSpec((count, HEAD), lambda i: (0, PER_KV)),
            pl.BlockSpec((count, HEAD), lambda i: (0, PER_KV + 1)),
        ],
        out_specs=tile,
        out_shape=jax.ShapeDtypeStruct((BLOCKS, KEYS, QW), jnp.bfloat16),
        scratch_shapes=[
            pltpu.VMEM((count, HEAD), jnp.bfloat16),
            pltpu.VMEM((BLOCKS, KEYS, HEAD), jnp.bfloat16),
            pltpu.VMEM((KEYS, LANES), jnp.float32),
            pltpu.VMEM((VALUE_ROWS, count), jnp.bfloat16),
            pltpu.VMEM((BLOCKS * (BLOCKS + 1) // 2, KEYS, LANES), jnp.float32),
        ],
        compiler_params=pltpu.CompilerParams(vmem_limit_bytes=GRANT),
        name="attend",
    )(lengths, rows.reshape(BLOCKS, KEYS, ROW_W), rows, rows)
    return out.reshape(count, QW)


def body(query_rows, key_rows, token_values, group_of_row, doc_lengths):
    devices = lax.axis_size("dp") * lax.axis_size("ctx")
    group = group_of_row.reshape(1, group_of_row.shape[0])
    packed = pack(group, query_rows, key_rows, token_values)
    arrived = lax.all_to_all(
        packed.reshape(devices, SLOT, ROW_W), ("dp", "ctx"), split_axis=0, concat_axis=0, tiled=True
    )
    result = attend(doc_lengths, arrived.reshape(devices * SLOT, ROW_W))
    returned = lax.all_to_all(
        result.reshape(devices, SLOT, QW), ("dp", "ctx"), split_axis=0, concat_axis=0, tiled=True
    )
    return unpack(group, returned.reshape(GROUPS, KV_HEADS, SLOT, QW))


def solution(mesh):
    rows = P(("dp", "ctx"), None)
    return jax.shard_map(
        body,
        mesh=mesh,
        in_specs=(rows, rows, rows, rows, P("dp", None)),
        out_specs=rows,
        check_vma=False,
    )
```

time: 183 us -> 177 us (0.967)
  Pallas kernels: 32.1 us -> 23.2 us
  local copies, waits for them, and re-layouts: 0 us -> 3.79 us
  blocking collectives: 152 us -> 150 us
    pallas_call x1, Pallas kernels: 23.2 us -> 18.8 us  [attend(): pl.pallas_call(attend_kernel, grid=(KEYS // ROWS,), in_specs=[pl.BlockSpe...]
    unnamed x0 -> x12, local copies, waits for them, and re-layouts: none -> 3.79 us
    pallas_call x1, Pallas kernels: 4.68 us -> 1.96 us  [pack(): pl.pallas_call(pack_kernel, grid=(KV_HEADS // STEP,), in_specs=[pl.BlockS...]
where the time goes in v6:
time: 177 us
  blocking collectives  150 us (85%)
  Pallas kernels  23.2 us (13%)
  local copies, waits for them, and re-layouts  3.79 us (2%)
    all_to_all x1, blocking collectives, body(): lax.all_to_all(packed.reshape(devices, SLOT, ROW_W), ('dp', 'ctx'), split...  90.2 us
    all_to_all x1, blocking collectives, body(): lax.all_to_all(result.reshape(devices, SLOT, QW), ('dp', 'ctx'), split_ax...  59.8 us
    pallas_call x1, Pallas kernels, attend(): pl.pallas_call(attend_kernel, grid=(KEYS // ROWS,), in_specs=[pl.BlockSpe...  18.8 us
    unnamed x12, local copies, waits for them, and re-layouts  3.79 us

profile of v6, /device:TPU:1, one launch (start us, length us, event | category | flops | bytes accessed | tf_op | source)
XLA Modules:
  0.0 177.0 jit_solution(3359606191456794670)
XLA Ops:
  0.0 0.0 copy-start
  0.0 1.2 copy-done
  1.2 0.0 copy-start.1
  1.2 0.9 copy-done.1
  2.2 0.0 copy-start.2
  2.2 0.9 copy-done.2
  3.1 0.0 copy-start.3
  3.1 0.7 copy-done.3
  3.8 2.0 %pack.1 = bf16[32,8,8,768]{3,2,1,0:T(8,128)(2,1)S(1)} custom-call(s32[1,128]{1,0:T(1,128)S(1)} %bitcast.12, bf16[128,4096]{1,0:T(8,128)(2,1)S(1)} %copy-done, bf16[128,1024]{1,0:T(8,128)(2,1)S(1)} %copy-done.1, bf16[128,1024]{1,0:T(8,128)(2,1)S(1)} %copy-done.2), custom_call_target="tpu_custom_call" | custom-call | tf_op jit(solution)/shard_map/pack/pallas_call | solution.py:68
  5.8 0.0 copy-start.5
  5.8 90.2 %all_to_all.10 = bf16[256,8,768]{2,1,0:T(8,128)(2,1)S(1)} all-to-all(bf16[256,8,768]{2,1,0:T(8,128)(2,1)S(1)} %bitcast.9), channel_id=1, replica_groups=mesh['dp'=32,'ctx'=8] {'dp','ctx'}, dimensions={0} | all-to-all | bytes 6291456 | tf_op jit(solution)/shard_map/all_to_all | solution.py:230
  96.0 0.0 copy-done.5
  96.0 18.8 %attend.1 = bf16[4,512,512]{2,1,0:T(8,128)(2,1)S(1)} custom-call(s32[1,2]{1,0:T(1,128)S(1)} %copy-done.5, bf16[4,512,768]{2,1,0:T(8,128)(2,1)S(1)} %bitcast.6, bf16[2048,768]{1,0:T(8,128)(2,1)S(1)} %bitcast.7, bf16[2048,768]{1,0:T(8,128)(2,1)S(1)} %bitcast.8), custom_call_target="tpu_custom_call" | custom-call | tf_op jit(solution)/shard_map/attend/pallas_call | solution.py:202
  114.8 0.0 copy-start.4
  114.8 59.8 %all_to_all.11 = bf16[256,8,512]{2,1,0:T(8,128)(2,1)S(1)} all-to-all(bf16[256,8,512]{2,1,0:T(8,128)(2,1)S(1)} %bitcast.11), channel_id=1, replica_groups=mesh['dp'=32,'ctx'=8] {'dp','ctx'}, dimensions={0} | all-to-all | bytes 4194304 | tf_op jit(solution)/shard_map/all_to_all | solution.py:234
  174.6 0.0 copy-done.4
  174.6 2.5 %unpack.1 = bf16[128,4096]{1,0:T(8,128)(2,1)} custom-call(s32[1,128]{1,0:T(1,128)S(1)} %bitcast.13, bf16[32,8,8,512]{3,2,1,0:T(8,128)(2,1)S(1)} %bitcast.10), custom_call_target="tpu_custom_call" | custom-call | tf_op jit(solution)/shard_map/unpack/pallas_call | solution.py:104
Async XLA Ops:
  0.0 1.2 copy-start
  1.2 0.9 copy-start.1
  2.2 0.9 copy-start.2
  3.1 0.7 copy-start.3
  5.8 90.3 %copy-start.5 = (s32[1,2]{1,0:T(1,128)S(1)}, s32[1,2]{1,0:T(1,128)}, u32[]{:S(2)}) copy-start(s32[1,2]{1,0:T(1,128)} %len_ref.1) | copy-start | bytes 28
  114.8 59.8 %copy-start.4 = (s32[128,1]{0,1:T(1,128)S(1)}, s32[128,1]{0,1:T(1,128)}, u32[]{:S(2)}) copy-start(s32[128,1]{0,1:T(1,128)} %param.8) | copy-start | bytes 1540

commit v7 on v6

--- a/solution.py
+++ b/solution.py
@@ -20,6 +20,8 @@
 KEYS = 512
 ROWS = 64
 LANES = PER_KV * ROWS
+CTX = 8
+PART = BLOCKS * ROWS
 GRANT = 24 << 20
 VALUE_ROWS = HEAD + 16
 STEP = 2
@@ -58,9 +60,9 @@
     empty = (1.0 - jnp.sum(pick.astype(jnp.float32), axis=1, keepdims=True)) * EMPTY
     for j in range(STEP):
         head = slice(j * HEAD, (j + 1) * HEAD)
-        out_ref[:, j, :, 0:QW] = laid(moved(q_ref[:, j * QW : (j + 1) * QW]))
-        out_ref[:, j, :, QW : QW + HEAD] = laid(moved(k_ref[:, head]))
-        out_ref[:, j, :, QW + HEAD :] = laid(moved(v_ref[:, head]) + empty)
+        out_ref[j, :, :, 0:QW] = laid(moved(q_ref[:, j * QW : (j + 1) * QW]))
+        out_ref[j, :, :, QW : QW + HEAD] = laid(moved(k_ref[:, head]))
+        out_ref[j, :, :, QW + HEAD :] = laid(moved(v_ref[:, head]) + empty)
 
 
 def pack(group, q, k, v):
@@ -74,12 +76,12 @@
             pl.BlockSpec((rows, STEP * HEAD), lambda j: (0, j)),
             pl.BlockSpec((rows, STEP * HEAD), lambda j: (0, j)),
         ],
-        out_specs=pl.BlockSpec((GROUPS, STEP, SLOT, ROW_W), lambda j: (0, j, 0, 0)),
-        out_shape=jax.ShapeDtypeStruct((GROUPS, KV_HEADS, SLOT, ROW_W), jnp.bfloat16),
+        out_specs=pl.BlockSpec((STEP, GROUPS, SLOT, ROW_W), lambda j: (j, 0, 0, 0)),
+        out_shape=jax.ShapeDtypeStruct((KV_HEADS, GROUPS, SLOT, ROW_W), jnp.bfloat16),
         scratch_shapes=[pltpu.VMEM((GROUPS * SLOT, rows), jnp.bfloat16)],
         compiler_params=pltpu.CompilerParams(vmem_limit_bytes=GRANT),
         name="pack",
-    )(group, q, k, v)
+    )(group, *(pltpu.with_memory_space_constraint(x, pltpu.HBM) for x in (q, k, v)))
 
 
 def unpack_kernel(group_ref, o_ref, out_ref, pick_ref):
@@ -93,7 +95,7 @@
         pick_ref[...] = jnp.transpose(jnp.where(slot == target, 1.0, 0.0)).astype(jnp.bfloat16)
 
     for j in range(STEP):
-        x = o_ref[:, j].reshape(slots, QW)
+        x = o_ref[j].reshape(slots, QW)
         out_ref[:, j * QW : (j + 1) * QW] = jnp.dot(
             pick_ref[...], x, preferred_element_type=jnp.float32
         ).astype(jnp.bfloat16)
@@ -106,7 +108,7 @@
         grid=(KV_HEADS // STEP,),
         in_specs=[
             pl.BlockSpec((1, rows), lambda j: (0, 0)),
-            pl.BlockSpec((GROUPS, STEP, SLOT, QW), lambda j: (0, j, 0, 0)),
+            pl.BlockSpec((STEP, GROUPS, SLOT, QW), lambda j: (j, 0, 0, 0)),
         ],
         out_specs=pl.BlockSpec((rows, STEP * QW), lambda j: (0, j)),
         out_shape=jax.ShapeDtypeStruct((rows, KV_HEADS * QW), jnp.bfloat16),
@@ -120,60 +122,74 @@
     count = k_ref.shape[0]
     step = pl.program_id(0)
 
+    def joined(ref, b):
+        low = b * ROWS
+        return jnp.concatenate(
+            [ref[c * PART + low : c * PART + low + ROWS, :] for c in range(CTX)], axis=0
+        )
+
     @pl.when(step == 0)
     def _():
         first_len = len_ref[0, 0].astype(jnp.float32)
-        sources = count // SLOT
-        shape = (sources, SLOT, HEAD)
+        shape = (GROUPS, SLOT, HEAD)
         lane = lax.broadcasted_iota(jnp.int32, shape, 2).astype(jnp.float32)
         slot = lax.broadcasted_iota(jnp.int32, shape, 1).astype(jnp.float32)
         value = v_ref[...].astype(jnp.float32)
-        used = jnp.broadcast_to(
-            jnp.where(value.reshape(shape)[:, :, 0:1] < 0.5 * EMPTY, 1.0, 0.0), shape
-        )
+        used = [
+            jnp.broadcast_to(
+                jnp.where(part.reshape(shape)[:, :, 0:1] < 0.5 * EMPTY, 1.0, 0.0), shape
+            )
+            for part in (value[c * PART : (c + 1) * PART] for c in range(CTX))
+        ]
+        number = [jnp.sum(u, axis=1) for u in used]
         before = jnp.where(
-            lax.broadcasted_iota(jnp.int32, (sources, sources), 0)
-            > lax.broadcasted_iota(jnp.int32, (sources, sources), 1),
+            lax.broadcasted_iota(jnp.int32, (GROUPS, GROUPS), 0)
+            > lax.broadcasted_iota(jnp.int32, (GROUPS, GROUPS), 1),
             1.0,
             0.0,
         )
         base = jnp.dot(
             before.astype(jnp.bfloat16),
-            jnp.sum(used, axis=1).astype(jnp.bfloat16),
+            sum(number).astype(jnp.bfloat16),
             preferred_element_type=jnp.float32,
         )
-        rank = base[:, None, :] + slot
-        code = jnp.where(used > 0.5, jnp.where(rank < first_len, 0.0, 1.0), 2.0)
-        hit = lane == code
-        feat_ref[...] = jnp.where(hit, 1.0, 0.0).reshape(count, HEAD).astype(jnp.bfloat16)
-        mask_ref[...] = jnp.where(hit, 0.0, -FAR).reshape(mask_ref.shape).astype(jnp.bfloat16)
-        ahead_ref[...] = (
-            lax.broadcasted_iota(jnp.int32, (KEYS, LANES), 0)
-            - lax.broadcasted_iota(jnp.int32, (KEYS, LANES), 1) % ROWS
-        ).astype(jnp.float32)
-        vt_ref[0:HEAD, :] = jnp.transpose(value).astype(jnp.bfloat16)
+        for c in range(CTX):
+            rank = base[:, None, :] + slot
+            base = base + number[c]
+            code = jnp.where(used[c] > 0.5, jnp.where(rank < first_len, 0.0, 1.0), 2.0)
+            hit = lane == code
+            at = slice(c * PART, (c + 1) * PART)
+            feat_ref[at, :] = jnp.where(hit, 1.0, 0.0).reshape(PART, HEAD).astype(jnp.bfloat16)
+            mask_ref[at, :] = jnp.where(hit, 0.0, -FAR).reshape(PART, HEAD).astype(jnp.bfloat16)
+        u = lax.broadcasted_iota(jnp.int32, (KEYS, LANES), 0)
+        t = lax.broadcasted_iota(jnp.int32, (KEYS, LANES), 1) % ROWS
+        u_order = u % ROWS // SLOT * (CTX * SLOT) + u // ROWS * SLOT + u % SLOT
+        ahead_ref[...] = (u_order - t // SLOT * (CTX * SLOT) - t % SLOT).astype(jnp.float32)
+        for b in range(BLOCKS):
+            vt_ref[0:HEAD, b * KEYS : (b + 1) * KEYS] = jnp.transpose(joined(value, b)).astype(
+                jnp.bfloat16
+            )
         vt_ref[HEAD:, :] = jnp.where(
             lax.broadcasted_iota(jnp.int32, (VALUE_ROWS - HEAD, count), 0) == 0, 1.0, 0.0
         ).astype(jnp.bfloat16)
 
     scale = math.log2(math.e) / math.sqrt(HEAD)
-    offset = pl.multiple_of(step * ROWS, ROWS)
-    bias = jnp.where(ahead_ref[...] <= offset.astype(jnp.float32), 0.0, -2.0 * FAR)
+    bias = jnp.where(ahead_ref[...] <= (step * SLOT).astype(jnp.float32), 0.0, -2.0 * FAR)
+
     queries = []
     for i in range(BLOCKS):
-        mask = mask_ref[i, pl.ds(offset, ROWS), :]
+        mask = mask_ref[pl.ds(pl.multiple_of(step * PART + i * ROWS, ROWS), ROWS), :]
         queries.append(
             jnp.concatenate(
                 [
-                    jnp.concatenate([q_ref[i, :, h * HEAD : (h + 1) * HEAD], mask], axis=1)
+                    jnp.concatenate([q_ref[0, i, :, h * HEAD : (h + 1) * HEAD], mask], axis=1)
                     for h in range(PER_KV)
                 ],
                 axis=0,
             )
         )
     for b in range(BLOCKS):
-        at = slice(b * KEYS, (b + 1) * KEYS)
-        key = jnp.concatenate([k_ref[at, :], feat_ref[at, :]], axis=1)
+        key = jnp.concatenate([joined(k_ref, b), joined(feat_ref, b)], axis=1)
         for i in range(b, BLOCKS):
             s = lax.dot_general(
                 key, queries[i], (((1,), (1,)), ((), ())), preferred_element_type=jnp.float32
@@ -193,15 +209,15 @@
             acc = part if acc is None else acc + part
         out = jnp.transpose(acc[0:HEAD] * (1.0 / acc[HEAD : HEAD + 1])).astype(jnp.bfloat16)
         for h in range(PER_KV):
-            o_ref[i, :, h * HEAD : (h + 1) * HEAD] = out[h * ROWS : (h + 1) * ROWS]
+            o_ref[0, i, :, h * HEAD : (h + 1) * HEAD] = out[h * ROWS : (h + 1) * ROWS]
 
 
 def attend(lengths, rows):
     count = rows.shape[0]
-    tile = pl.BlockSpec((BLOCKS, ROWS, QW), lambda i: (0, i, 0))
+    tile = pl.BlockSpec((1, BLOCKS, ROWS, QW), lambda c: (c, 0, 0, 0))
     out = pl.pallas_call(
         attend_kernel,
-        grid=(KEYS // ROWS,),
+        grid=(CTX,),
         in_specs=[
             pl.BlockSpec(memory_space=pltpu.SMEM),
             tile,
@@ -209,17 +225,17 @@
             pl.BlockSpec((count, HEAD), lambda i: (0, PER_KV + 1)),
         ],
         out_specs=tile,
-        out_shape=jax.ShapeDtypeStruct((BLOCKS, KEYS, QW), jnp.bfloat16),
+        out_shape=jax.ShapeDtypeStruct((CTX, BLOCKS, ROWS, QW), jnp.bfloat16),
         scratch_shapes=[
             pltpu.VMEM((count, HEAD), jnp.bfloat16),
-            pltpu.VMEM((BLOCKS, KEYS, HEAD), jnp.bfloat16),
+            pltpu.VMEM((count, HEAD), jnp.bfloat16),
             pltpu.VMEM((KEYS, LANES), jnp.float32),
             pltpu.VMEM((VALUE_ROWS, count), jnp.bfloat16),
             pltpu.VMEM((BLOCKS * (BLOCKS + 1) // 2, KEYS, LANES), jnp.float32),
         ],
         compiler_params=pltpu.CompilerParams(vmem_limit_bytes=GRANT),
         name="attend",
-    )(lengths, rows.reshape(BLOCKS, KEYS, ROW_W), rows, rows)
+    )(lengths, rows.reshape(CTX, BLOCKS, ROWS, ROW_W), rows, rows)
     return out.reshape(count, QW)
 
 
@@ -228,13 +244,13 @@
     group = group_of_row.reshape(1, group_of_row.shape[0])
     packed = pack(group, query_rows, key_rows, token_values)
     arrived = lax.all_to_all(
-        packed.reshape(devices, SLOT, ROW_W), ("dp", "ctx"), split_axis=0, concat_axis=0, tiled=True
+        packed.reshape(devices, SLOT, ROW_W), ("ctx", "dp"), split_axis=0, concat_axis=0, tiled=True
     )
     result = attend(doc_lengths, arrived.reshape(devices * SLOT, ROW_W))
     returned = lax.all_to_all(
-        result.reshape(devices, SLOT, QW), ("dp", "ctx"), split_axis=0, concat_axis=0, tiled=True
-    )
-    return unpack(group, returned.reshape(GROUPS, KV_HEADS, SLOT, QW))
+        result.reshape(devices, SLOT, QW), ("ctx", "dp"), split_axis=0, concat_axis=0, tiled=True
+    )
+    return unpack(group, returned.reshape(KV_HEADS, GROUPS, SLOT, QW))
 
 
 def solution(mesh):

time: 177 us -> 176 us (level)
  local copies, waits for them, and re-layouts: 3.79 us -> 0.67 us
    unnamed x12 -> x6, local copies, waits for them, and re-layouts: 3.79 us -> 0.67 us
where the time goes in v7:
time: 176 us
  blocking collectives  151 us (86%)
  Pallas kernels  24.1 us (14%)
    all_to_all x1, blocking collectives, body(): lax.all_to_all(packed.reshape(devices, SLOT, ROW_W), ('ctx', 'dp'), split...  91.5 us
    all_to_all x1, blocking collectives, body(): lax.all_to_all(result.reshape(devices, SLOT, QW), ('ctx', 'dp'), split_ax...  59.2 us
    pallas_call x1, Pallas kernels, attend(): pl.pallas_call(attend_kernel, grid=(CTX,), in_specs=[pl.BlockSpec(memory_...  18.5 us

profile of v7, /device:TPU:1, one launch (start us, length us, event | category | flops | bytes accessed | tf_op | source)
XLA Modules:
  0.0 175.6 jit_solution(18289062517555143706)
XLA Ops:
  0.0 0.0 copy-start
  0.0 0.7 copy-done
  0.7 3.3 %pack.1 = bf16[8,32,8,768]{3,2,1,0:T(8,128)(2,1)S(1)} custom-call(s32[1,128]{1,0:T(1,128)S(1)} %bitcast.12, bf16[128,4096]{1,0:T(8,128)(2,1)} %q_ref.1, bf16[128,1024]{1,0:T(8,128)(2,1)} %k_ref.1, bf16[128,1024]{1,0:T(8,128)(2,1)} %v_ref.1), custom_call_target="tpu_custom_call" | custom-call | tf_op jit(solution)/shard_map/pack/pallas_call | solution.py:70
  3.9 0.0 copy-start.2
  3.9 91.5 %all_to_all.10 = bf16[256,8,768]{2,1,0:T(8,128)(2,1)S(1)} all-to-all(bf16[256,8,768]{2,1,0:T(8,128)(2,1)S(1)} %bitcast.9), channel_id=1, replica_groups=mesh['dp'=32,'ctx'=8] {'ctx','dp'}, dimensions={0} | all-to-all | bytes 6291456 | tf_op jit(solution)/shard_map/all_to_all | solution.py:246
  95.5 0.0 copy-done.2
  95.5 18.5 %attend.1 = bf16[8,4,64,512]{3,2,1,0:T(8,128)(2,1)S(1)} custom-call(s32[1,2]{1,0:T(1,128)S(1)} %copy-done.2, bf16[8,4,64,768]{3,2,1,0:T(8,128)(2,1)S(1)} %bitcast.6, bf16[2048,768]{1,0:T(8,128)(2,1)S(1)} %bitcast.7, bf16[2048,768]{1,0:T(8,128)(2,1)S(1)} %bitcast.8), custom_call_target="tpu_custom_call" | custom-call | tf_op jit(solution)/shard_map/attend/pallas_call | solution.py:218
  114.0 0.0 copy-start.1
  114.0 59.2 %all_to_all.11 = bf16[256,8,512]{2,1,0:T(8,128)(2,1)S(1)} all-to-all(bf16[256,8,512]{2,1,0:T(8,128)(2,1)S(1)} %bitcast.11), channel_id=1, replica_groups=mesh['dp'=32,'ctx'=8] {'ctx','dp'}, dimensions={0} | all-to-all | bytes 4194304 | tf_op jit(solution)/shard_map/all_to_all | solution.py:250
  173.2 0.0 copy-done.1
  173.2 2.3 %unpack.1 = bf16[128,4096]{1,0:T(8,128)(2,1)} custom-call(s32[1,128]{1,0:T(1,128)S(1)} %bitcast.13, bf16[8,32,8,512]{3,2,1,0:T(8,128)(2,1)S(1)} %bitcast.10), custom_call_target="tpu_custom_call" | custom-call | tf_op jit(solution)/shard_map/unpack/pallas_call | solution.py:106
Async XLA Ops:
  0.0 0.7 copy-start
  3.9 91.6 %copy-start.2 = (s32[1,2]{1,0:T(1,128)S(1)}, s32[1,2]{1,0:T(1,128)}, u32[]{:S(2)}) copy-start(s32[1,2]{1,0:T(1,128)} %len_ref.1) | copy-start | bytes 28
  114.0 59.2 %copy-start.1 = (s32[128,1]{0,1:T(1,128)S(1)}, s32[128,1]{0,1:T(1,128)}, u32[]{:S(2)}) copy-start(s32[128,1]{0,1:T(1,128)} %param.8) | copy-start | bytes 1540

commit v8 on v5

--- a/solution.py
+++ b/solution.py
@@ -22,8 +22,8 @@
 ROWS = SPAN * SLOT
 LANES = PER_KV * ROWS
 VALUE_ROWS = HEAD + 16
-PARTS = 1
-HEADS = KV_HEADS // PARTS
+PARTS = (2, 6)
+GRANT = 28 << 20
 
 
 def slot_targets(group_row):
@@ -48,6 +48,10 @@
     return x.reshape(GROUPS, SLOT, x.shape[1]).astype(jnp.bfloat16)
 
 
+def off_chip(x):
+    return pltpu.with_memory_space_constraint(x, pltpu.HBM)
+
+
 def pack_kv_kernel(group_ref, k_ref, v_ref, out_ref):
     pick = selection(group_ref[...])
     empty = (1.0 - jnp.sum(pick, axis=1, keepdims=True)) * EMPTY
@@ -63,53 +67,47 @@
     return pl.pallas_call(
         pack_kv_kernel,
         out_shape=jax.ShapeDtypeStruct((GROUPS, SLOT, 2 * k.shape[1]), jnp.bfloat16),
+        compiler_params=pltpu.CompilerParams(vmem_limit_bytes=GRANT),
         name="pack_kv",
-    )(group, k, v)
-
-
-def pack_q_kernel(group_ref, q_ref, *refs):
-    outs, pick_ref = refs[:-1], refs[-1]
-    step = pl.program_id(0)
-
-    @pl.when(step == 0)
+    )(group, off_chip(k), off_chip(v))
+
+
+def pack_q_kernel(group_ref, q_ref, out_ref, pick_ref):
+    @pl.when(pl.program_id(0) == 0)
     def _():
         pick_ref[...] = selection(group_ref[...]).astype(jnp.bfloat16)
 
-    for part, out_ref in enumerate(outs):
-
-        @pl.when(step == part)
-        def _(out_ref=out_ref):
-            out_ref[...] = laid(
-                jnp.dot(pick_ref[...], q_ref[...], preferred_element_type=jnp.float32)
-            )
+    out_ref[...] = laid(jnp.dot(pick_ref[...], q_ref[...], preferred_element_type=jnp.float32))
 
 
 def pack_q(group, q):
     rows, width = q.shape
-    part = width // PARTS
-    shape = (GROUPS, SLOT, part)
+    part = 2 * QW
     return pl.pallas_call(
         pack_q_kernel,
-        grid=(PARTS,),
+        grid=(width // part,),
         in_specs=[
             pl.BlockSpec((1, rows), lambda i: (0, 0)),
             pl.BlockSpec((rows, part), lambda i: (0, i)),
         ],
-        out_specs=[pl.BlockSpec(shape, lambda i: (0, 0, 0))] * PARTS,
-        out_shape=[jax.ShapeDtypeStruct(shape, jnp.bfloat16)] * PARTS,
+        out_specs=pl.BlockSpec((GROUPS, SLOT, part), lambda i: (0, 0, i)),
+        out_shape=jax.ShapeDtypeStruct((GROUPS, SLOT, width), jnp.bfloat16),
         scratch_shapes=[pltpu.VMEM((GROUPS * SLOT, rows), jnp.bfloat16)],
+        compiler_params=pltpu.CompilerParams(vmem_limit_bytes=GRANT),
         name="pack_q",
-    )(group, q)
+    )(group, off_chip(q))
 
 
 def unpack_kernel(group_ref, *refs):
     parts, out_ref = refs[:-1], refs[-1]
     pick = jnp.transpose(selection(group_ref[...])).astype(jnp.bfloat16)
-    for i, ref in enumerate(parts):
+    low = 0
+    for ref in parts:
         width = ref.shape[2]
-        out_ref[:, i * width : (i + 1) * width] = jnp.dot(
+        out_ref[:, low : low + width] = jnp.dot(
             pick, ref[...].reshape(GROUPS * SLOT, width), preferred_element_type=jnp.float32
         ).astype(jnp.bfloat16)
+        low += width
 
 
 def unpack(group, parts):
@@ -118,6 +116,7 @@
         out_shape=jax.ShapeDtypeStruct(
             (group.shape[1], sum(p.shape[2] for p in parts)), jnp.bfloat16
         ),
+        compiler_params=pltpu.CompilerParams(vmem_limit_bytes=GRANT),
         name="unpack",
     )(group, *parts)
 
@@ -178,6 +177,9 @@
             lax.broadcasted_iota(jnp.int32, (VALUE_ROWS - HEAD, BLOCKS * KEYS), 0) == 0, 1.0, 0.0
         ).astype(jnp.bfloat16)
 
+    def place(i, b):
+        return i * (i + 1) // 2 + b
+
     def joined(refs, span):
         return jnp.concatenate([ref[span].reshape(ROWS, HEAD) for ref in refs], axis=0)
 
@@ -205,14 +207,14 @@
             s = lax.dot_general(
                 key, queries[i], (((1,), (1,)), ((), ())), preferred_element_type=jnp.float32
             )
-            s_ref[i, b] = s + bias_ref[...] if i == b else s
+            s_ref[place(i, b)] = s + bias_ref[...] if i == b else s
     for i in range(BLOCKS):
-        top = jnp.max(s_ref[i, 0], axis=0, keepdims=True)
+        top = jnp.max(s_ref[place(i, 0)], axis=0, keepdims=True)
         for b in range(1, i + 1):
-            top = jnp.maximum(top, jnp.max(s_ref[i, b], axis=0, keepdims=True))
+            top = jnp.maximum(top, jnp.max(s_ref[place(i, b)], axis=0, keepdims=True))
         acc = None
         for b in range(i + 1):
-            w = jnp.exp2((s_ref[i, b] - top) * scale).astype(jnp.bfloat16)
+            w = jnp.exp2((s_ref[place(i, b)] - top) * scale).astype(jnp.bfloat16)
             part = jnp.dot(
                 vt_ref[:, b * KEYS : (b + 1) * KEYS], w, preferred_element_type=jnp.float32
             )
@@ -224,33 +226,33 @@
             ]
 
 
-def attend(lengths, who, q, keys, values):
+def attend(lengths, who, q, keys, values, low, heads):
     count = GROUPS * SLOT
 
-    def heads(first):
-        return pl.BlockSpec((GROUPS, SLOT, HEAD), lambda j: (0, 0, first + j))
+    def slabs(first):
+        return pl.BlockSpec((GROUPS, SLOT, HEAD), lambda j: (0, 0, first + low + j))
 
     blocks = keys + values
     return pl.pallas_call(
         attend_kernel,
-        grid=(HEADS,),
+        grid=(heads,),
         in_specs=[
             pl.BlockSpec(memory_space=pltpu.SMEM),
             pl.BlockSpec(memory_space=pltpu.SMEM),
-            pl.BlockSpec((count, QW), lambda j: (0, j)),
-            *(heads(first) for _, first in blocks),
+            pl.BlockSpec((count, QW), lambda j: (0, low + j)),
+            *(slabs(first) for _, first in blocks),
         ],
         out_specs=pl.BlockSpec((count, QW), lambda j: (0, j)),
-        out_shape=jax.ShapeDtypeStruct((count, HEADS * QW), jnp.bfloat16),
+        out_shape=jax.ShapeDtypeStruct((count, heads * QW), jnp.bfloat16),
         scratch_shapes=[
             pltpu.VMEM((BLOCKS, KEYS, HEAD), jnp.bfloat16),
             pltpu.VMEM((count, HEAD), jnp.bfloat16),
             pltpu.VMEM((KEYS, LANES), jnp.float32),
             pltpu.VMEM((VALUE_ROWS, BLOCKS * KEYS), jnp.bfloat16),
-            pltpu.VMEM((BLOCKS, BLOCKS, KEYS, LANES), jnp.float32),
+            pltpu.VMEM((BLOCKS * (BLOCKS + 1) // 2, KEYS, LANES), jnp.float32),
         ],
         cost_estimate=pl.CostEstimate(
-            flops=10**10, transcendentals=4 * 10**7, bytes_accessed=16 * 10**6
+            flops=heads * 10**9, transcendentals=heads * 5 * 10**6, bytes_accessed=heads * 2 * 10**6
         ),
         name="attend",
     )(lengths, who, q, *(array for array, _ in blocks))
@@ -284,12 +286,16 @@
 def body(query_rows, key_rows, token_values, group_of_row, doc_lengths):
     group = group_of_row.reshape(1, group_of_row.shape[0])
     sent = pack_kv(group, key_rows, token_values)
-    (queries,) = pack_q(group, query_rows)
+    queries = pack_q(group, query_rows)
     kv, queries = lax.optimization_barrier((exchange(sent), queries))
     keys, values, who = gather(kv)
-    arrived = exchange(queries).reshape(GROUPS * SLOT, HEADS * QW)
-    out = attend(doc_lengths, who, arrived, keys, values)
-    return unpack(group, [exchange(out.reshape(GROUPS, SLOT, HEADS * QW))])
+    arrived = exchange(queries).reshape(GROUPS * SLOT, queries.shape[2])
+    outs, low = [], 0
+    for heads in PARTS:
+        out = attend(doc_lengths, who, arrived, keys, values, low, heads)
+        outs.append(exchange(out.reshape(GROUPS, SLOT, out.shape[1])))
+        low += heads
+    return unpack(group, outs)
 
 
 def solution(mesh):

time: 179 us -> 180 us (level)
  blocking collectives: 56.6 us -> 46.2 us
  starting transfers between devices: 38 us -> 46.3 us
  Pallas kernels: 30.5 us -> 33.3 us
    all_to_all x1, blocking collectives: 56.6 us -> 46.2 us  [exchange(): return lax.all_to_all(x, 'dp', split_axis=0, concat_axis=0, tiled=True)]
    all_to_all x2 -> x3, starting transfers between devices: 18.4 us -> 26.7 us  [exchange(): return lax.all_to_all(x, 'dp', split_axis=0, concat_axis=0, tiled=True)]
    pallas_call x2 -> x3, Pallas kernels: 24.7 us -> 29.2 us  [the longest x2 24.9 us: attend(): pl.pallas_call(attend_kernel, grid=(heads,), in_specs=[pl.BlockSpec(memor...]
    all_to_all x2 -> x3, waiting for transfers between devices: 23.6 us -> 22.7 us  [exchange(): return lax.all_to_all(x, 'dp', split_axis=0, concat_axis=0, tiled=True)]
  transfers between devices with their start and end apart: 11 -> 12, of which waited for: 6 -> 6; matrix products, arithmetic and copies ran while one was open for 2% -> 2% of each run, Pallas kernels for 2% -> 12%
where the time goes in v8:
time: 180 us; the launch traced here: 177 us
  waiting for transfers between devices  46.8 us (26%)
  starting transfers between devices  46.3 us (26%)
  blocking collectives  46.2 us (26%)
  Pallas kernels  33.3 us (18%)
  local copies, waits for them, and re-layouts  4.83 us (3%)
    all_to_all x1, blocking collectives, exchange(): return lax.all_to_all(x, 'dp', split_axis=0, concat_axis=0, tiled=True)  46.2 us
    all_to_all x3, starting transfers between devices, exchange(): return lax.all_to_all(x, 'dp', split_axis=0, concat_axis=0, tiled=True)  26.7 us
    pallas_call x2, Pallas kernels, attend(): pl.pallas_call(attend_kernel, grid=(heads,), in_specs=[pl.BlockSpec(memor...  24.9 us
    all_to_all x3, waiting for transfers between devices, exchange(): return lax.all_to_all(x, 'dp', split_axis=0, concat_axis=0, tiled=True)  22.7 us
    ppermute x1, waiting for transfers between devices, gather(): after = lax.ppermute(kv, 'ctx', left)  18.2 us
    ppermute x5, starting transfers between devices, gather(): lax.ppermute(x, 'ctx', across)  13.4 us
    pallas_call x1, Pallas kernels, pack_q(): pl.pallas_call(pack_q_kernel, grid=(width // part,), in_specs=[pl.BlockSp...  4.27 us
    ppermute x1, waiting for transfers between devices, gather(): far_values = lax.ppermute(after[:, :, half:], 'ctx', left)  3.89 us
  transfers between devices with their start and end apart: 12, of which 6 were waited for; matrix products, arithmetic and copies ran while one was open for 2% of the time, Pallas kernels for 12%

profile of v8, /device:TPU:1, one launch (start us, length us, event | category | flops | bytes accessed | tf_op | source)
XLA Modules:
  0.0 177.4 jit_solution(5389461066858426388)
XLA Ops:
  0.0 0.7 copy-done
  0.7 2.5 %pack_kv.1 = bf16[32,8,2048]{2,1,0:T(8,128)(2,1)} custom-call(s32[1,128]{1,0:T(1,128)S(1)} %bitcast.13, bf16[128,1024]{1,0:T(8,128)(2,1)} %k_ref.1, bf16[128,1024]{1,0:T(8,128)(2,1)} %v_ref.1), custom_call_target="tpu_custom_call" | custom-call | tf_op jit(solution)/shard_map/pack_kv/pallas_call | solution.py:67
  3.3 12.0 %all-to-all-start = ((bf16[32,8,2048]{2,1,0:T(8,128)(2,1)}), bf16[32,8,2048]{2,1,0:T(8,128)(2,1)S(1)}, u32[]{:S(2)}, u32[]{:S(2)}) async-start(bf16[32,8,2048]{2,1,0:T(8,128)(2,1)} %pack_kv.1), calls=%async_computation | async-start | bytes 2097152 | tf_op jit(solution)/shard_map/all_to_all | solution.py:262
  15.3 4.3 %pack_q.1 = bf16[32,8,4096]{2,1,0:T(8,128)(2,1)} custom-call(s32[1,128]{1,0:T(1,128)S(1)} %bitcast.14, bf16[128,4096]{1,0:T(8,128)(2,1)} %q_ref.1), custom_call_target="tpu_custom_call" | custom-call | tf_op jit(solution)/shard_map/pack_q/pallas_call | solution.py:86
  19.6 21.9 %all-to-all-done.refs_0_.refs_8_ = bf16[32,8,2048]{2,1,0:T(8,128)(2,1)S(1)} async-done(((bf16[32,8,2048]{2,1,0:T(8,128)(2,1)}), bf16[32,8,2048]{2,1,0:T(8,128)(2,1)S(1)}, u32[]{:S(2)}, u32[]{:S(2)}) %all-to-all-start) | async-done | bytes 1048608 | tf_op jit(solution)/shard_map/all_to_all | solution.py:262
  41.5 6.4 %all-to-all-start.1 = ((bf16[32,8,4096]{2,1,0:T(8,128)(2,1)}), bf16[32,8,4096]{2,1,0:T(8,128)(2,1)S(1)}, u32[]{:S(2)}, u32[]{:S(2)}) async-start(bf16[32,8,4096]{2,1,0:T(8,128)(2,1)} %pack_q.1), calls=%async_computation.1 | async-start | bytes 4194304 | tf_op jit(solution)/shard_map/all_to_all | solution.py:262
  47.9 2.5 %collective-permute-start.1 = (bf16[32,8,2048]{2,1,0:T(8,128)(2,1)S(1)}, bf16[32,8,2048]{2,1,0:T(8,128)(2,1)}, u32[]{:S(2)}, u32[]{:S(2)}) collective-permute-start(bf16[32,8,2048]{2,1,0:T(8,128)(2,1)S(1)} %all-to-all-done.refs_0_.refs_8_), channel_id=1, source_target_pairs={{0,6},{1,7},{2,0},{3,1},{4,2},{5,3},{6,4},{7,5},{8,14},{9,15},{10,... | collective-permute-start | bytes 3145736 | tf_op jit(solution)/shard_map/ppermute | solution.py:272
  50.4 2.3 %collective-permute-start.3 = (bf16[32,8,2048]{2,1,0:T(8,128)(2,1)S(1)}, bf16[32,8,2048]{2,1,0:T(8,128)(2,1)}, u32[]{:S(2)}, u32[]{:S(2)}) collective-permute-start(bf16[32,8,2048]{2,1,0:T(8,128)(2,1)S(1)} %all-to-all-done.refs_0_.refs_8_), channel_id=1, source_target_pairs={{0,1},{1,0},{2,3},{3,2},{4,5},{5,4},{6,7},{7,6},{8,9},{9,8},{10,11... | collective-permute-start | bytes 3145736 | tf_op jit(solution)/shard_map/ppermute | solution.py:277
  52.7 18.2 %collective-permute-done.1.refs_2_.refs_10_ = bf16[32,8,2048]{2,1,0:T(8,128)(2,1)} collective-permute-done((bf16[32,8,2048]{2,1,0:T(8,128)(2,1)S(1)}, bf16[32,8,2048]{2,1,0:T(8,128)(2,1)}, u32[]{:S(2)}, u32[]{:S(2)}) %collective-permute-start.1) | collective-permute-done | bytes 1048608 | tf_op jit(solution)/shard_map/ppermute | solution.py:272
  70.9 1.1 slice.9
  72.0 3.6 %collective-permute-start.7 = (bf16[32,8,1024]{2,1,0:T(8,128)(2,1)S(1)}, bf16[32,8,1024]{2,1,0:T(8,128)(2,1)}, u32[]{:S(2)}, u32[]{:S(2)}) collective-permute-start(bf16[32,8,1024]{2,1,0:T(8,128)(2,1)S(1)} %slice.9), channel_id=1, source_target_pairs={{0,6},{1,7},{2,0},{3,1},{4,2},{5,3},{6,4},{7,5},{8,14},{9,15},{10,... | collective-permute-start | bytes 1572872 | tf_op jit(solution)/shard_map/ppermute | solution.py:274
  75.6 1.1 slice.8
  76.8 3.2 %collective-permute-start.5 = (bf16[32,8,2048]{2,1,0:T(8,128)(2,1)}, bf16[32,8,2048]{2,1,0:T(8,128)(2,1)}, u32[]{:S(2)}, u32[]{:S(2)}) collective-permute-start(bf16[32,8,2048]{2,1,0:T(8,128)(2,1)} %collective-permute-done.1.refs_2_.refs_10_), channel_id=1, source_target_pairs={{0,1},{1,0},{2,3},{3,2},{4,5},{5,4},{6,7},{7,6},{8,9},{9,8},{10,11... | collective-permute-start | bytes 3145736 | tf_op jit(solution)/shard_map/ppermute | solution.py:277
  80.1 3.9 %collective-permute-done.7.refs_11_ = bf16[32,8,1024]{2,1,0:T(8,128)(2,1)} collective-permute-done((bf16[32,8,1024]{2,1,0:T(8,128)(2,1)S(1)}, bf16[32,8,1024]{2,1,0:T(8,128)(2,1)}, u32[]{:S(2)}, u32[]{:S(2)}) %collective-permute-start.7) | collective-permute-done | bytes 524320 | tf_op jit(solution)/shard_map/ppermute | solution.py:274
  84.0 3.7 %collective-permute-start.8 = (bf16[32,8,1024]{2,1,0:T(8,128)(2,1)}, bf16[32,8,1024]{2,1,0:T(8,128)(2,1)}, u32[]{:S(2)}, u32[]{:S(2)}) collective-permute-start(bf16[32,8,1024]{2,1,0:T(8,128)(2,1)} %collective-permute-done.7.refs_11_), channel_id=1, source_target_pairs={{0,1},{1,0},{2,3},{3,2},{4,5},{5,4},{6,7},{7,6},{8,9},{9,8},{10,11... | collective-permute-start | bytes 1572872 | tf_op jit(solution)/shard_map/ppermute | solution.py:277
  88.4 4.0 %collective-permute-start.6 = (bf16[32,8,1024]{2,1,0:T(8,128)(2,1)}, bf16[32,8,1024]{2,1,0:T(8,128)(2,1)}, u32[]{:S(2)}, u32[]{:S(2)}) collective-permute-start(bf16[32,8,1024]{2,1,0:T(8,128)(2,1)} %collective-permute-done.2.refs_3_), channel_id=1, source_target_pairs={{0,1},{1,0},{2,3},{3,2},{4,5},{5,4},{6,7},{7,6},{8,9},{9,8},{10,11... | collective-permute-start | bytes 1572872 | tf_op jit(solution)/shard_map/ppermute | solution.py:277
  93.0 1.3 collective-permute-done.6.refs_7_
  94.3 0.8 all-to-all-done.1
  95.1 1.3 copy-done.2
  96.5 7.9 %attend.2 = bf16[256,1024]{1,0:T(8,128)(2,1)} custom-call(s32[1,2]{1,0:T(1,128)} %len_ref.3, s32[1,8]{1,0:T(1,128)} %bitcast.20, bf16[256,4096]{1,0:T(8,128)(2,1)} %bitcast.16, bf16[32,8,2048]{2,1,0:T(8,128)(2,1)} %copy-done.3, bf16[32,8,2048]{2,1,0:T(8,128)(2,1)} %collective-permute-done.refs_1_.refs_9_, ...), custom_call_target="tpu_custom_call" | custom-call | flops 2000000000 | bytes 4000000 | tf_op jit(solution)/shard_map/attend/pallas_call | solution.py:236
  104.3 8.3 %all-to-all-start.2 = ((bf16[32,8,1024]{2,1,0:T(8,128)(2,1)}), bf16[32,8,1024]{2,1,0:T(8,128)(2,1)S(1)}, u32[]{:S(2)}, u32[]{:S(2)}) async-start(bf16[32,8,1024]{2,1,0:T(8,128)(2,1)} %bitcast.19), calls=%async_computation.2 | async-start | bytes 1048576 | tf_op jit(solution)/shard_map/all_to_all | solution.py:262
  112.6 17.0 %attend.3 = bf16[256,3072]{1,0:T(8,128)(2,1)} custom-call(s32[1,2]{1,0:T(1,128)} %len_ref.3, s32[1,8]{1,0:T(1,128)} %bitcast.21, bf16[256,4096]{1,0:T(8,128)(2,1)} %bitcast.17, bf16[32,8,2048]{2,1,0:T(8,128)(2,1)} %copy-done.3, bf16[32,8,2048]{2,1,0:T(8,128)(2,1)} %collective-permute-done.refs_1_.refs_9_, ...), custom_call_target="tpu_custom_call" | custom-call | flops 6000000000 | bytes 12000000 | tf_op jit(solution)/shard_map/attend/pallas_call | solution.py:236
  129.7 46.2 %all_to_all.20.refs_1_ = bf16[32,8,3072]{2,1,0:T(8,128)(2,1)S(1)} all-to-all(bf16[32,8,3072]{2,1,0:T(8,128)(2,1)} %bitcast.18), channel_id=1, replica_groups=mesh['dp'=32,'ctx'=8] {'dp'}, dimensions={0} | all-to-all | bytes 3145728 | tf_op jit(solution)/shard_map/all_to_all | solution.py:262
  175.8 1.6 unpack.1
  (17 shorter events, 1.5 us)
Async XLA Ops:
  0.0 15.3 %copy-start.1 = (s32[128,1]{0,1:T(1,128)S(1)}, s32[128,1]{0,1:T(1,128)}, u32[]{:S(2)}) copy-start(s32[128,1]{0,1:T(1,128)} %param.8) | copy-start | bytes 1540
  0.0 0.7 copy-start
  3.3 38.2 %all-to-all-start = ((bf16[32,8,2048]{2,1,0:T(8,128)(2,1)}), bf16[32,8,2048]{2,1,0:T(8,128)(2,1)S(1)}, u32[]{:S(2)}, u32[]{:S(2)}) async-start(bf16[32,8,2048]{2,1,0:T(8,128)(2,1)} %pack_kv.1), calls=%async_computation | async-start | bytes 2097152 | tf_op jit(solution)/shard_map/all_to_all | solution.py:262
  41.5 53.6 %copy-start.3 = (bf16[32,8,2048]{2,1,0:T(8,128)(2,1)}, bf16[32,8,2048]{2,1,0:T(8,128)(2,1)S(1)}, u32[]{:S(2)}) copy-start(bf16[32,8,2048]{2,1,0:T(8,128)(2,1)S(1)} %all-to-all-done.refs_0_.refs_8_) | copy-start | bytes 3145732
  41.5 53.6 %all-to-all-start.1 = ((bf16[32,8,4096]{2,1,0:T(8,128)(2,1)}), bf16[32,8,4096]{2,1,0:T(8,128)(2,1)S(1)}, u32[]{:S(2)}, u32[]{:S(2)}) async-start(bf16[32,8,4096]{2,1,0:T(8,128)(2,1)} %pack_q.1), calls=%async_computation.1 | async-start | bytes 4194304 | tf_op jit(solution)/shard_map/all_to_all | solution.py:262
  47.9 23.0 %collective-permute-start.1 = (bf16[32,8,2048]{2,1,0:T(8,128)(2,1)S(1)}, bf16[32,8,2048]{2,1,0:T(8,128)(2,1)}, u32[]{:S(2)}, u32[]{:S(2)}) collective-permute-start(bf16[32,8,2048]{2,1,0:T(8,128)(2,1)S(1)} %all-to-all-done.refs_0_.refs_8_), channel_id=1, source_target_pairs={{0,6},{1,7},{2,0},{3,1},{4,2},{5,3},{6,4},{7,5},{8,14},{9,15},{10,... | collective-permute-start | bytes 3145736 | tf_op jit(solution)/shard_map/ppermute | solution.py:272
  50.4 25.2 %collective-permute-start = (bf16[32,8,2048]{2,1,0:T(8,128)(2,1)S(1)}, bf16[32,8,2048]{2,1,0:T(8,128)(2,1)}, u32[]{:S(2)}, u32[]{:S(2)}) collective-permute-start(bf16[32,8,2048]{2,1,0:T(8,128)(2,1)S(1)} %all-to-all-done.refs_0_.refs_8_), channel_id=1, source_target_pairs={{0,2},{1,3},{2,4},{3,5},{4,6},{5,7},{6,0},{7,1},{8,10},{9,11},{10,... | collective-permute-start | bytes 3145736 | tf_op jit(solution)/shard_map/ppermute | solution.py:271
  50.4 42.6 %collective-permute-start.3 = (bf16[32,8,2048]{2,1,0:T(8,128)(2,1)S(1)}, bf16[32,8,2048]{2,1,0:T(8,128)(2,1)}, u32[]{:S(2)}, u32[]{:S(2)}) collective-permute-start(bf16[32,8,2048]{2,1,0:T(8,128)(2,1)S(1)} %all-to-all-done.refs_0_.refs_8_), channel_id=1, source_target_pairs={{0,1},{1,0},{2,3},{3,2},{4,5},{5,4},{6,7},{7,6},{8,9},{9,8},{10,11... | collective-permute-start | bytes 3145736 | tf_op jit(solution)/shard_map/ppermute | solution.py:277
  72.0 12.0 %collective-permute-start.7 = (bf16[32,8,1024]{2,1,0:T(8,128)(2,1)S(1)}, bf16[32,8,1024]{2,1,0:T(8,128)(2,1)}, u32[]{:S(2)}, u32[]{:S(2)}) collective-permute-start(bf16[32,8,1024]{2,1,0:T(8,128)(2,1)S(1)} %slice.9), channel_id=1, source_target_pairs={{0,6},{1,7},{2,0},{3,1},{4,2},{5,3},{6,4},{7,5},{8,14},{9,15},{10,... | collective-permute-start | bytes 1572872 | tf_op jit(solution)/shard_map/ppermute | solution.py:274
  76.7 11.7 %collective-permute-start.2 = (bf16[32,8,1024]{2,1,0:T(8,128)(2,1)S(1)}, bf16[32,8,1024]{2,1,0:T(8,128)(2,1)}, u32[]{:S(2)}, u32[]{:S(2)}) collective-permute-start(bf16[32,8,1024]{2,1,0:T(8,128)(2,1)S(1)} %slice.8), channel_id=1, source_target_pairs={{0,2},{1,3},{2,4},{3,5},{4,6},{5,7},{6,0},{7,1},{8,10},{9,11},{10,... | collective-permute-start | bytes 1572872 | tf_op jit(solution)/shard_map/ppermute | solution.py:273
  76.8 17.5 %collective-permute-start.5 = (bf16[32,8,2048]{2,1,0:T(8,128)(2,1)}, bf16[32,8,2048]{2,1,0:T(8,128)(2,1)}, u32[]{:S(2)}, u32[]{:S(2)}) collective-permute-start(bf16[32,8,2048]{2,1,0:T(8,128)(2,1)} %collective-permute-done.1.refs_2_.refs_10_), channel_id=1, source_target_pairs={{0,1},{1,0},{2,3},{3,2},{4,5},{5,4},{6,7},{7,6},{8,9},{9,8},{10,11... | collective-permute-start | bytes 3145736 | tf_op jit(solution)/shard_map/ppermute | solution.py:277
  80.0 14.3 %collective-permute-start.4 = (bf16[32,8,2048]{2,1,0:T(8,128)(2,1)}, bf16[32,8,2048]{2,1,0:T(8,128)(2,1)}, u32[]{:S(2)}, u32[]{:S(2)}) collective-permute-start(bf16[32,8,2048]{2,1,0:T(8,128)(2,1)} %collective-permute-done.refs_1_.refs_9_), channel_id=1, source_target_pairs={{0,1},{1,0},{2,3},{3,2},{4,5},{5,4},{6,7},{7,6},{8,9},{9,8},{10,11... | collective-permute-start | bytes 3145736 | tf_op jit(solution)/shard_map/ppermute | solution.py:277
  84.0 9.0 %collective-permute-start.8 = (bf16[32,8,1024]{2,1,0:T(8,128)(2,1)}, bf16[32,8,1024]{2,1,0:T(8,128)(2,1)}, u32[]{:S(2)}, u32[]{:S(2)}) collective-permute-start(bf16[32,8,1024]{2,1,0:T(8,128)(2,1)} %collective-permute-done.7.refs_11_), channel_id=1, source_target_pairs={{0,1},{1,0},{2,3},{3,2},{4,5},{5,4},{6,7},{7,6},{8,9},{9,8},{10,11... | collective-permute-start | bytes 1572872 | tf_op jit(solution)/shard_map/ppermute | solution.py:277
  88.4 5.9 %collective-permute-start.6 = (bf16[32,8,1024]{2,1,0:T(8,128)(2,1)}, bf16[32,8,1024]{2,1,0:T(8,128)(2,1)}, u32[]{:S(2)}, u32[]{:S(2)}) collective-permute-start(bf16[32,8,1024]{2,1,0:T(8,128)(2,1)} %collective-permute-done.2.refs_3_), channel_id=1, source_target_pairs={{0,1},{1,0},{2,3},{3,2},{4,5},{5,4},{6,7},{7,6},{8,9},{9,8},{10,11... | collective-permute-start | bytes 1572872 | tf_op jit(solution)/shard_map/ppermute | solution.py:277
  95.1 1.3 copy-start.2
  104.3 25.4 %all-to-all-start.2 = ((bf16[32,8,1024]{2,1,0:T(8,128)(2,1)}), bf16[32,8,1024]{2,1,0:T(8,128)(2,1)S(1)}, u32[]{:S(2)}, u32[]{:S(2)}) async-start(bf16[32,8,1024]{2,1,0:T(8,128)(2,1)} %bitcast.19), calls=%async_computation.2 | async-start | bytes 1048576 | tf_op jit(solution)/shard_map/all_to_all | solution.py:262

commit v9 on v7

--- a/solution.py
+++ b/solution.py
@@ -22,6 +22,9 @@
 LANES = PER_KV * ROWS
 CTX = 8
 PART = BLOCKS * ROWS
+NEAR = ROWS // 2
+HALF = KEYS // 2
+SIDE = LANES // 2
 GRANT = 24 << 20
 VALUE_ROWS = HEAD + 16
 STEP = 2
@@ -81,7 +84,7 @@
         scratch_shapes=[pltpu.VMEM((GROUPS * SLOT, rows), jnp.bfloat16)],
         compiler_params=pltpu.CompilerParams(vmem_limit_bytes=GRANT),
         name="pack",
-    )(group, *(pltpu.with_memory_space_constraint(x, pltpu.HBM) for x in (q, k, v)))
+    )(*(pltpu.with_memory_space_constraint(x, pltpu.HBM) for x in (group, q, k, v)))
 
 
 def unpack_kernel(group_ref, o_ref, out_ref, pick_ref):
@@ -123,10 +126,10 @@
     step = pl.program_id(0)
 
     def joined(ref, b):
-        low = b * ROWS
-        return jnp.concatenate(
-            [ref[c * PART + low : c * PART + low + ROWS, :] for c in range(CTX)], axis=0
-        )
+        lows = [
+            c * PART + b * ROWS + half * NEAR for half in range(2) for c in range(CTX)
+        ]
+        return jnp.concatenate([ref[low : low + NEAR, :] for low in lows], axis=0)
 
     @pl.when(step == 0)
     def _():
@@ -141,7 +144,20 @@
             )
             for part in (value[c * PART : (c + 1) * PART] for c in range(CTX))
         ]
-        number = [jnp.sum(u, axis=1) for u in used]
+        slots_of = jnp.where(
+            lax.broadcasted_iota(jnp.int32, (GROUPS, PART), 0)
+            == lax.broadcasted_iota(jnp.int32, (GROUPS, PART), 1) // SLOT,
+            1.0,
+            0.0,
+        ).astype(jnp.bfloat16)
+        number = [
+            jnp.dot(
+                slots_of,
+                u.reshape(PART, HEAD).astype(jnp.bfloat16),
+                preferred_element_type=jnp.float32,
+            )
+            for u in used
+        ]
         before = jnp.where(
             lax.broadcasted_iota(jnp.int32, (GROUPS, GROUPS), 0)
             > lax.broadcasted_iota(jnp.int32, (GROUPS, GROUPS), 1),
@@ -161,10 +177,13 @@
             at = slice(c * PART, (c + 1) * PART)
             feat_ref[at, :] = jnp.where(hit, 1.0, 0.0).reshape(PART, HEAD).astype(jnp.bfloat16)
             mask_ref[at, :] = jnp.where(hit, 0.0, -FAR).reshape(PART, HEAD).astype(jnp.bfloat16)
-        u = lax.broadcasted_iota(jnp.int32, (KEYS, LANES), 0)
-        t = lax.broadcasted_iota(jnp.int32, (KEYS, LANES), 1) % ROWS
-        u_order = u % ROWS // SLOT * (CTX * SLOT) + u // ROWS * SLOT + u % SLOT
-        ahead_ref[...] = (u_order - t // SLOT * (CTX * SLOT) - t % SLOT).astype(jnp.float32)
+        u = lax.broadcasted_iota(jnp.int32, (HALF, SIDE), 0)
+        u_order = u % NEAR // SLOT * (CTX * SLOT) + u // NEAR * SLOT + u % SLOT
+        t = lax.broadcasted_iota(jnp.int32, (1, LANES), 1)
+        t_order = t // SIDE * (HALF) + t % NEAR // SLOT * (CTX * SLOT) + t % SLOT
+        ahead_ref[...] = (jnp.concatenate([u_order, u_order], axis=1) - t_order).astype(
+            jnp.float32
+        )
         for b in range(BLOCKS):
             vt_ref[0:HEAD, b * KEYS : (b + 1) * KEYS] = jnp.transpose(joined(value, b)).astype(
                 jnp.bfloat16
@@ -178,38 +197,58 @@
 
     queries = []
     for i in range(BLOCKS):
-        mask = mask_ref[pl.ds(pl.multiple_of(step * PART + i * ROWS, ROWS), ROWS), :]
-        queries.append(
-            jnp.concatenate(
-                [
-                    jnp.concatenate([q_ref[0, i, :, h * HEAD : (h + 1) * HEAD], mask], axis=1)
-                    for h in range(PER_KV)
-                ],
-                axis=0,
-            )
+        pieces = []
+        for half in range(2):
+            at = slice(half * NEAR, (half + 1) * NEAR)
+            mask = mask_ref[
+                pl.ds(pl.multiple_of(step * PART + i * ROWS + half * NEAR, NEAR), NEAR), :
+            ]
+            pieces += [
+                jnp.concatenate([q_ref[0, i, at, h * HEAD : (h + 1) * HEAD], mask], axis=1)
+                for h in range(PER_KV)
+            ]
+        queries.append(jnp.concatenate(pieces, axis=0))
+
+    def place(i, b):
+        return i * (i + 1) // 2 + b
+
+    def product(key, query):
+        return lax.dot_general(
+            key, query, (((1,), (1,)), ((), ())), preferred_element_type=jnp.float32
         )
+
     for b in range(BLOCKS):
         key = jnp.concatenate([joined(k_ref, b), joined(feat_ref, b)], axis=1)
-        for i in range(b, BLOCKS):
-            s = lax.dot_general(
-                key, queries[i], (((1,), (1,)), ((), ())), preferred_element_type=jnp.float32
+        s_ref[place(b, b), 0:HALF, :] = product(key[0:HALF], queries[b]) + bias
+        s_ref[place(b, b), HALF:, SIDE:] = product(key[HALF:], queries[b][SIDE:]) + bias[:, 0:SIDE]
+        for i in range(b + 1, BLOCKS):
+            s_ref[place(i, b)] = product(key, queries[i])
+    for i in range(BLOCKS):
+        top = jnp.max(s_ref[place(i, i), 0:HALF, :], axis=0, keepdims=True)
+        for b in range(i):
+            top = jnp.maximum(top, jnp.max(s_ref[place(i, b)], axis=0, keepdims=True))
+        late = jnp.max(s_ref[place(i, i), HALF:, SIDE:], axis=0, keepdims=True)
+        late = jnp.maximum(top[:, SIDE:], late)
+        top = jnp.concatenate([top[:, 0:SIDE], late], axis=1)
+
+        def part(s, top, low):
+            w = jnp.exp2((s - top) * scale).astype(jnp.bfloat16)
+            return jnp.dot(
+                vt_ref[:, low : low + s.shape[0]], w, preferred_element_type=jnp.float32
             )
-            s_ref[i * (i + 1) // 2 + b] = s + bias if i == b else s
-    for i in range(BLOCKS):
-        low = i * (i + 1) // 2
-        top = jnp.max(s_ref[low], axis=0, keepdims=True)
-        for b in range(1, i + 1):
-            top = jnp.maximum(top, jnp.max(s_ref[low + b], axis=0, keepdims=True))
-        acc = None
-        for b in range(i + 1):
-            w = jnp.exp2((s_ref[low + b] - top) * scale).astype(jnp.bfloat16)
-            part = jnp.dot(
-                vt_ref[:, b * KEYS : (b + 1) * KEYS], w, preferred_element_type=jnp.float32
-            )
-            acc = part if acc is None else acc + part
+
+        acc = part(s_ref[place(i, i), 0:HALF, :], top, i * KEYS)
+        for b in range(i):
+            acc = acc + part(s_ref[place(i, b)], top, b * KEYS)
+        more = part(s_ref[place(i, i), HALF:, SIDE:], late, i * KEYS + HALF)
+        acc = jnp.concatenate([acc[:, 0:SIDE], acc[:, SIDE:] + more], axis=1)
         out = jnp.transpose(acc[0:HEAD] * (1.0 / acc[HEAD : HEAD + 1])).astype(jnp.bfloat16)
-        for h in range(PER_KV):
-            o_ref[0, i, :, h * HEAD : (h + 1) * HEAD] = out[h * ROWS : (h + 1) * ROWS]
+        for half in range(2):
+            for h in range(PER_KV):
+                low = half * SIDE + h * NEAR
+                o_ref[0, i, half * NEAR : (half + 1) * NEAR, h * HEAD : (h + 1) * HEAD] = out[
+                    low : low + NEAR
+                ]
 
 
 def attend(lengths, rows):
@@ -229,7 +268,7 @@
         scratch_shapes=[
             pltpu.VMEM((count, HEAD), jnp.bfloat16),
             pltpu.VMEM((count, HEAD), jnp.bfloat16),
-            pltpu.VMEM((KEYS, LANES), jnp.float32),
+            pltpu.VMEM((HALF, LANES), jnp.float32),
             pltpu.VMEM((VALUE_ROWS, count), jnp.bfloat16),
             pltpu.VMEM((BLOCKS * (BLOCKS + 1) // 2, KEYS, LANES), jnp.float32),
         ],

time: 176 us -> 174 us (0.989)
  no operation moved by 1% of the time
where the time goes in v9:
time: 174 us; the launch traced here: 173 us
  blocking collectives  151 us (87%)
  Pallas kernels  22.6 us (13%)
    all_to_all x1, blocking collectives, body(): lax.all_to_all(packed.reshape(devices, SLOT, ROW_W), ('ctx', 'dp'), split...  91.5 us
    all_to_all x1, blocking collectives, body(): lax.all_to_all(result.reshape(devices, SLOT, QW), ('ctx', 'dp'), split_ax...  59.2 us
    pallas_call x1, Pallas kernels, attend(): pl.pallas_call(attend_kernel, grid=(CTX,), in_specs=[pl.BlockSpec(memory_...  17 us

profile of v9, /device:TPU:1, one launch (start us, length us, event | category | flops | bytes accessed | tf_op | source)
XLA Modules:
  0.0 173.4 jit_solution(12178646000816105808)
XLA Ops:
  0.0 3.3 %pack.1 = bf16[8,32,8,768]{3,2,1,0:T(8,128)(2,1)S(1)} custom-call(s32[1,128]{1,0:T(1,128)} %bitcast.12, bf16[128,4096]{1,0:T(8,128)(2,1)} %q_ref.1, bf16[128,1024]{1,0:T(8,128)(2,1)} %k_ref.1, bf16[128,1024]{1,0:T(8,128)(2,1)} %v_ref.1), custom_call_target="tpu_custom_call" | custom-call | tf_op jit(solution)/shard_map/pack/pallas_call | solution.py:73
  3.3 0.0 copy-start.1
  3.3 91.5 %all_to_all.10 = bf16[256,8,768]{2,1,0:T(8,128)(2,1)S(1)} all-to-all(bf16[256,8,768]{2,1,0:T(8,128)(2,1)S(1)} %bitcast.9), channel_id=1, replica_groups=mesh['dp'=32,'ctx'=8] {'ctx','dp'}, dimensions={0} | all-to-all | bytes 6291456 | tf_op jit(solution)/shard_map/all_to_all | solution.py:285
  94.8 0.0 copy-done.1
  94.8 17.0 %attend.1 = bf16[8,4,64,512]{3,2,1,0:T(8,128)(2,1)S(1)} custom-call(s32[1,2]{1,0:T(1,128)S(1)} %copy-done.1, bf16[8,4,64,768]{3,2,1,0:T(8,128)(2,1)S(1)} %bitcast.6, bf16[2048,768]{1,0:T(8,128)(2,1)S(1)} %bitcast.7, bf16[2048,768]{1,0:T(8,128)(2,1)S(1)} %bitcast.8), custom_call_target="tpu_custom_call" | custom-call | tf_op jit(solution)/shard_map/attend/pallas_call | solution.py:257
  111.9 0.0 copy-start
  111.9 59.2 %all_to_all.11 = bf16[256,8,512]{2,1,0:T(8,128)(2,1)S(1)} all-to-all(bf16[256,8,512]{2,1,0:T(8,128)(2,1)S(1)} %bitcast.11), channel_id=1, replica_groups=mesh['dp'=32,'ctx'=8] {'ctx','dp'}, dimensions={0} | all-to-all | bytes 4194304 | tf_op jit(solution)/shard_map/all_to_all | solution.py:289
  171.1 0.0 copy-done
  171.1 2.3 %unpack.1 = bf16[128,4096]{1,0:T(8,128)(2,1)} custom-call(s32[1,128]{1,0:T(1,128)S(1)} %bitcast.13, bf16[8,32,8,512]{3,2,1,0:T(8,128)(2,1)S(1)} %bitcast.10), custom_call_target="tpu_custom_call" | custom-call | tf_op jit(solution)/shard_map/unpack/pallas_call | solution.py:109
Async XLA Ops:
  3.3 91.6 %copy-start.1 = (s32[1,2]{1,0:T(1,128)S(1)}, s32[1,2]{1,0:T(1,128)}, u32[]{:S(2)}) copy-start(s32[1,2]{1,0:T(1,128)} %len_ref.1) | copy-start | bytes 28
  111.9 59.2 %copy-start = (s32[128,1]{0,1:T(1,128)S(1)}, s32[128,1]{0,1:T(1,128)}, u32[]{:S(2)}) copy-start(s32[128,1]{0,1:T(1,128)} %param.8) | copy-start | bytes 1540

commit v10 on v9

--- a/solution.py
+++ b/solution.py
@@ -27,7 +27,7 @@
 SIDE = LANES // 2
 GRANT = 24 << 20
 VALUE_ROWS = HEAD + 16
-STEP = 2
+STEP = 4
 
 
 def slot_targets(group_row):

time: 174 us -> 172 us (0.989)
  no operation moved by 1% of the time
where the time goes in v10:
time: 172 us
  blocking collectives  151 us (88%)
  Pallas kernels  21.1 us (12%)
    all_to_all x1, blocking collectives, body(): lax.all_to_all(packed.reshape(devices, SLOT, ROW_W), ('ctx', 'dp'), split...  91.5 us
    all_to_all x1, blocking collectives, body(): lax.all_to_all(result.reshape(devices, SLOT, QW), ('ctx', 'dp'), split_ax...  59.2 us
    pallas_call x1, Pallas kernels, attend(): pl.pallas_call(attend_kernel, grid=(CTX,), in_specs=[pl.BlockSpec(memory_...  17 us

profile of v10, /device:TPU:1, one launch (start us, length us, event | category | flops | bytes accessed | tf_op | source)
XLA Modules:
  0.0 171.9 jit_solution(2954532624115739260)
XLA Ops:
  0.0 2.4 %pack.1 = bf16[8,32,8,768]{3,2,1,0:T(8,128)(2,1)S(1)} custom-call(s32[1,128]{1,0:T(1,128)} %bitcast.12, bf16[128,4096]{1,0:T(8,128)(2,1)} %q_ref.1, bf16[128,1024]{1,0:T(8,128)(2,1)} %k_ref.1, bf16[128,1024]{1,0:T(8,128)(2,1)} %v_ref.1), custom_call_target="tpu_custom_call" | custom-call | tf_op jit(solution)/shard_map/pack/pallas_call | solution.py:73
  2.4 0.0 copy-start.1
  2.5 91.5 %all_to_all.10 = bf16[256,8,768]{2,1,0:T(8,128)(2,1)S(1)} all-to-all(bf16[256,8,768]{2,1,0:T(8,128)(2,1)S(1)} %bitcast.9), channel_id=1, replica_groups=mesh['dp'=32,'ctx'=8] {'ctx','dp'}, dimensions={0} | all-to-all | bytes 6291456 | tf_op jit(solution)/shard_map/all_to_all | solution.py:285
  94.0 0.0 copy-done.1
  94.0 17.0 %attend.1 = bf16[8,4,64,512]{3,2,1,0:T(8,128)(2,1)S(1)} custom-call(s32[1,2]{1,0:T(1,128)S(1)} %copy-done.1, bf16[8,4,64,768]{3,2,1,0:T(8,128)(2,1)S(1)} %bitcast.6, bf16[2048,768]{1,0:T(8,128)(2,1)S(1)} %bitcast.7, bf16[2048,768]{1,0:T(8,128)(2,1)S(1)} %bitcast.8), custom_call_target="tpu_custom_call" | custom-call | tf_op jit(solution)/shard_map/attend/pallas_call | solution.py:257
  111.0 0.0 copy-start
  111.1 59.2 %all_to_all.11 = bf16[256,8,512]{2,1,0:T(8,128)(2,1)S(1)} all-to-all(bf16[256,8,512]{2,1,0:T(8,128)(2,1)S(1)} %bitcast.11), channel_id=1, replica_groups=mesh['dp'=32,'ctx'=8] {'ctx','dp'}, dimensions={0} | all-to-all | bytes 4194304 | tf_op jit(solution)/shard_map/all_to_all | solution.py:289
  170.3 0.0 copy-done
  170.3 1.6 unpack.1
Async XLA Ops:
  2.4 91.6 %copy-start.1 = (s32[1,2]{1,0:T(1,128)S(1)}, s32[1,2]{1,0:T(1,128)}, u32[]{:S(2)}) copy-start(s32[1,2]{1,0:T(1,128)} %len_ref.1) | copy-start | bytes 28
  111.0 59.2 %copy-start = (s32[128,1]{0,1:T(1,128)S(1)}, s32[128,1]{0,1:T(1,128)}, u32[]{:S(2)}) copy-start(s32[128,1]{0,1:T(1,128)} %param.8) | copy-start | bytes 1540
